TPU v7x, 32 devices: a whole 2x2x4 slice. The times are simulated.
32 devices in a mesh: seq: 4 (over x, core), dp: 8 (over z, y).
Axes of the slice: x: 2, y: 2, z: 4, core: 2. Of those that a mesh axis runs over, the one named last changes fastest.
Arguments:
- inputs: bfloat16 [8, 1024, 4096], P('dp', 'seq'), may hold values from -6 to 6
- queries: bfloat16 [8, 1024, 256], P('dp', 'seq'), may hold values from -6 to 6
- keys: bfloat16 [8, 1024, 256], P('dp', 'seq'), may hold values from -6 to 6
- values: bfloat16 [8, 1024, 256], P('dp', 'seq'), may hold values from -6 to 6
- out_grad: bfloat16 [8, 1024, 256], P('dp', 'seq'), may hold values from -6 to 6
Outputs:
- qkv_grad: bfloat16 [8, 1024, 768], P('dp', 'seq')
- weight_grad: float32 [4096, 768], P('dp')
All inputs are finite; a program needn't handle non-finite values.
Results may differ from a plain program's by a relative error of at most 0.014.
Values may be sent and summed in bfloat16 or wider, within the bound.
No kernel may reach another device: no remote copies, remote signals or barrier semaphores. Data moves between devices by JAX's collectives and lax.ppermute only.
A program may use at most 64 MiB of HBM per device.

v0:
```python
import jax
import jax.numpy as jnp
from jax import lax
from jax.sharding import PartitionSpec as P

HS = 128
HEADS = 2


def block_grads(query, key, value, grad_out, prefix, suffix, scale):
    count = query.shape[0]
    causal = jnp.arange(count)[:, None] >= jnp.arange(count)[None, :]
    f32 = jnp.float32
    score_a = jnp.einsum("thd,shd->hts", grad_out, value, preferred_element_type=f32)
    score_a = jnp.where(causal[None], score_a, 0.0).astype(jnp.bfloat16)
    score_b = jnp.einsum("thd,shd->hts", query, key, preferred_element_type=f32)
    score_b = jnp.where(causal[None], score_b, 0.0).astype(jnp.bfloat16)
    grad_q = jnp.einsum("hts,shd->thd", score_a, key, preferred_element_type=f32) + jnp.einsum(
        "thb,hab->tha", grad_out, prefix, preferred_element_type=f32
    )
    grad_k = jnp.einsum("htj,thd->jhd", score_a, query, preferred_element_type=f32) + jnp.einsum(
        "jhb,hab->jha", value, suffix, preferred_element_type=f32
    )
    grad_v = jnp.einsum("htj,thd->jhd", score_b, grad_out, preferred_element_type=f32) + jnp.einsum(
        "jha,hab->jhb", key, suffix, preferred_element_type=f32
    )
    joined = jnp.concatenate([grad_q, grad_k, grad_v], axis=1) * scale
    return joined.reshape(count, -1).astype(jnp.bfloat16)


def on_device(inputs, queries, keys, values, out_grad):
    tokens = queries.shape[1]
    seq_count = lax.axis_size("seq")
    batch_count = lax.axis_size("dp")
    length_all = tokens * seq_count
    scale = 1.0 / jnp.sqrt(jnp.float32(HS * length_all))
    weight_scale = 1.0 / jnp.sqrt(jnp.float32(batch_count * length_all))
    shape = (tokens, HEADS, HS)
    query = queries[0].reshape(shape)
    key = keys[0].reshape(shape)
    value = values[0].reshape(shape)
    grad_out = out_grad[0].reshape(shape)
    kv_state = jnp.einsum("lhi,lhj->hij", key, value, preferred_element_type=jnp.float32).astype(
        jnp.bfloat16
    )
    dq_state = jnp.einsum(
        "lhi,lhj->hij", query, grad_out, preferred_element_type=jnp.float32
    ).astype(jnp.bfloat16)
    stacked = jnp.stack([kv_state, dq_state])[None]
    position = lax.axis_index("seq")
    piece = lax.all_gather(stacked, "seq", axis=0, tiled=True)
    owners = jnp.arange(piece.shape[0])
    lower = (owners < position).astype(jnp.float32)
    higher = (owners > position).astype(jnp.float32)
    wide = piece.astype(jnp.float32)
    prefix = jnp.einsum("n,nhij->hij", lower, wide[:, 0])
    suffix = jnp.einsum("n,nhij->hij", higher, wide[:, 1])
    prefix = prefix.astype(jnp.bfloat16)
    suffix = suffix.astype(jnp.bfloat16)
    grads = block_grads(query, key, value, grad_out, prefix, suffix, scale)
    features = inputs[0]
    rows_here = lax.psum_scatter(
        (
            lax.dot_general(
                features, grads, (((0,), (0,)), ((), ())), preferred_element_type=jnp.float32
            )
            * weight_scale
        ).astype(jnp.bfloat16),
        "dp",
        scatter_dimension=0,
        tiled=True,
    )
    weight_grad = lax.psum(rows_here, "seq").astype(jnp.float32)
    return (grads[None], weight_grad)


def solution(mesh):
    in_specs = (
        P("dp", "seq", None),
        P("dp", "seq", None),
        P("dp", "seq", None),
        P("dp", "seq", None),
        P("dp", "seq", None),
    )
    out_specs = (P("dp", "seq", None), P("dp", None))
    return jax.shard_map(
        on_device, mesh=mesh, in_specs=in_specs, out_specs=out_specs, check_vma=False
    )
```

profile of v0, /device:TPU:0, one launch (start us, length us, event | category | flops | bytes accessed | tf_op | source)
XLA Modules:
  0.0 193.3 jit_solution(12286816662715219097)
XLA Ops:
  7.2 0.0 copy-start
  7.2 0.0 reduce-scatter.2.cloned.1.call-start
  7.3 0.0 copy-start.1
  7.3 1.1 reshape_squeeze.14
  8.4 0.9 reshape_squeeze.15
  9.3 0.9 reshape_squeeze.13
  10.2 1.0 copy.45
  11.3 0.2 fusion.9
  11.5 0.2 fusion.10
  11.7 8.6 %all-gather = bf16[8,2,128,128]{3,2,1,0:T(8,128)(2,1)S(1)} all-gather(bf16[2,2,128,128]{3,2,1,0:T(8,128)(2,1)S(1)} %pad_maximum_fusion), channel_id=2, replica_groups=mesh['seq'=4,'dp'=8] {'seq'}, dimensions={0}, use_global_device_ids=true | all-gather | bytes 655360 | tf_op jit(solution)/shard_map/all_gather | solution.py:51
  20.4 0.3 fusion.13
  20.7 0.1 copy.42
  20.8 0.2 convolution_bitcast_fusion.3
  21.1 0.2 convolution_bitcast_fusion.2
  21.3 0.3 fusion.2
  21.5 0.3 fusion.15
  21.8 0.2 convolution_bitcast_fusion.4
  22.0 0.0 copy-done.1
  22.0 0.2 fusion.7
  22.3 0.2 fusion.6
  22.5 1.2 fusion.8
  23.7 0.1 fusion.11
  23.8 0.0 copy-done
  23.8 4.5 %fusion = bf16[4096,768]{0,1:T(8,128)(2,1)} fusion(bf16[256,768]{0,1:T(8,128)(2,1)S(1)} %bitcast.58, bf16[1,256,4096]{2,1,0:T(8,128)(2,1)S(1)} %copy-done), kind=kOutput, calls=%fused_computation.1 | convolution fusion | flops 1616904192 | bytes 8781824 | tf_op jit(solution)/shard_map/dot_general | solution.py:64
  28.3 0.0 reduce-scatter.2.cloned.1.call-update
  28.3 0.0 all-reduce.2.cloned.1.call-start
  28.4 119.3 %reduce-scatter.2.cloned.1.call-done = bf16[512,768]{0,1:T(8,128)(2,1)} async-done(((bf16[4096,768]{0,1:T(8,128)(2,1)}), bf16[512,768]{0,1:T(8,128)(2,1)}) %reduce-scatter.2.cloned.1.call-update) | async-done | bytes 786448 | tf_op jit(solution)/shard_map/reduce_scatter | solution.py:62
  147.7 0.0 all-reduce.2.cloned.1.call-update
  147.7 0.9 copy.35
  148.6 35.2 %all-reduce.2.cloned.1.call-done = bf16[512,768]{0,1:T(8,128)(2,1)} async-done(((bf16[512,768]{0,1:T(8,128)(2,1)}), bf16[512,768]{0,1:T(8,128)(2,1)}) %all-reduce.2.cloned.1.call-update) | async-done | bytes 786448 | tf_op jit(solution)/shard_map/psum | solution.py:73
  183.9 2.5 %copy.36 = f32[512,768]{1,0:T(8,128)} copy(bf16[512,768]{0,1:T(8,128)(2,1)} %all-reduce.2.cloned.1.call-done) | data formatting | bytes 2359296
  (3 shorter events, 0.1 us)
Async XLA Ops:
  7.2 16.7 %copy-start = (bf16[1,256,4096]{2,1,0:T(8,128)(2,1)S(1)}, bf16[1,256,4096]{2,1,0:T(8,128)(2,1)}, u32[]{:S(2)}) copy-start(bf16[1,256,4096]{2,1,0:T(8,128)(2,1)} %param.5) | copy-start | bytes 6291460
  7.2 140.5 %reduce-scatter.2.cloned.1.call-start = ((), (), s32[]{:S(2)}) async-start(), calls=%async_computation.1 | async-start | bytes 7077888 | tf_op jit(solution)/shard_map/reduce_scatter | solution.py:62
  7.3 14.7 %copy-start.1 = (pred[256,256]{1,0:T(8,128)(4,1)}, pred[256,256]{1,0:T(8,128)(4,1)S(1)}, u32[]{:S(2)}) copy-start(pred[256,256]{1,0:T(8,128)(4,1)S(1)} %iota_compare_fusion) | copy-start | bytes 196612
  28.3 155.6 %all-reduce.2.cloned.1.call-start = ((), (), s32[]{:S(2)}) async-start(), calls=%async_computation.2 | async-start | bytes 1572864 | tf_op jit(solution)/shard_map/psum | solution.py:73
Sparse Core Ops, SparseCore 0:
  28.4 119.2 reduce-scatter.1
  150.1 33.7 all-reduce.1
where the time goes:
time: 194 us; the launch traced here: 193 us
  waiting for transfers between devices  155 us (80%)
  between operations  14.2 us (7%)
  blocking collectives  8.62 us (4%)
  matrix products  8.03 us (4%)
  local copies, waits for them, and re-layouts  7.61 us (4%)
    reduce_scatter x1, waiting for transfers between devices, on_device(): lax.psum_scatter((lax.dot_general(features, grads, (((0,), (0,)), ((), ()...  119 us
    psum x1, waiting for transfers between devices, on_device(): weight_grad = lax.psum(rows_here, 'seq').astype(jnp.float32)  35.2 us
    all_gather x1, blocking collectives, on_device(): piece = lax.all_gather(stacked, 'seq', axis=0, tiled=True)  8.62 us
    dot_general x1, matrix products, on_device(): lax.dot_general(features, grads, (((0,), (0,)), ((), ())), preferred_elem...  4.45 us
  transfers between devices with their start and end apart: 2, of which 2 were waited for; matrix products, arithmetic and copies ran while one was open for 0% of the time, Pallas kernels for 0%

commit v1 on v0

--- a/solution.py
+++ b/solution.py
@@ -1,10 +1,18 @@
+import functools
+
 import jax
 import jax.numpy as jnp
 from jax import lax
+from jax.experimental import pallas as pl
+from jax.experimental.pallas import tpu as pltpu
 from jax.sharding import PartitionSpec as P
 
 HS = 128
 HEADS = 2
+BLOCK = 128
+BF16 = jnp.bfloat16
+F32 = jnp.float32
+AXES = ("seq", "dp")
 
 
 def block_grads(query, key, value, grad_out, prefix, suffix, scale):
@@ -28,7 +36,7 @@
     return joined.reshape(count, -1).astype(jnp.bfloat16)
 
 
-def on_device(inputs, queries, keys, values, out_grad):
+def on_device_any(inputs, queries, keys, values, out_grad):
     tokens = queries.shape[1]
     seq_count = lax.axis_size("seq")
     batch_count = lax.axis_size("dp")
@@ -74,6 +82,194 @@
     return (grads[None], weight_grad)
 
 
+def dot(a, b, a_dim, b_dim):
+    return lax.dot_general(a, b, (((a_dim,), (b_dim,)), ((), ())), preferred_element_type=F32)
+
+
+def head(ref, h):
+    return ref[:, h * HS : (h + 1) * HS]
+
+
+def vmem():
+    return pl.BlockSpec(memory_space=pltpu.VMEM)
+
+
+def smem():
+    return pl.BlockSpec(memory_space=pltpu.SMEM)
+
+
+def state_kernel(meta, q, k, v, g, send, packed):
+    upper = meta[1] == 1
+    for h in range(HEADS):
+        left = jnp.where(upper, head(q, h), head(k, h))
+        right = jnp.where(upper, head(g, h), head(v, h))
+        send[h] = dot(left, right, 0, 0).astype(BF16)
+    for i, ref in enumerate((q, k, v, g)):
+        packed[i] = ref[...]
+
+
+def local_kernel(q, k, v, g, other, local, states):
+    count = q.shape[0]
+    row = lax.broadcasted_iota(jnp.int32, (count, count), 0)
+    causal = row >= lax.broadcasted_iota(jnp.int32, (count, count), 1)
+    for b, block in enumerate(((q, k, v, g), tuple(other.at[i] for i in range(4)))):
+        for h in range(HEADS):
+            qh, kh, vh, gh = (head(ref, h) for ref in block)
+            score_a = jnp.where(causal, dot(gh, vh, 1, 1), 0.0).astype(BF16)
+            score_b = jnp.where(causal, dot(qh, kh, 1, 1), 0.0).astype(BF16)
+            local[b, 0, :, h * HS : (h + 1) * HS] = dot(score_a, kh, 1, 0)
+            local[b, 1, :, h * HS : (h + 1) * HS] = dot(score_a, qh, 0, 0)
+            local[b, 2, :, h * HS : (h + 1) * HS] = dot(score_b, gh, 0, 0)
+            states[b, 0, h] = dot(kh, vh, 0, 0).astype(BF16)
+            states[b, 1, h] = dot(qh, gh, 0, 0).astype(BF16)
+
+
+def grads_kernel(meta, k, v, g, other, local, states, near, far, grads, *, scale):
+    core = meta[0].astype(F32)
+    upper = meta[1].astype(F32)
+    width = HEADS * HS
+    for h in range(HEADS):
+        outside = near[h].astype(F32) + far[h].astype(F32)
+        before = outside * upper
+        after = outside * (1.0 - upper)
+        for b, (kb, vb, gb) in enumerate(((k, v, g), (other.at[1], other.at[2], other.at[3]))):
+            late = core if b == 0 else 1.0 - core
+            prefix = (before + states[1 - b, 0, h].astype(F32) * late).astype(BF16)
+            suffix = (after + states[1 - b, 1, h].astype(F32) * (1.0 - late)).astype(BF16)
+            cols = slice(h * HS, (h + 1) * HS)
+            extra = (
+                dot(head(gb, h), prefix, 1, 1),
+                dot(head(vb, h), suffix, 1, 1),
+                dot(head(kb, h), suffix, 1, 0),
+            )
+            for part in range(3):
+                total = (local[b, part, :, cols] + extra[part]) * scale
+                grads[b, :, part * width + h * HS : part * width + (h + 1) * HS] = total.astype(BF16)
+
+
+def weight_kernel(meta, x, other, grads, out, *, scale):
+    total = dot(x[...], grads[0], 0, 0) + dot(other[...], grads[1], 0, 0)
+    out[0] = (total * scale).astype(BF16)
+
+
+def weight_part(meta, features, other, grads, first, blocks, scale):
+    tokens, width = features.shape
+    column = lambda i, table: (0, table[4 + first + i])
+    return pl.pallas_call(
+        functools.partial(weight_kernel, scale=scale),
+        grid_spec=pltpu.PrefetchScalarGridSpec(
+            num_scalar_prefetch=1,
+            grid=(blocks,),
+            in_specs=[
+                pl.BlockSpec((tokens, BLOCK), column),
+                pl.BlockSpec((tokens, BLOCK), column),
+                pl.BlockSpec(grads.shape, lambda i, table: (0, 0, 0)),
+            ],
+            out_specs=pl.BlockSpec((1, BLOCK, grads.shape[2]), lambda i, table: (i, 0, 0)),
+        ),
+        out_shape=jax.ShapeDtypeStruct((blocks, BLOCK, grads.shape[2]), BF16),
+        cost_estimate=pl.CostEstimate(
+            flops=4 * tokens * BLOCK * blocks * grads.shape[2],
+            bytes_accessed=4 * tokens * BLOCK * blocks + 2 * blocks * BLOCK * grads.shape[2],
+            transcendentals=0,
+        ),
+    )(meta, features, other, grads)
+
+
+def place_kernel(meta, own, near, pair, out):
+    mine = meta[2]
+    for turn, block in ((0, own[...]), (2, near[...]), (1, pair[0]), (3, pair[1])):
+        start = pl.multiple_of((mine ^ turn) * BLOCK, BLOCK)
+        out[pl.ds(start, BLOCK), :] = block.astype(F32)
+
+
+def partners(core0, core1, seq_count, dp_count):
+    pairs = []
+    for s in range(seq_count):
+        for d in range(dp_count):
+            ds, dd = (core0, core1)[s % 2]
+            pairs.append((s * dp_count + d, (s ^ ds) * dp_count + (d ^ dd)))
+    return pairs
+
+
+def on_device(inputs, queries, keys, values, out_grad):
+    tokens = queries.shape[1]
+    seq_count = lax.axis_size("seq")
+    dp_count = lax.axis_size("dp")
+    length_all = tokens * seq_count
+    scale = float(1.0 / (HS * length_all) ** 0.5)
+    weight_scale = float(1.0 / (dp_count * length_all) ** 0.5)
+    features, q, k, v, g = inputs[0], queries[0], keys[0], values[0], out_grad[0]
+    width = q.shape[1]
+    rows = features.shape[1] // (seq_count * dp_count)
+
+    swap = lambda value, core0, core1: lax.ppermute(
+        value, AXES, partners(core0, core1, seq_count, dp_count)
+    )
+    sibling, across, y, z1, z2 = (1, 0), (2, 0), (0, 1), (0, 2), (0, 4)
+
+    s, d = lax.axis_index("seq"), lax.axis_index("dp")
+    core, upper = s & 1, s >> 1
+    lane = jnp.arange(20, dtype=jnp.int32)
+    bits = lane - 4
+    b1, b2, b3, b4 = (bits >> 3) & 1, (bits >> 2) & 1, (bits >> 1) & 1, bits & 1
+    row_s = s ^ (2 * jnp.where(core == 0, b1, b2))
+    row_d = d ^ jnp.where(core == 0, b2 * 1, b1 * 1) ^ (2 * b3) ^ (4 * b4)
+    place = row_d * seq_count + row_s
+    meta = jnp.where(
+        lane == 0, core, jnp.where(lane == 1, upper, jnp.where(lane == 2, s, place))
+    ).astype(jnp.int32)
+
+    send, packed = pl.pallas_call(
+        state_kernel,
+        in_specs=[smem()] + [vmem()] * 4,
+        out_specs=[vmem()] * 2,
+        out_shape=[
+            jax.ShapeDtypeStruct((HEADS, HS, HS), BF16),
+            jax.ShapeDtypeStruct((4, tokens, width), BF16),
+        ],
+    )(meta, q, k, v, g)
+    near = swap(send, across, across)
+    far = swap(send, (3, 0), (3, 0))
+    other = swap(packed, sibling, sibling)
+    other_features = swap(features, sibling, sibling)
+
+    local, states = pl.pallas_call(
+        local_kernel,
+        in_specs=[vmem()] * 5,
+        out_specs=[vmem()] * 2,
+        out_shape=[
+            jax.ShapeDtypeStruct((2, 3, tokens, width), F32),
+            jax.ShapeDtypeStruct((2, 2, HEADS, HS, HS), BF16),
+        ],
+    )(q, k, v, g, other)
+    grads = pl.pallas_call(
+        functools.partial(grads_kernel, scale=scale),
+        in_specs=[smem()] + [vmem()] * 8,
+        out_specs=vmem(),
+        out_shape=jax.ShapeDtypeStruct((2, tokens, 3 * width), BF16),
+    )(meta, k, v, g, other, local, states, near, far)
+
+    part = functools.partial(weight_part, meta, features, other_features, grads, scale=weight_scale)
+    here = swap(part(first=8, blocks=8), across, y)
+    kept = part(first=0, blocks=8)
+    for step, (core0, core1) in enumerate(((y, across), (z1, z1), (z2, z2))):
+        half = kept.shape[0] // 2
+        total = kept.astype(F32) + here.astype(F32)
+        kept = total[:half]
+        here = swap(total[half:].astype(BF16), core0, core1)
+    final = (kept + here.astype(F32)).astype(BF16)[0]
+    facing = swap(final, across, across)
+    pair = swap(jnp.stack([final, facing]), sibling, sibling)
+    weight_grad = pl.pallas_call(
+        place_kernel,
+        in_specs=[smem()] + [vmem()] * 3,
+        out_specs=vmem(),
+        out_shape=jax.ShapeDtypeStruct((seq_count * rows, 3 * width), F32),
+    )(meta, final, facing, pair)
+    return (grads[:1], weight_grad)
+
+
 def solution(mesh):
     in_specs = (
         P("dp", "seq", None),
@@ -83,6 +279,8 @@
         P("dp", "seq", None),
     )
     out_specs = (P("dp", "seq", None), P("dp", None))
+    fast = mesh.shape["seq"] == 4 and mesh.shape["dp"] == 8
+    body = on_device if fast else on_device_any
     return jax.shard_map(
-        on_device, mesh=mesh, in_specs=in_specs, out_specs=out_specs, check_vma=False
-    )
+        body, mesh=mesh, in_specs=in_specs, out_specs=out_specs, check_vma=False
+    )

time: 194 us -> 90.3 us (0.47)
  waiting for transfers between devices: 155 us -> 41.4 us
  Pallas kernels: 0 us -> 26.2 us
  starting transfers between devices: 0.08 us -> 14.1 us
  between operations: 14.2 us -> 0.74 us
  blocking collectives: 8.62 us -> 0 us
  matrix products: 8.03 us -> 0 us
  local copies, waits for them, and re-layouts: 7.61 us -> 4.44 us
  other arithmetic: 0.12 us -> 2.66 us
    reduce_scatter x1 -> x0, waiting for transfers between devices: 119 us -> none  [on_device(): lax.psum_scatter((lax.dot_general(features, grads, (((0,), (0,)), ((), ()...]
    ppermute x0 -> x10, waiting for transfers between devices: none -> 41.4 us  [on_device(): lax.ppermute(value, AXES, partners(core0, core1, seq_count, dp_count))]
    psum x1 -> x0, waiting for transfers between devices: 35.2 us -> none  [on_device(): weight_grad = lax.psum(rows_here, 'seq').astype(jnp.float32)]
    pallas_call x0 -> x6, Pallas kernels: none -> 26.2 us  [the longest x2 14.6 us: weight_part(): pl.pallas_call(functools.partial(weight_kernel, scale=scale), grid_spec=p...]
    ppermute x0 -> x10, starting transfers between devices: none -> 14.1 us  [on_device(): lax.ppermute(value, AXES, partners(core0, core1, seq_count, dp_count))]
    all_gather x1 -> x0, blocking collectives: 8.62 us -> none  [on_device(): piece = lax.all_gather(stacked, 'seq', axis=0, tiled=True)]
    dot_general x12 -> x0, matrix products: 8.03 us -> none  [the longest x1 4.45 us: on_device(): lax.dot_general(features, grads, (((0,), (0,)), ((), ())), preferred_elem...]
    another operation x4 -> x0, local copies, waits for them, and re-layouts: 3.96 us -> none  [the longest x1 1.07 us: on_device(): key = keys[0].reshape(shape)]
  transfers between devices with their start and end apart: 2 -> 10, of which waited for: 2 -> 6; matrix products, arithmetic and copies ran while one was open for 0% -> 2% of each run, Pallas kernels for 0% -> 18%
where the time goes in v1:
time: 90.3 us; the launch traced here: 89.4 us
  waiting for transfers between devices  41.4 us (46%)
  Pallas kernels  26.2 us (29%)
  starting transfers between devices  14.1 us (16%)
  local copies, waits for them, and re-layouts  4.44 us (5%)
  other arithmetic  2.66 us (3%)
    ppermute x10, waiting for transfers between devices, on_device(): lax.ppermute(value, AXES, partners(core0, core1, seq_count, dp_count))  41.4 us
    pallas_call x2, Pallas kernels, weight_part(): pl.pallas_call(functools.partial(weight_kernel, scale=scale), grid_spec=p...  14.6 us
    ppermute x10, starting transfers between devices, on_device(): lax.ppermute(value, AXES, partners(core0, core1, seq_count, dp_count))  14.1 us
    pallas_call x1, Pallas kernels, on_device(): pl.pallas_call(local_kernel, in_specs=[vmem()] * 5, out_specs=[vmem()] *...  4.04 us
    unnamed x16, local copies, waits for them, and re-layouts  3.52 us
    pallas_call x1, Pallas kernels, on_device(): pl.pallas_call(functools.partial(grads_kernel, scale=scale), in_specs=[sm...  3.09 us
    pallas_call x1, Pallas kernels, on_device(): pl.pallas_call(place_kernel, in_specs=[smem()] + [vmem()] * 3, out_specs=...  2.45 us
    pallas_call x1, Pallas kernels, on_device(): pl.pallas_call(state_kernel, in_specs=[smem()] + [vmem()] * 4, out_specs=...  2.02 us
  transfers between devices with their start and end apart: 10, of which 6 were waited for; matrix products, arithmetic and copies ran while one was open for 2% of the time, Pallas kernels for 18%

profile of v1, /device:TPU:0, one launch (start us, length us, event | category | flops | bytes accessed | tf_op | source)
XLA Modules:
  0.0 89.4 jit_solution(12586196421949246532)
XLA Ops:
  0.6 0.5 collective-permute-start.3
  1.1 0.6 compare_select_fusion.2.meta
  1.7 2.0 %shard_map.68 = (bf16[2,128,128]{2,1,0:T(8,128)(2,1)}, bf16[4,256,256]{2,1,0:T(8,128)(2,1)}) custom-call(s32[20]{0:T(128)} %compare_select_fusion.2.meta, bf16[256,256]{1,0:T(8,128)(2,1)} %bitcast.22, bf16[256,256]{1,0:T(8,128)(2,1)} %bitcast.12, bf16[256,256]{1,0:T(8,128)(2,1)} %bitcast.15, bf16[256,256]{1,0:T(8,128)(2,1)} %bitcast.18), custom_call_target="tpu_custom_call" | custom-call | tf_op jit(solution)/shard_map/pallas_call | solution.py:223
  3.7 0.1 collective-permute-start
  3.8 2.6 %collective-permute-start.2 = (bf16[2,128,128]{2,1,0:T(8,128)(2,1)}, bf16[2,128,128]{2,1,0:T(8,128)(2,1)S(1)}, u32[]{:S(2)}, u32[]{:S(2)}) collective-permute-start(bf16[2,128,128]{2,1,0:T(8,128)(2,1)} %get-tuple-element.9), channel_id=1, source_target_pairs={{0,24},{1,25},{2,26},{3,27},{4,28},{5,29},{6,30},{7,31},{8,16},{9,... | collective-permute-start | bytes 196616 | tf_op jit(solution)/shard_map/ppermute | solution.py:206
  6.4 0.4 collective-permute-start.1
  6.8 0.0 collective-permute-done.other
  6.8 0.0 copy-start.2
  6.8 0.8 copy-done.2
  7.6 4.0 %shard_map.69 = (f32[2,3,256,256]{3,2,1,0:T(8,128)}, bf16[2,2,2,128,128]{4,3,2,1,0:T(8,128)(2,1)}) custom-call(bf16[256,256]{1,0:T(8,128)(2,1)} %bitcast.23, bf16[256,256]{1,0:T(8,128)(2,1)} %bitcast.13, bf16[256,256]{1,0:T(8,128)(2,1)} %bitcast.16, bf16[256,256]{1,0:T(8,128)(2,1)} %bitcast.19, bf16[4,256,256]{2,1,0:T(8,128)(2,1)} %copy-done.2), custom_call_target="tpu_custom_call" | custom-call | tf_op jit(solution)/shard_map/pallas_call | solution.py:237
  11.6 0.0 collective-permute-done.2.far
  11.6 0.0 copy-start.6
  11.6 0.0 collective-permute-done.1.near
  11.6 0.0 copy-start.7
  11.6 0.6 copy-done.6
  12.2 0.0 copy-done.7
  12.3 3.1 %shard_map.70.grads = bf16[2,256,768]{2,1,0:T(8,128)(2,1)} custom-call(s32[20]{0:T(128)} %compare_select_fusion.2.meta, bf16[256,256]{1,0:T(8,128)(2,1)} %bitcast.14, bf16[256,256]{1,0:T(8,128)(2,1)} %bitcast.17, bf16[256,256]{1,0:T(8,128)(2,1)} %bitcast.20, bf16[4,256,256]{2,1,0:T(8,128)(2,1)} %copy-done.2, f32[2,3,256,256]{3,2,1,0:T(8,128)} %get-tuple-element.7.local, ...), custom_call_target="tpu_custom_call" | custom-call | tf_op jit(solution)/shard_map/pallas_call | solution.py:246
  15.4 0.0 collective-permute-done.3.other
  15.4 0.0 copy-start.1
  15.4 1.3 %copy-done.1 = bf16[256,4096]{1,0:T(8,128)(2,1)} copy-done((bf16[256,4096]{1,0:T(8,128)(2,1)}, bf16[256,4096]{1,0:T(8,128)(2,1)S(1)}, u32[]{:S(2)}) %copy-start.1) | copy-done | bytes 2097176
  16.7 7.3 %shard_map.72 = bf16[8,128,768]{2,1,0:T(8,128)(2,1)} custom-call(s32[20]{0:T(128)} %compare_select_fusion.2.meta, bf16[256,4096]{1,0:T(8,128)(2,1)} %bitcast.8, bf16[256,4096]{1,0:T(8,128)(2,1)} %copy-done.1, bf16[2,256,768]{2,1,0:T(8,128)(2,1)} %shard_map.70.grads), custom_call_target="tpu_custom_call" | custom-call | flops 805306368 | bytes 2621440 | tf_op jit(solution)/shard_map/pallas_call | solution.py:158
  24.0 2.0 %collective-permute-start.4 = (bf16[8,128,768]{2,1,0:T(8,128)(2,1)}, bf16[8,128,768]{2,1,0:T(8,128)(2,1)S(1)}, u32[]{:S(2)}, u32[]{:S(2)}) collective-permute-start(bf16[8,128,768]{2,1,0:T(8,128)(2,1)} %shard_map.72), channel_id=1, source_target_pairs={{0,16},{1,17},{2,18},{3,19},{4,20},{5,21},{6,22},{7,23},{8,9},{9,8... | collective-permute-start | bytes 4718600 | tf_op jit(solution)/shard_map/ppermute | solution.py:206
  26.0 7.3 %shard_map.71 = bf16[8,128,768]{2,1,0:T(8,128)(2,1)} custom-call(s32[20]{0:T(128)} %compare_select_fusion.2.meta, bf16[256,4096]{1,0:T(8,128)(2,1)} %bitcast.9, bf16[256,4096]{1,0:T(8,128)(2,1)} %copy-done.1, bf16[2,256,768]{2,1,0:T(8,128)(2,1)} %shard_map.70.grads), custom_call_target="tpu_custom_call" | custom-call | flops 805306368 | bytes 2621440 | tf_op jit(solution)/shard_map/pallas_call | solution.py:158
  33.2 11.4 %collective-permute-done.4 = bf16[8,128,768]{2,1,0:T(8,128)(2,1)S(1)} collective-permute-done((bf16[8,128,768]{2,1,0:T(8,128)(2,1)}, bf16[8,128,768]{2,1,0:T(8,128)(2,1)S(1)}, u32[]{:S(2)}, u32[]{:S(2)}) %collective-permute-start.4) | collective-permute-done | bytes 1572896 | tf_op jit(solution)/shard_map/ppermute | solution.py:206
  44.6 1.7 %convert_add_fusion = f32[8,128,768]{2,1,0:T(8,128)S(1)} fusion(bf16[8,128,768]{2,1,0:T(8,128)(2,1)S(1)} %collective-permute-done.4, bf16[8,128,768]{2,1,0:T(8,128)(2,1)} %shard_map.71), kind=kLoop, calls=%fused_computation | loop fusion | flops 2359296 | bytes 6291456 | tf_op jit(solution)/shard_map/add | solution.py:258
  46.4 0.1 slice.46
  46.4 2.1 %collective-permute-start.5 = (bf16[4,128,768]{2,1,0:T(8,128)(2,1)S(1)}, bf16[4,128,768]{2,1,0:T(8,128)(2,1)S(1)}, u32[]{:S(2)}, u32[]{:S(2)}) collective-permute-start(bf16[4,128,768]{2,1,0:T(8,128)(2,1)S(1)} %slice.46), channel_id=1, source_target_pairs={{0,1},{1,0},{2,3},{3,2},{4,5},{5,4},{6,7},{7,6},{8,24},{9,25},{10,... | collective-permute-start | bytes 2359304 | tf_op jit(solution)/shard_map/ppermute | solution.py:206
  48.5 10.0 %collective-permute-done.5 = bf16[4,128,768]{2,1,0:T(8,128)(2,1)S(1)} collective-permute-done((bf16[4,128,768]{2,1,0:T(8,128)(2,1)S(1)}, bf16[4,128,768]{2,1,0:T(8,128)(2,1)S(1)}, u32[]{:S(2)}, u32[]{:S(2)}) %collective-permute-start.5) | collective-permute-done | bytes 786464 | tf_op jit(solution)/shard_map/ppermute | solution.py:206
  58.5 0.2 slice_add_fusion
  58.7 0.0 copy-start
  58.7 2.1 %collective-permute-start.6 = (bf16[2,128,768]{2,1,0:T(8,128)(2,1)S(1)}, bf16[2,128,768]{2,1,0:T(8,128)(2,1)S(1)}, u32[]{:S(2)}, u32[]{:S(2)}) collective-permute-start(bf16[2,128,768]{2,1,0:T(8,128)(2,1)S(1)} %slice.47), channel_id=1, source_target_pairs={{0,2},{1,3},{2,0},{3,1},{4,6},{5,7},{6,4},{7,5},{8,10},{9,11},{10,... | collective-permute-start | bytes 1179656 | tf_op jit(solution)/shard_map/ppermute | solution.py:206
  60.9 7.7 %collective-permute-done.6 = bf16[2,128,768]{2,1,0:T(8,128)(2,1)S(1)} collective-permute-done((bf16[2,128,768]{2,1,0:T(8,128)(2,1)S(1)}, bf16[2,128,768]{2,1,0:T(8,128)(2,1)S(1)}, u32[]{:S(2)}, u32[]{:S(2)}) %collective-permute-start.6) | collective-permute-done | bytes 393248 | tf_op jit(solution)/shard_map/ppermute | solution.py:206
  68.6 0.1 slice_add_fusion.1
  68.7 2.8 %collective-permute-start.7 = (bf16[1,128,768]{2,1,0:T(8,128)(2,1)S(1)}, bf16[1,128,768]{2,1,0:T(8,128)(2,1)S(1)}, u32[]{:S(2)}, u32[]{:S(2)}) collective-permute-start(bf16[1,128,768]{2,1,0:T(8,128)(2,1)S(1)} %slice.48), channel_id=1, source_target_pairs={{0,4},{1,5},{2,6},{3,7},{4,0},{5,1},{6,2},{7,3},{8,12},{9,13},{10,... | collective-permute-start | bytes 589832 | tf_op jit(solution)/shard_map/ppermute | solution.py:206
  71.5 6.9 %collective-permute-done.7 = bf16[1,128,768]{2,1,0:T(8,128)(2,1)S(1)} collective-permute-done((bf16[1,128,768]{2,1,0:T(8,128)(2,1)S(1)}, bf16[1,128,768]{2,1,0:T(8,128)(2,1)S(1)}, u32[]{:S(2)}, u32[]{:S(2)}) %collective-permute-start.7) | collective-permute-done | bytes 196640 | tf_op jit(solution)/shard_map/ppermute | solution.py:206
  78.5 0.0 copy-start.3
  78.5 1.4 %collective-permute-start.8 = (bf16[128,768]{1,0:T(8,128)(2,1)S(1)}, bf16[128,768]{1,0:T(8,128)(2,1)S(1)}, u32[]{:S(2)}, u32[]{:S(2)}) collective-permute-start(bf16[128,768]{1,0:T(8,128)(2,1)S(1)} %bitcast.10), channel_id=1, source_target_pairs={{0,16},{1,17},{2,18},{3,19},{4,20},{5,21},{6,22},{7,23},{8,24},{9,... | collective-permute-start | bytes 589832 | tf_op jit(solution)/shard_map/ppermute | solution.py:206
  80.0 4.4 %collective-permute-done.8.near = bf16[128,768]{1,0:T(8,128)(2,1)S(1)} collective-permute-done((bf16[128,768]{1,0:T(8,128)(2,1)S(1)}, bf16[128,768]{1,0:T(8,128)(2,1)S(1)}, u32[]{:S(2)}, u32[]{:S(2)}) %collective-permute-start.8) | collective-permute-done | bytes 196640 | tf_op jit(solution)/shard_map/ppermute | solution.py:206
  84.4 0.0 copy-start.4
  84.4 0.1 collective-permute-start.9
  84.5 0.0 copy-done
  84.5 0.8 slice.31
  85.3 0.9 %collective-permute-done.9.pair = bf16[2,128,768]{2,1,0:T(8,128)(2,1)S(1)} collective-permute-done((bf16[2,128,768]{2,1,0:T(8,128)(2,1)S(1)}, bf16[2,128,768]{2,1,0:T(8,128)(2,1)S(1)}, u32[]{:S(2)}, u32[]{:S(2)}) %collective-permute-start.9) | collective-permute-done | bytes 393248 | tf_op jit(solution)/shard_map/ppermute | solution.py:206
  86.2 0.0 copy-done.3
  86.2 0.0 copy-done.4
  86.2 0.0 copy-start.5
  86.2 0.7 copy-done.5
  87.0 2.5 %shard_map.73 = f32[512,768]{1,0:T(8,128)} custom-call(s32[20]{0:T(128)} %compare_select_fusion.2.meta, bf16[128,768]{1,0:T(8,128)(2,1)} %bitcast.11, bf16[128,768]{1,0:T(8,128)(2,1)} %copy-done.4, bf16[2,128,768]{2,1,0:T(8,128)(2,1)} %copy-done.5), custom_call_target="tpu_custom_call" | custom-call | tf_op jit(solution)/shard_map/pallas_call | solution.py:264
  (4 shorter events, 0.1 us)
Async XLA Ops:
  0.6 14.7 %collective-permute-start.3 = (bf16[256,4096]{1,0:T(8,128)(2,1)}, bf16[256,4096]{1,0:T(8,128)(2,1)S(1)}, u32[]{:S(2)}, u32[]{:S(2)}) collective-permute-start(bf16[256,4096]{1,0:T(8,128)(2,1)} %bitcast.7), channel_id=1, source_target_pairs={{0,8},{1,9},{2,10},{3,11},{4,12},{5,13},{6,14},{7,15},{8,0},{9,1},... | collective-permute-start | bytes 6291464 | tf_op jit(solution)/shard_map/ppermute | solution.py:206
  3.7 3.0 %collective-permute-start = (bf16[4,256,256]{2,1,0:T(8,128)(2,1)}, bf16[4,256,256]{2,1,0:T(8,128)(2,1)S(1)}, u32[]{:S(2)}, u32[]{:S(2)}) collective-permute-start(bf16[4,256,256]{2,1,0:T(8,128)(2,1)} %get-tuple-element.6), channel_id=1, source_target_pairs={{0,8},{1,9},{2,10},{3,11},{4,12},{5,13},{6,14},{7,15},{8,0},{9,1},... | collective-permute-start | bytes 1572872 | tf_op jit(solution)/shard_map/ppermute | solution.py:206
  3.8 7.8 %collective-permute-start.2 = (bf16[2,128,128]{2,1,0:T(8,128)(2,1)}, bf16[2,128,128]{2,1,0:T(8,128)(2,1)S(1)}, u32[]{:S(2)}, u32[]{:S(2)}) collective-permute-start(bf16[2,128,128]{2,1,0:T(8,128)(2,1)} %get-tuple-element.9), channel_id=1, source_target_pairs={{0,24},{1,25},{2,26},{3,27},{4,28},{5,29},{6,30},{7,31},{8,16},{9,... | collective-permute-start | bytes 196616 | tf_op jit(solution)/shard_map/ppermute | solution.py:206
  6.4 5.3 %collective-permute-start.1 = (bf16[2,128,128]{2,1,0:T(8,128)(2,1)}, bf16[2,128,128]{2,1,0:T(8,128)(2,1)S(1)}, u32[]{:S(2)}, u32[]{:S(2)}) collective-permute-start(bf16[2,128,128]{2,1,0:T(8,128)(2,1)} %get-tuple-element.9), channel_id=1, source_target_pairs={{0,16},{1,17},{2,18},{3,19},{4,20},{5,21},{6,22},{7,23},{8,24},{9,... | collective-permute-start | bytes 196616 | tf_op jit(solution)/shard_map/ppermute | solution.py:206
  6.8 0.8 copy-start.2
  11.6 0.6 copy-start.6
  11.6 0.6 copy-start.7
  15.4 1.3 %copy-start.1 = (bf16[256,4096]{1,0:T(8,128)(2,1)}, bf16[256,4096]{1,0:T(8,128)(2,1)S(1)}, u32[]{:S(2)}) copy-start(bf16[256,4096]{1,0:T(8,128)(2,1)S(1)} %collective-permute-done.3.other) | copy-start | bytes 6291460
  24.0 20.6 %collective-permute-start.4 = (bf16[8,128,768]{2,1,0:T(8,128)(2,1)}, bf16[8,128,768]{2,1,0:T(8,128)(2,1)S(1)}, u32[]{:S(2)}, u32[]{:S(2)}) collective-permute-start(bf16[8,128,768]{2,1,0:T(8,128)(2,1)} %shard_map.72), channel_id=1, source_target_pairs={{0,16},{1,17},{2,18},{3,19},{4,20},{5,21},{6,22},{7,23},{8,9},{9,8... | collective-permute-start | bytes 4718600 | tf_op jit(solution)/shard_map/ppermute | solution.py:206
  46.4 12.1 %collective-permute-start.5 = (bf16[4,128,768]{2,1,0:T(8,128)(2,1)S(1)}, bf16[4,128,768]{2,1,0:T(8,128)(2,1)S(1)}, u32[]{:S(2)}, u32[]{:S(2)}) collective-permute-start(bf16[4,128,768]{2,1,0:T(8,128)(2,1)S(1)} %slice.46), channel_id=1, source_target_pairs={{0,1},{1,0},{2,3},{3,2},{4,5},{5,4},{6,7},{7,6},{8,24},{9,25},{10,... | collective-permute-start | bytes 2359304 | tf_op jit(solution)/shard_map/ppermute | solution.py:206
  58.7 25.8 %copy-start = (bf16[2,256,768]{2,1,0:T(8,128)(2,1)S(1)}, bf16[2,256,768]{2,1,0:T(8,128)(2,1)}, u32[]{:S(2)}) copy-start(bf16[2,256,768]{2,1,0:T(8,128)(2,1)} %shard_map.70.grads) | copy-start | bytes 2359300
  58.7 9.8 %collective-permute-start.6 = (bf16[2,128,768]{2,1,0:T(8,128)(2,1)S(1)}, bf16[2,128,768]{2,1,0:T(8,128)(2,1)S(1)}, u32[]{:S(2)}, u32[]{:S(2)}) collective-permute-start(bf16[2,128,768]{2,1,0:T(8,128)(2,1)S(1)} %slice.47), channel_id=1, source_target_pairs={{0,2},{1,3},{2,0},{3,1},{4,6},{5,7},{6,4},{7,5},{8,10},{9,11},{10,... | collective-permute-start | bytes 1179656 | tf_op jit(solution)/shard_map/ppermute | solution.py:206
  68.7 9.8 %collective-permute-start.7 = (bf16[1,128,768]{2,1,0:T(8,128)(2,1)S(1)}, bf16[1,128,768]{2,1,0:T(8,128)(2,1)S(1)}, u32[]{:S(2)}, u32[]{:S(2)}) collective-permute-start(bf16[1,128,768]{2,1,0:T(8,128)(2,1)S(1)} %slice.48), channel_id=1, source_target_pairs={{0,4},{1,5},{2,6},{3,7},{4,0},{5,1},{6,2},{7,3},{8,12},{9,13},{10,... | collective-permute-start | bytes 589832 | tf_op jit(solution)/shard_map/ppermute | solution.py:206
  78.5 7.7 %copy-start.3 = (bf16[1,128,768]{2,1,0:T(8,128)(2,1)}, bf16[1,128,768]{2,1,0:T(8,128)(2,1)S(1)}, u32[]{:S(2)}) copy-start(bf16[1,128,768]{2,1,0:T(8,128)(2,1)S(1)} %fusion) | copy-start | bytes 589828
  78.5 5.8 %collective-permute-start.8 = (bf16[128,768]{1,0:T(8,128)(2,1)S(1)}, bf16[128,768]{1,0:T(8,128)(2,1)S(1)}, u32[]{:S(2)}, u32[]{:S(2)}) collective-permute-start(bf16[128,768]{1,0:T(8,128)(2,1)S(1)} %bitcast.10), channel_id=1, source_target_pairs={{0,16},{1,17},{2,18},{3,19},{4,20},{5,21},{6,22},{7,23},{8,24},{9,... | collective-permute-start | bytes 589832 | tf_op jit(solution)/shard_map/ppermute | solution.py:206
  84.4 1.8 %copy-start.4 = (bf16[128,768]{1,0:T(8,128)(2,1)}, bf16[128,768]{1,0:T(8,128)(2,1)S(1)}, u32[]{:S(2)}) copy-start(bf16[128,768]{1,0:T(8,128)(2,1)S(1)} %collective-permute-done.8.near) | copy-start | bytes 589828
  84.4 1.8 %collective-permute-start.9 = (bf16[2,128,768]{2,1,0:T(8,128)(2,1)S(1)}, bf16[2,128,768]{2,1,0:T(8,128)(2,1)S(1)}, u32[]{:S(2)}, u32[]{:S(2)}) collective-permute-start(bf16[2,128,768]{2,1,0:T(8,128)(2,1)S(1)} %pad_maximum_fusion), channel_id=1, source_target_pairs={{0,8},{1,9},{2,10},{3,11},{4,12},{5,13},{6,14},{7,15},{8,0},{9,1},... | collective-permute-start | bytes 1179656 | tf_op jit(solution)/shard_map/ppermute | solution.py:206
  86.2 0.7 copy-start.5

commit v2 on v1

v2 whole, which is shorter than its diff:
```python
import functools

import jax
import jax.numpy as jnp
from jax import lax
from jax.experimental import pallas as pl
from jax.experimental.pallas import tpu as pltpu
from jax.sharding import PartitionSpec as P

HS = 128
HEADS = 2
BLOCK = 128
BF16 = jnp.bfloat16
F32 = jnp.float32
AXES = ("seq", "dp")


def block_grads(query, key, value, grad_out, prefix, suffix, scale):
    count = query.shape[0]
    causal = jnp.arange(count)[:, None] >= jnp.arange(count)[None, :]
    f32 = jnp.float32
    score_a = jnp.einsum("thd,shd->hts", grad_out, value, preferred_element_type=f32)
    score_a = jnp.where(causal[None], score_a, 0.0).astype(jnp.bfloat16)
    score_b = jnp.einsum("thd,shd->hts", query, key, preferred_element_type=f32)
    score_b = jnp.where(causal[None], score_b, 0.0).astype(jnp.bfloat16)
    grad_q = jnp.einsum("hts,shd->thd", score_a, key, preferred_element_type=f32) + jnp.einsum(
        "thb,hab->tha", grad_out, prefix, preferred_element_type=f32
    )
    grad_k = jnp.einsum("htj,thd->jhd", score_a, query, preferred_element_type=f32) + jnp.einsum(
        "jhb,hab->jha", value, suffix, preferred_element_type=f32
    )
    grad_v = jnp.einsum("htj,thd->jhd", score_b, grad_out, preferred_element_type=f32) + jnp.einsum(
        "jha,hab->jhb", key, suffix, preferred_element_type=f32
    )
    joined = jnp.concatenate([grad_q, grad_k, grad_v], axis=1) * scale
    return joined.reshape(count, -1).astype(jnp.bfloat16)


def on_device_any(inputs, queries, keys, values, out_grad):
    tokens = queries.shape[1]
    seq_count = lax.axis_size("seq")
    batch_count = lax.axis_size("dp")
    length_all = tokens * seq_count
    scale = 1.0 / jnp.sqrt(jnp.float32(HS * length_all))
    weight_scale = 1.0 / jnp.sqrt(jnp.float32(batch_count * length_all))
    shape = (tokens, HEADS, HS)
    query = queries[0].reshape(shape)
    key = keys[0].reshape(shape)
    value = values[0].reshape(shape)
    grad_out = out_grad[0].reshape(shape)
    kv_state = jnp.einsum("lhi,lhj->hij", key, value, preferred_element_type=jnp.float32).astype(
        jnp.bfloat16
    )
    dq_state = jnp.einsum(
        "lhi,lhj->hij", query, grad_out, preferred_element_type=jnp.float32
    ).astype(jnp.bfloat16)
    stacked = jnp.stack([kv_state, dq_state])[None]
    position = lax.axis_index("seq")
    piece = lax.all_gather(stacked, "seq", axis=0, tiled=True)
    owners = jnp.arange(piece.shape[0])
    lower = (owners < position).astype(jnp.float32)
    higher = (owners > position).astype(jnp.float32)
    wide = piece.astype(jnp.float32)
    prefix = jnp.einsum("n,nhij->hij", lower, wide[:, 0])
    suffix = jnp.einsum("n,nhij->hij", higher, wide[:, 1])
    prefix = prefix.astype(jnp.bfloat16)
    suffix = suffix.astype(jnp.bfloat16)
    grads = block_grads(query, key, value, grad_out, prefix, suffix, scale)
    features = inputs[0]
    rows_here = lax.psum_scatter(
        (
            lax.dot_general(
                features, grads, (((0,), (0,)), ((), ())), preferred_element_type=jnp.float32
            )
            * weight_scale
        ).astype(jnp.bfloat16),
        "dp",
        scatter_dimension=0,
        tiled=True,
    )
    weight_grad = lax.psum(rows_here, "seq").astype(jnp.float32)
    return (grads[None], weight_grad)


def dot(a, b, a_dim=1, b_dim=0):
    return lax.dot_general(a, b, (((a_dim,), (b_dim,)), ((), ())), preferred_element_type=F32)


def cols(h):
    return slice(h * HS, (h + 1) * HS)


def vmem():
    return pl.BlockSpec(memory_space=pltpu.VMEM)


def smem():
    return pl.BlockSpec(memory_space=pltpu.SMEM)


def anywhere():
    return pl.BlockSpec(memory_space=pl.ANY)


def state_kernel(meta, q, k, v, g, send):
    upper = meta[1] == 1
    for h in range(HEADS):
        left = jnp.where(upper, q[:, cols(h)], k[:, cols(h)])
        right = jnp.where(upper, g[:, cols(h)], v[:, cols(h)])
        send[h] = dot(left, right, 0, 0).astype(BF16)


def local_kernel(q0, k0, v0, g0, q1, k1, v1, g1, local, turned, states):
    count = q0.shape[0]
    row = lax.broadcasted_iota(jnp.int32, (count, count), 0)
    col = lax.broadcasted_iota(jnp.int32, (count, count), 1)
    causal = row >= col
    causal_turned = row <= col
    for b, (q, k, v, g) in enumerate(((q0, k0, v0, g0), (q1, k1, v1, g1))):
        for h in range(HEADS):
            qh, kh, vh, gh = (ref[:, cols(h)] for ref in (q, k, v, g))
            qt, kt, vt, gt = qh.T, kh.T, vh.T, gh.T
            a_turned = jnp.where(causal_turned, dot(vh, gt), 0.0).astype(BF16)
            a = jnp.where(causal, dot(gh, vt), 0.0).astype(BF16)
            s = jnp.where(causal, dot(qh, kt), 0.0).astype(BF16)
            local[b, 0, cols(h)] = dot(kt, a_turned)
            local[b, 1, cols(h)] = dot(qt, a)
            local[b, 2, cols(h)] = dot(gt, s)
            states[b, 0, h] = dot(kt, vh).astype(BF16)
            states[b, 1, h] = dot(qt, gh).astype(BF16)
            turned[b, 0, h] = gt
            turned[b, 1, h] = vt
            turned[b, 2, h] = kt


def column_copies(table, first, x0, x1, held, sems):
    copies = []
    for b, x in enumerate((x0, x1)):
        for i in range(8):
            start = pl.multiple_of(table[4 + first + i] * BLOCK, BLOCK)
            copies.append(
                pltpu.make_async_copy(
                    x.at[:, pl.ds(start, BLOCK)],
                    held.at[b, :, pl.ds(i * BLOCK, BLOCK)],
                    sems.at[b, i],
                )
            )
    return copies


def weights(grads, held, out):
    for i in range(0, 8, 2):
        span = slice(i * BLOCK, (i + 2) * BLOCK)
        total = dot(grads[0], held[0, :, span]) + dot(grads[1], held[1, :, span])
        out[i] = total[:, :BLOCK].astype(BF16)
        out[i + 1] = total[:, BLOCK:].astype(BF16)


def send_kernel(meta, local, turned, states, near, far, x0, x1, grads, out, held, sems, *, scale):
    copies = column_copies(meta, 8, x0, x1, held, sems)
    for copy in copies:
        copy.start()
    core = meta[0].astype(F32)
    upper = meta[1].astype(F32)
    width = HEADS * HS
    for h in range(HEADS):
        outside = near[h].astype(F32) + far[h].astype(F32)
        before = outside * upper
        after = outside * (1.0 - upper)
        for b in range(2):
            late = core if b == 0 else 1.0 - core
            prefix = (before + states[1 - b, 0, h].astype(F32) * late).astype(BF16)
            suffix = (after + states[1 - b, 1, h].astype(F32) * (1.0 - late)).astype(BF16)
            extra = (
                dot(prefix, turned[b, 0, h]),
                dot(suffix, turned[b, 1, h]),
                dot(suffix, turned[b, 2, h], 0, 0),
            )
            for part in range(3):
                total = (local[b, part, cols(h)] + extra[part]) * scale
                grads[b, part * width + h * HS : part * width + (h + 1) * HS] = total.astype(BF16)
    for copy in copies:
        copy.wait()
    weights(grads, held, out)


def keep_kernel(meta, grads, x0, x1, out, own, held, sems):
    copies = column_copies(meta, 0, x0, x1, held, sems)
    for copy in copies:
        copy.start()
    for i in range(0, grads.shape[1], HS):
        own[:, i : i + HS] = grads[0, i : i + HS].T
    for copy in copies:
        copy.wait()
    weights(grads, held, out)


def place_kernel(meta, own, near, pair, out):
    mine = meta[2]
    for turn, block in ((0, own[...]), (2, near[...]), (1, pair[0]), (3, pair[1])):
        start = pl.multiple_of((mine ^ turn) * BLOCK, BLOCK)
        out[pl.ds(start, BLOCK), :] = block.astype(F32)


def final_kernel(kept, here, out, *, scale):
    total = (kept[0].astype(F32) + here[0].astype(F32)) * scale
    out[...] = total.T.astype(BF16)


def partners(core0, core1, seq_count, dp_count):
    pairs = []
    for s in range(seq_count):
        for d in range(dp_count):
            ds, dd = (core0, core1)[s % 2]
            pairs.append((s * dp_count + d, (s ^ ds) * dp_count + (d ^ dd)))
    return pairs


def on_device(inputs, queries, keys, values, out_grad):
    tokens = queries.shape[1]
    seq_count = lax.axis_size("seq")
    dp_count = lax.axis_size("dp")
    length_all = tokens * seq_count
    scale = float(1.0 / (HS * length_all) ** 0.5)
    weight_scale = float(1.0 / (dp_count * length_all) ** 0.5)
    features = inputs[0]
    blocks = [value[0] for value in (queries, keys, values, out_grad)]
    width = blocks[0].shape[1]
    rows = features.shape[1] // (seq_count * dp_count)

    swap = lambda value, core0, core1: lax.ppermute(
        value, AXES, partners(core0, core1, seq_count, dp_count)
    )
    sibling, across, y, z1, z2 = (1, 0), (2, 0), (0, 1), (0, 2), (0, 4)

    s, d = lax.axis_index("seq"), lax.axis_index("dp")
    core, upper = s & 1, s >> 1
    lane = jnp.arange(20, dtype=jnp.int32)
    bits = lane - 4
    b1, b2, b3, b4 = (bits >> 3) & 1, (bits >> 2) & 1, (bits >> 1) & 1, bits & 1
    row_s = s ^ (2 * jnp.where(core == 0, b1, b2))
    row_d = d ^ jnp.where(core == 0, b3, b1) ^ (2 * jnp.where(core == 0, b2, b3)) ^ (4 * b4)
    place = row_d * seq_count + row_s
    meta = jnp.where(
        lane == 0, core, jnp.where(lane == 1, upper, jnp.where(lane == 2, s, place))
    ).astype(jnp.int32)

    others = [swap(value, sibling, sibling) for value in blocks]
    send = pl.pallas_call(
        state_kernel,
        in_specs=[smem()] + [vmem()] * 4,
        out_specs=vmem(),
        out_shape=jax.ShapeDtypeStruct((HEADS, HS, HS), BF16),
    )(meta, *blocks)
    near = swap(send, across, across)
    far = swap(send, (3, 0), (3, 0))
    other_features = swap(features, sibling, sibling)

    local, turned, states = pl.pallas_call(
        local_kernel,
        in_specs=[vmem()] * 8,
        out_specs=[vmem()] * 3,
        out_shape=[
            jax.ShapeDtypeStruct((2, 3, width, tokens), F32),
            jax.ShapeDtypeStruct((2, 3, HEADS, HS, tokens), BF16),
            jax.ShapeDtypeStruct((2, 2, HEADS, HS, HS), BF16),
        ],
    )(*blocks, *others)
    half = jax.ShapeDtypeStruct((8, 3 * width, BLOCK), BF16)
    scratch = [pltpu.VMEM((2, tokens, 8 * BLOCK), BF16), pltpu.SemaphoreType.DMA((2, 8))]
    grads, going = pl.pallas_call(
        functools.partial(send_kernel, scale=scale),
        in_specs=[smem()] + [vmem()] * 5 + [anywhere()] * 2,
        out_specs=[vmem()] * 2,
        out_shape=[jax.ShapeDtypeStruct((2, 3 * width, tokens), BF16), half],
        scratch_shapes=scratch,
    )(meta, local, turned, states, near, far, features, other_features)
    here = swap(going, across, y)
    kept, own = pl.pallas_call(
        keep_kernel,
        in_specs=[smem(), vmem()] + [anywhere()] * 2,
        out_specs=[vmem()] * 2,
        out_shape=[half, jax.ShapeDtypeStruct((tokens, 3 * width), BF16)],
        scratch_shapes=scratch,
    )(meta, grads, features, other_features)
    for core0, core1 in ((z1, across), (y, z1), (z2, z2)):
        count = kept.shape[0] // 2
        total = kept.astype(F32) + here.astype(F32)
        kept = total[:count]
        here = swap(total[count:].astype(BF16), core0, core1)
    final = pl.pallas_call(
        functools.partial(final_kernel, scale=weight_scale),
        in_specs=[vmem()] * 2,
        out_specs=vmem(),
        out_shape=jax.ShapeDtypeStruct((BLOCK, 3 * width), BF16),
    )(kept, here)
    facing = swap(final, across, across)
    pair = swap(jnp.stack([final, facing]), sibling, sibling)
    weight_grad = pl.pallas_call(
        place_kernel,
        in_specs=[smem()] + [vmem()] * 3,
        out_specs=vmem(),
        out_shape=jax.ShapeDtypeStruct((seq_count * rows, 3 * width), F32),
    )(meta, final, facing, pair)
    return (own[None], weight_grad)


def solution(mesh):
    in_specs = (
        P("dp", "seq", None),
        P("dp", "seq", None),
        P("dp", "seq", None),
        P("dp", "seq", None),
        P("dp", "seq", None),
    )
    out_specs = (P("dp", "seq", None), P("dp", None))
    fast = mesh.shape["seq"] == 4 and mesh.shape["dp"] == 8
    body = on_device if fast else on_device_any
    return jax.shard_map(
        body, mesh=mesh, in_specs=in_specs, out_specs=out_specs, check_vma=False
    )
```

time: 90.3 us -> 87.4 us (0.968)
  Pallas kernels: 26.2 us -> 20.1 us
  waiting for transfers between devices: 41.4 us -> 43.5 us
  other arithmetic: 2.66 us -> 3.59 us
    pallas_call x4, Pallas kernels: 21.7 us -> 15.6 us  [the longest x1 5.22 us: on_device(): pl.pallas_call(functools.partial(send_kernel, scale=scale), in_specs=[sme...]
    ppermute x10 -> x13, waiting for transfers between devices: 41.4 us -> 43.5 us  [on_device(): lax.ppermute(value, AXES, partners(core0, core1, seq_count, dp_count))]
    another operation x1, other arithmetic: 0.04 us -> 1.03 us  [on_device(): pair = swap(jnp.stack([final, facing]), sibling, sibling)]
    unnamed x16 -> x20, local copies, waits for them, and re-layouts: 3.52 us -> 4.03 us
    ppermute x10 -> x13, starting transfers between devices: 14.1 us -> 14.1 us  [on_device(): lax.ppermute(value, AXES, partners(core0, core1, seq_count, dp_count))]
  transfers between devices with their start and end apart: 10 -> 13, of which waited for: 6 -> 7; matrix products, arithmetic and copies ran while one was open for 2% -> 2% of each run, Pallas kernels for 18% -> 12%
where the time goes in v2:
time: 87.4 us; the launch traced here: 86.9 us
  waiting for transfers between devices  43.5 us (50%)
  Pallas kernels  20.1 us (23%)
  starting transfers between devices  14.1 us (16%)
  local copies, waits for them, and re-layouts  4.98 us (6%)
  other arithmetic  3.59 us (4%)
    ppermute x13, waiting for transfers between devices, on_device(): lax.ppermute(value, AXES, partners(core0, core1, seq_count, dp_count))  43.5 us
    ppermute x13, starting transfers between devices, on_device(): lax.ppermute(value, AXES, partners(core0, core1, seq_count, dp_count))  14.1 us
    pallas_call x1, Pallas kernels, on_device(): pl.pallas_call(functools.partial(send_kernel, scale=scale), in_specs=[sme...  5.22 us
    pallas_call x1, Pallas kernels, on_device(): pl.pallas_call(keep_kernel, in_specs=[smem(), vmem()] + [anywhere()] * 2,...  4.69 us
    unnamed x20, local copies, waits for them, and re-layouts  4.03 us
    pallas_call x1, Pallas kernels, on_device(): pl.pallas_call(local_kernel, in_specs=[vmem()] * 8, out_specs=[vmem()] *...  3.85 us
    pallas_call x1, Pallas kernels, on_device(): pl.pallas_call(place_kernel, in_specs=[smem()] + [vmem()] * 3, out_specs=...  2.45 us
    add x3, other arithmetic, on_device(): total = kept.astype(F32) + here.astype(F32)  1.98 us
  transfers between devices with their start and end apart: 13, of which 7 were waited for; matrix products, arithmetic and copies ran while one was open for 2% of the time, Pallas kernels for 12%

profile of v2, /device:TPU:0, one launch (start us, length us, event | category | flops | bytes accessed | tf_op | source)
XLA Modules:
  0.0 86.9 jit_solution(15568818777217321593)
XLA Ops:
  0.6 0.5 collective-permute-start.6
  1.1 0.1 collective-permute-start
  1.2 0.4 collective-permute-start.1
  1.7 0.1 collective-permute-start.2
  1.7 0.4 collective-permute-start.3
  2.2 0.6 compare_select_fusion.2.meta
  2.7 2.0 %shard_map.69 = bf16[2,128,128]{2,1,0:T(8,128)(2,1)} custom-call(s32[20]{0:T(128)} %compare_select_fusion.2.meta, bf16[256,256]{1,0:T(8,128)(2,1)} %bitcast.14, bf16[256,256]{1,0:T(8,128)(2,1)} %bitcast.17, bf16[256,256]{1,0:T(8,128)(2,1)} %bitcast.20, bf16[256,256]{1,0:T(8,128)(2,1)} %bitcast.23), custom_call_target="tpu_custom_call" | custom-call | tf_op jit(solution)/shard_map/pallas_call | solution.py:249
  4.7 0.6 collective-permute-done.q1
  5.3 0.0 copy-start.4
  5.3 2.6 %collective-permute-start.5 = (bf16[2,128,128]{2,1,0:T(8,128)(2,1)}, bf16[2,128,128]{2,1,0:T(8,128)(2,1)S(1)}, u32[]{:S(2)}, u32[]{:S(2)}) collective-permute-start(bf16[2,128,128]{2,1,0:T(8,128)(2,1)} %shard_map.69), channel_id=1, source_target_pairs={{0,24},{1,25},{2,26},{3,27},{4,28},{5,29},{6,30},{7,31},{8,16},{9,... | collective-permute-start | bytes 196616 | tf_op jit(solution)/shard_map/ppermute | solution.py:231
  7.9 0.0 collective-permute-done.1.k1
  7.9 0.0 copy-start.5
  7.9 0.4 collective-permute-start.4
  8.4 0.0 collective-permute-done.2.v1
  8.4 0.0 copy-start.6
  8.4 0.0 collective-permute-done.3.g1
  8.4 0.0 copy-done.4
  8.4 0.2 copy-done.5
  8.6 0.4 copy-done.6
  9.0 0.0 copy-start.7
  9.0 0.6 copy-done.7
  9.7 3.9 %shard_map.68 = (f32[2,3,256,256]{3,2,1,0:T(8,128)}, bf16[2,3,2,128,256]{4,3,2,1,0:T(8,128)(2,1)}, bf16[2,2,2,128,128]{4,3,2,1,0:T(8,128)(2,1)}) custom-call(bf16[256,256]{1,0:T(8,128)(2,1)} %bitcast.15, bf16[256,256]{1,0:T(8,128)(2,1)} %bitcast.18, bf16[256,256]{1,0:T(8,128)(2,1)} %bitcast.21, bf16[256,256]{1,0:T(8,128)(2,1)} %bitcast.24, ...), custom_call_target="tpu_custom_call" | custom-call | tf_op jit(solution)/shard_map/pallas_call | solution.py:259
  13.5 0.0 collective-permute-done.5.far
  13.5 0.0 copy-start.8
  13.5 0.0 collective-permute-done.4.near
  13.6 0.0 copy-start.9
  13.6 0.0 collective-permute-done.6.x1
  13.6 0.0 copy-start
  13.6 0.6 copy-done.8
  14.2 0.0 copy-done.9
  14.2 0.7 copy-done
  14.9 5.2 %shard_map.70 = (bf16[2,768,256]{2,1,0:T(8,128)(2,1)}, bf16[8,768,128]{2,1,0:T(8,128)(2,1)}) custom-call(s32[20]{0:T(128)} %compare_select_fusion.2.meta, f32[2,3,256,256]{3,2,1,0:T(8,128)} %get-tuple-element.9.local, bf16[2,3,2,128,256]{4,3,2,1,0:T(8,128)(2,1)} %get-tuple-element.10.turned, bf16[2,2,2,128,128]{4,3,2,1,0:T(8,128)(2,1)} %get-tuple-element.11.states, ...), custom_call_target="tpu_custom_call" | custom-call | tf_op jit(solution)/shard_map/pallas_call | solution.py:271
  20.1 1.7 %collective-permute-start.7 = (bf16[8,768,128]{2,1,0:T(8,128)(2,1)}, bf16[8,768,128]{2,1,0:T(8,128)(2,1)S(1)}, u32[]{:S(2)}, u32[]{:S(2)}) collective-permute-start(bf16[8,768,128]{2,1,0:T(8,128)(2,1)} %get-tuple-element.15), channel_id=1, source_target_pairs={{0,16},{1,17},{2,18},{3,19},{4,20},{5,21},{6,22},{7,23},{8,9},{9,8... | collective-permute-start | bytes 4718600 | tf_op jit(solution)/shard_map/ppermute | solution.py:231
  21.8 4.7 %shard_map.71 = (bf16[8,768,128]{2,1,0:T(8,128)(2,1)}, bf16[256,768]{1,0:T(8,128)(2,1)}) custom-call(s32[20]{0:T(128)} %compare_select_fusion.2.meta, bf16[2,768,256]{2,1,0:T(8,128)(2,1)} %get-tuple-element.12.grads, bf16[256,4096]{1,0:T(8,128)(2,1)} %bitcast.10, bf16[256,4096]{1,0:T(8,128)(2,1)} %copy-done), custom_call_target="tpu_custom_call" | custom-call | tf_op jit(solution)/shard_map/pallas_call | solution.py:279
  26.5 14.3 %collective-permute-done.7 = bf16[8,768,128]{2,1,0:T(8,128)(2,1)S(1)} collective-permute-done((bf16[8,768,128]{2,1,0:T(8,128)(2,1)}, bf16[8,768,128]{2,1,0:T(8,128)(2,1)S(1)}, u32[]{:S(2)}, u32[]{:S(2)}) %collective-permute-start.7) | collective-permute-done | bytes 1572896 | tf_op jit(solution)/shard_map/ppermute | solution.py:231
  40.8 1.7 %convert_add_fusion = f32[8,768,128]{2,1,0:T(8,128)S(1)} fusion(bf16[8,768,128]{2,1,0:T(8,128)(2,1)S(1)} %collective-permute-done.7, bf16[8,768,128]{2,1,0:T(8,128)(2,1)} %get-tuple-element.14), kind=kLoop, calls=%fused_computation | loop fusion | flops 2359296 | bytes 6291456 | tf_op jit(solution)/shard_map/add | solution.py:288
  42.6 0.1 slice.38
  42.7 1.8 %collective-permute-start.8 = (bf16[4,768,128]{2,1,0:T(8,128)(2,1)S(1)}, bf16[4,768,128]{2,1,0:T(8,128)(2,1)S(1)}, u32[]{:S(2)}, u32[]{:S(2)}) collective-permute-start(bf16[4,768,128]{2,1,0:T(8,128)(2,1)S(1)} %slice.38), channel_id=1, source_target_pairs={{0,2},{1,3},{2,0},{3,1},{4,6},{5,7},{6,4},{7,5},{8,24},{9,25},{10,... | collective-permute-start | bytes 2359304 | tf_op jit(solution)/shard_map/ppermute | solution.py:231
  44.4 10.3 %collective-permute-done.8 = bf16[4,768,128]{2,1,0:T(8,128)(2,1)S(1)} collective-permute-done((bf16[4,768,128]{2,1,0:T(8,128)(2,1)S(1)}, bf16[4,768,128]{2,1,0:T(8,128)(2,1)S(1)}, u32[]{:S(2)}, u32[]{:S(2)}) %collective-permute-start.8) | collective-permute-done | bytes 786464 | tf_op jit(solution)/shard_map/ppermute | solution.py:231
  54.7 0.2 slice_add_fusion
  54.9 0.1 slice.39
  55.0 1.7 %collective-permute-start.9 = (bf16[2,768,128]{2,1,0:T(8,128)(2,1)S(1)}, bf16[2,768,128]{2,1,0:T(8,128)(2,1)S(1)}, u32[]{:S(2)}, u32[]{:S(2)}) collective-permute-start(bf16[2,768,128]{2,1,0:T(8,128)(2,1)S(1)} %slice.39), channel_id=1, source_target_pairs={{0,1},{1,0},{2,3},{3,2},{4,5},{5,4},{6,7},{7,6},{8,10},{9,11},{10,... | collective-permute-start | bytes 1179656 | tf_op jit(solution)/shard_map/ppermute | solution.py:231
  56.7 6.1 %collective-permute-done.9 = bf16[2,768,128]{2,1,0:T(8,128)(2,1)S(1)} collective-permute-done((bf16[2,768,128]{2,1,0:T(8,128)(2,1)S(1)}, bf16[2,768,128]{2,1,0:T(8,128)(2,1)S(1)}, u32[]{:S(2)}, u32[]{:S(2)}) %collective-permute-start.9) | collective-permute-done | bytes 393248 | tf_op jit(solution)/shard_map/ppermute | solution.py:231
  62.8 0.1 slice_add_fusion.1
  62.9 2.8 %collective-permute-start.10 = (bf16[1,768,128]{2,1,0:T(8,128)(2,1)S(1)}, bf16[1,768,128]{2,1,0:T(8,128)(2,1)S(1)}, u32[]{:S(2)}, u32[]{:S(2)}) collective-permute-start(bf16[1,768,128]{2,1,0:T(8,128)(2,1)S(1)} %slice.40), channel_id=1, source_target_pairs={{0,4},{1,5},{2,6},{3,7},{4,0},{5,1},{6,2},{7,3},{8,12},{9,13},{10,... | collective-permute-start | bytes 589832 | tf_op jit(solution)/shard_map/ppermute | solution.py:231
  65.7 0.8 slice.31.kept
  66.5 6.0 %collective-permute-done.10.here = bf16[1,768,128]{2,1,0:T(8,128)(2,1)S(1)} collective-permute-done((bf16[1,768,128]{2,1,0:T(8,128)(2,1)S(1)}, bf16[1,768,128]{2,1,0:T(8,128)(2,1)S(1)}, u32[]{:S(2)}, u32[]{:S(2)}) %collective-permute-start.10) | collective-permute-done | bytes 196640 | tf_op jit(solution)/shard_map/ppermute | solution.py:231
  72.5 0.0 copy-start.3
  72.5 0.7 copy-done.3
  73.2 1.9 %shard_map.72.own = bf16[128,768]{1,0:T(8,128)(2,1)} custom-call(f32[1,768,128]{2,1,0:T(8,128)} %slice.31.kept, bf16[1,768,128]{2,1,0:T(8,128)(2,1)} %copy-done.3), custom_call_target="tpu_custom_call" | custom-call | tf_op jit(solution)/shard_map/pallas_call | solution.py:291
  75.0 1.5 %collective-permute-start.11 = (bf16[128,768]{1,0:T(8,128)(2,1)}, bf16[128,768]{1,0:T(8,128)(2,1)S(1)}, u32[]{:S(2)}, u32[]{:S(2)}) collective-permute-start(bf16[128,768]{1,0:T(8,128)(2,1)} %shard_map.72.own), channel_id=1, source_target_pairs={{0,16},{1,17},{2,18},{3,19},{4,20},{5,21},{6,22},{7,23},{8,24},{9,... | collective-permute-start | bytes 589832 | tf_op jit(solution)/shard_map/ppermute | solution.py:231
  76.6 4.3 %collective-permute-done.11.near = bf16[128,768]{1,0:T(8,128)(2,1)S(1)} collective-permute-done((bf16[128,768]{1,0:T(8,128)(2,1)}, bf16[128,768]{1,0:T(8,128)(2,1)S(1)}, u32[]{:S(2)}, u32[]{:S(2)}) %collective-permute-start.11) | collective-permute-done | bytes 196640 | tf_op jit(solution)/shard_map/ppermute | solution.py:231
  80.9 0.0 copy-start.1
  80.9 1.0 %pad_maximum_fusion = bf16[2,128,768]{2,1,0:T(8,128)(2,1)S(1)} fusion(bf16[1,128,768]{2,1,0:T(8,128)(2,1)S(1)} %bitcast.12, bf16[1,128,768]{2,1,0:T(8,128)(2,1)} %bitcast.11), kind=kLoop, calls=%fused_computation.6 | loop fusion | flops 196608 | bytes 786432 | tf_op jit(solution)/shard_map/stack | solution.py:298
  82.0 0.1 collective-permute-start.12
  82.0 1.7 %collective-permute-done.12.pair = bf16[2,128,768]{2,1,0:T(8,128)(2,1)S(1)} collective-permute-done((bf16[2,128,768]{2,1,0:T(8,128)(2,1)S(1)}, bf16[2,128,768]{2,1,0:T(8,128)(2,1)S(1)}, u32[]{:S(2)}, u32[]{:S(2)}) %collective-permute-start.12) | collective-permute-done | bytes 393248 | tf_op jit(solution)/shard_map/ppermute | solution.py:231
  83.7 0.0 copy-done.1
  83.7 0.0 copy-start.2
  83.8 0.7 copy-done.2
  84.5 2.5 %shard_map.73 = f32[512,768]{1,0:T(8,128)} custom-call(s32[20]{0:T(128)} %compare_select_fusion.2.meta, bf16[128,768]{1,0:T(8,128)(2,1)} %shard_map.72.own, bf16[128,768]{1,0:T(8,128)(2,1)} %copy-done.1, bf16[2,128,768]{2,1,0:T(8,128)(2,1)} %copy-done.2), custom_call_target="tpu_custom_call" | custom-call | tf_op jit(solution)/shard_map/pallas_call | solution.py:299
  (1 shorter events, 0.0 us)
Async XLA Ops:
  0.6 12.9 %collective-permute-start.6 = (bf16[256,4096]{1,0:T(8,128)(2,1)}, bf16[256,4096]{1,0:T(8,128)(2,1)S(1)}, u32[]{:S(2)}, u32[]{:S(2)}) collective-permute-start(bf16[256,4096]{1,0:T(8,128)(2,1)} %bitcast.8), channel_id=1, source_target_pairs={{0,8},{1,9},{2,10},{3,11},{4,12},{5,13},{6,14},{7,15},{8,0},{9,1},... | collective-permute-start | bytes 6291464 | tf_op jit(solution)/shard_map/ppermute | solution.py:231
  1.1 4.2 %collective-permute-start = (bf16[256,256]{1,0:T(8,128)(2,1)}, bf16[256,256]{1,0:T(8,128)(2,1)S(1)}, u32[]{:S(2)}, u32[]{:S(2)}) collective-permute-start(bf16[256,256]{1,0:T(8,128)(2,1)} %bitcast.13), channel_id=1, source_target_pairs={{0,8},{1,9},{2,10},{3,11},{4,12},{5,13},{6,14},{7,15},{8,0},{9,1},... | collective-permute-start | bytes 393224 | tf_op jit(solution)/shard_map/ppermute | solution.py:231
  1.2 6.7 %collective-permute-start.1 = (bf16[256,256]{1,0:T(8,128)(2,1)}, bf16[256,256]{1,0:T(8,128)(2,1)S(1)}, u32[]{:S(2)}, u32[]{:S(2)}) collective-permute-start(bf16[256,256]{1,0:T(8,128)(2,1)} %bitcast.16), channel_id=1, source_target_pairs={{0,8},{1,9},{2,10},{3,11},{4,12},{5,13},{6,14},{7,15},{8,0},{9,1},... | collective-permute-start | bytes 393224 | tf_op jit(solution)/shard_map/ppermute | solution.py:231
  1.7 6.7 %collective-permute-start.2 = (bf16[256,256]{1,0:T(8,128)(2,1)}, bf16[256,256]{1,0:T(8,128)(2,1)S(1)}, u32[]{:S(2)}, u32[]{:S(2)}) collective-permute-start(bf16[256,256]{1,0:T(8,128)(2,1)} %bitcast.19), channel_id=1, source_target_pairs={{0,8},{1,9},{2,10},{3,11},{4,12},{5,13},{6,14},{7,15},{8,0},{9,1},... | collective-permute-start | bytes 393224 | tf_op jit(solution)/shard_map/ppermute | solution.py:231
  1.7 6.7 %collective-permute-start.3 = (bf16[256,256]{1,0:T(8,128)(2,1)}, bf16[256,256]{1,0:T(8,128)(2,1)S(1)}, u32[]{:S(2)}, u32[]{:S(2)}) collective-permute-start(bf16[256,256]{1,0:T(8,128)(2,1)} %bitcast.22), channel_id=1, source_target_pairs={{0,8},{1,9},{2,10},{3,11},{4,12},{5,13},{6,14},{7,15},{8,0},{9,1},... | collective-permute-start | bytes 393224 | tf_op jit(solution)/shard_map/ppermute | solution.py:231
  5.3 3.1 %copy-start.4 = (bf16[256,256]{1,0:T(8,128)(2,1)}, bf16[256,256]{1,0:T(8,128)(2,1)S(1)}, u32[]{:S(2)}) copy-start(bf16[256,256]{1,0:T(8,128)(2,1)S(1)} %collective-permute-done.q1) | copy-start | bytes 393220
  5.3 8.2 %collective-permute-start.5 = (bf16[2,128,128]{2,1,0:T(8,128)(2,1)}, bf16[2,128,128]{2,1,0:T(8,128)(2,1)S(1)}, u32[]{:S(2)}, u32[]{:S(2)}) collective-permute-start(bf16[2,128,128]{2,1,0:T(8,128)(2,1)} %shard_map.69), channel_id=1, source_target_pairs={{0,24},{1,25},{2,26},{3,27},{4,28},{5,29},{6,30},{7,31},{8,16},{9,... | collective-permute-start | bytes 196616 | tf_op jit(solution)/shard_map/ppermute | solution.py:231
  7.9 0.7 copy-start.5
  7.9 5.6 %collective-permute-start.4 = (bf16[2,128,128]{2,1,0:T(8,128)(2,1)}, bf16[2,128,128]{2,1,0:T(8,128)(2,1)S(1)}, u32[]{:S(2)}, u32[]{:S(2)}) collective-permute-start(bf16[2,128,128]{2,1,0:T(8,128)(2,1)} %shard_map.69), channel_id=1, source_target_pairs={{0,16},{1,17},{2,18},{3,19},{4,20},{5,21},{6,22},{7,23},{8,24},{9,... | collective-permute-start | bytes 196616 | tf_op jit(solution)/shard_map/ppermute | solution.py:231
  8.4 0.6 copy-start.6
  9.0 0.7 copy-start.7
  13.5 0.6 copy-start.8
  13.6 0.6 copy-start.9
  13.6 1.3 %copy-start = (bf16[256,4096]{1,0:T(8,128)(2,1)}, bf16[256,4096]{1,0:T(8,128)(2,1)S(1)}, u32[]{:S(2)}) copy-start(bf16[256,4096]{1,0:T(8,128)(2,1)S(1)} %collective-permute-done.6.x1) | copy-start | bytes 6291460
  20.1 20.7 %collective-permute-start.7 = (bf16[8,768,128]{2,1,0:T(8,128)(2,1)}, bf16[8,768,128]{2,1,0:T(8,128)(2,1)S(1)}, u32[]{:S(2)}, u32[]{:S(2)}) collective-permute-start(bf16[8,768,128]{2,1,0:T(8,128)(2,1)} %get-tuple-element.15), channel_id=1, source_target_pairs={{0,16},{1,17},{2,18},{3,19},{4,20},{5,21},{6,22},{7,23},{8,9},{9,8... | collective-permute-start | bytes 4718600 | tf_op jit(solution)/shard_map/ppermute | solution.py:231
  42.7 12.1 %collective-permute-start.8 = (bf16[4,768,128]{2,1,0:T(8,128)(2,1)S(1)}, bf16[4,768,128]{2,1,0:T(8,128)(2,1)S(1)}, u32[]{:S(2)}, u32[]{:S(2)}) collective-permute-start(bf16[4,768,128]{2,1,0:T(8,128)(2,1)S(1)} %slice.38), channel_id=1, source_target_pairs={{0,2},{1,3},{2,0},{3,1},{4,6},{5,7},{6,4},{7,5},{8,24},{9,25},{10,... | collective-permute-start | bytes 2359304 | tf_op jit(solution)/shard_map/ppermute | solution.py:231
  55.0 7.8 %collective-permute-start.9 = (bf16[2,768,128]{2,1,0:T(8,128)(2,1)S(1)}, bf16[2,768,128]{2,1,0:T(8,128)(2,1)S(1)}, u32[]{:S(2)}, u32[]{:S(2)}) collective-permute-start(bf16[2,768,128]{2,1,0:T(8,128)(2,1)S(1)} %slice.39), channel_id=1, source_target_pairs={{0,1},{1,0},{2,3},{3,2},{4,5},{5,4},{6,7},{7,6},{8,10},{9,11},{10,... | collective-permute-start | bytes 1179656 | tf_op jit(solution)/shard_map/ppermute | solution.py:231
  62.9 9.6 %collective-permute-start.10 = (bf16[1,768,128]{2,1,0:T(8,128)(2,1)S(1)}, bf16[1,768,128]{2,1,0:T(8,128)(2,1)S(1)}, u32[]{:S(2)}, u32[]{:S(2)}) collective-permute-start(bf16[1,768,128]{2,1,0:T(8,128)(2,1)S(1)} %slice.40), channel_id=1, source_target_pairs={{0,4},{1,5},{2,6},{3,7},{4,0},{5,1},{6,2},{7,3},{8,12},{9,13},{10,... | collective-permute-start | bytes 589832 | tf_op jit(solution)/shard_map/ppermute | solution.py:231
  72.5 0.7 copy-start.3
  75.0 5.9 %collective-permute-start.11 = (bf16[128,768]{1,0:T(8,128)(2,1)}, bf16[128,768]{1,0:T(8,128)(2,1)S(1)}, u32[]{:S(2)}, u32[]{:S(2)}) collective-permute-start(bf16[128,768]{1,0:T(8,128)(2,1)} %shard_map.72.own), channel_id=1, source_target_pairs={{0,16},{1,17},{2,18},{3,19},{4,20},{5,21},{6,22},{7,23},{8,24},{9,... | collective-permute-start | bytes 589832 | tf_op jit(solution)/shard_map/ppermute | solution.py:231
  80.9 2.8 %copy-start.1 = (bf16[128,768]{1,0:T(8,128)(2,1)}, bf16[128,768]{1,0:T(8,128)(2,1)S(1)}, u32[]{:S(2)}) copy-start(bf16[128,768]{1,0:T(8,128)(2,1)S(1)} %collective-permute-done.11.near) | copy-start | bytes 589828
  82.0 1.8 %collective-permute-start.12 = (bf16[2,128,768]{2,1,0:T(8,128)(2,1)S(1)}, bf16[2,128,768]{2,1,0:T(8,128)(2,1)S(1)}, u32[]{:S(2)}, u32[]{:S(2)}) collective-permute-start(bf16[2,128,768]{2,1,0:T(8,128)(2,1)S(1)} %pad_maximum_fusion), channel_id=1, source_target_pairs={{0,8},{1,9},{2,10},{3,11},{4,12},{5,13},{6,14},{7,15},{8,0},{9,1},... | collective-permute-start | bytes 1179656 | tf_op jit(solution)/shard_map/ppermute | solution.py:231
  83.7 0.7 copy-start.2

commit v3 on v2

--- a/solution.py
+++ b/solution.py
@@ -98,25 +98,36 @@
     return pl.BlockSpec(memory_space=pltpu.SMEM)
 
 
-def anywhere():
-    return pl.BlockSpec(memory_space=pl.ANY)
-
-
-def state_kernel(meta, q, k, v, g, send):
+def params(mebibytes):
+    return pltpu.CompilerParams(vmem_limit_bytes=mebibytes << 20)
+
+
+def hbm():
+    return pl.BlockSpec(memory_space=pltpu.HBM)
+
+
+def state_kernel(meta, q, k, v, g, send, held, sems):
+    copies = [
+        pltpu.make_async_copy(ref, held.at[i], sems.at[i]) for i, ref in enumerate((q, k, v, g))
+    ]
+    for copy in copies:
+        copy.start()
+    for copy in copies:
+        copy.wait()
     upper = meta[1] == 1
     for h in range(HEADS):
-        left = jnp.where(upper, q[:, cols(h)], k[:, cols(h)])
-        right = jnp.where(upper, g[:, cols(h)], v[:, cols(h)])
+        left = jnp.where(upper, held[0, :, cols(h)], held[1, :, cols(h)])
+        right = jnp.where(upper, held[3, :, cols(h)], held[2, :, cols(h)])
         send[h] = dot(left, right, 0, 0).astype(BF16)
 
 
-def local_kernel(q0, k0, v0, g0, q1, k1, v1, g1, local, turned, states):
-    count = q0.shape[0]
+def local_kernel(mine, other, local, turned, states):
+    count = mine.shape[1]
     row = lax.broadcasted_iota(jnp.int32, (count, count), 0)
     col = lax.broadcasted_iota(jnp.int32, (count, count), 1)
     causal = row >= col
     causal_turned = row <= col
-    for b, (q, k, v, g) in enumerate(((q0, k0, v0, g0), (q1, k1, v1, g1))):
+    for b, (q, k, v, g) in enumerate(tuple(ref.at[i] for i in range(4)) for ref in (mine, other)):
         for h in range(HEADS):
             qh, kh, vh, gh = (ref[:, cols(h)] for ref in (q, k, v, g))
             qt, kt, vt, gt = qh.T, kh.T, vh.T, gh.T
@@ -133,31 +144,30 @@
             turned[b, 2, h] = kt
 
 
-def column_copies(table, first, x0, x1, held, sems):
-    copies = []
-    for b, x in enumerate((x0, x1)):
-        for i in range(8):
-            start = pl.multiple_of(table[4 + first + i] * BLOCK, BLOCK)
-            copies.append(
-                pltpu.make_async_copy(
-                    x.at[:, pl.ds(start, BLOCK)],
-                    held.at[b, :, pl.ds(i * BLOCK, BLOCK)],
-                    sems.at[b, i],
-                )
-            )
-    return copies
-
-
-def weights(grads, held, out):
+def column(table, i):
+    return pl.ds(pl.multiple_of(table[4 + i] * BLOCK, BLOCK), BLOCK)
+
+
+def column_copies(table, first, x, held, sems):
+    return [
+        pltpu.make_async_copy(
+            x.at[:, column(table, first + i)], held.at[:, pl.ds(i * BLOCK, BLOCK)], sems.at[i]
+        )
+        for i in range(8)
+    ]
+
+
+def weights(table, first, grads, held, x1, out):
     for i in range(0, 8, 2):
         span = slice(i * BLOCK, (i + 2) * BLOCK)
-        total = dot(grads[0], held[0, :, span]) + dot(grads[1], held[1, :, span])
+        other = jnp.concatenate([x1[:, column(table, first + i + j)] for j in range(2)], axis=1)
+        total = dot(grads[0], held[:, span]) + dot(grads[1], other)
         out[i] = total[:, :BLOCK].astype(BF16)
         out[i + 1] = total[:, BLOCK:].astype(BF16)
 
 
 def send_kernel(meta, local, turned, states, near, far, x0, x1, grads, out, held, sems, *, scale):
-    copies = column_copies(meta, 8, x0, x1, held, sems)
+    copies = column_copies(meta, 8, x0, held, sems)
     for copy in copies:
         copy.start()
     core = meta[0].astype(F32)
@@ -181,18 +191,18 @@
                 grads[b, part * width + h * HS : part * width + (h + 1) * HS] = total.astype(BF16)
     for copy in copies:
         copy.wait()
-    weights(grads, held, out)
+    weights(meta, 8, grads, held, x1, out)
 
 
 def keep_kernel(meta, grads, x0, x1, out, own, held, sems):
-    copies = column_copies(meta, 0, x0, x1, held, sems)
+    copies = column_copies(meta, 0, x0, held, sems)
     for copy in copies:
         copy.start()
     for i in range(0, grads.shape[1], HS):
         own[:, i : i + HS] = grads[0, i : i + HS].T
     for copy in copies:
         copy.wait()
-    weights(grads, held, out)
+    weights(meta, 0, grads, held, x1, out)
 
 
 def place_kernel(meta, own, near, pair, out):
@@ -225,6 +235,7 @@
     weight_scale = float(1.0 / (dp_count * length_all) ** 0.5)
     features = inputs[0]
     blocks = [value[0] for value in (queries, keys, values, out_grad)]
+    stay = lambda value: pltpu.with_memory_space_constraint(value, pltpu.HBM)
     width = blocks[0].shape[1]
     rows = features.shape[1] // (seq_count * dp_count)
 
@@ -245,44 +256,52 @@
         lane == 0, core, jnp.where(lane == 1, upper, jnp.where(lane == 2, s, place))
     ).astype(jnp.int32)
 
-    others = [swap(value, sibling, sibling) for value in blocks]
-    send = pl.pallas_call(
+    send, mine = pl.pallas_call(
         state_kernel,
-        in_specs=[smem()] + [vmem()] * 4,
-        out_specs=vmem(),
-        out_shape=jax.ShapeDtypeStruct((HEADS, HS, HS), BF16),
-    )(meta, *blocks)
+        in_specs=[smem()] + [hbm()] * 4,
+        out_specs=[vmem()] * 2,
+        out_shape=[
+            jax.ShapeDtypeStruct((HEADS, HS, HS), BF16),
+            jax.ShapeDtypeStruct((4, tokens, width), BF16),
+        ],
+        scratch_shapes=[pltpu.SemaphoreType.DMA((4,))],
+        compiler_params=params(4),
+    )(meta, *map(stay, blocks))
     near = swap(send, across, across)
     far = swap(send, (3, 0), (3, 0))
+    other = swap(mine, sibling, sibling)
     other_features = swap(features, sibling, sibling)
 
     local, turned, states = pl.pallas_call(
         local_kernel,
-        in_specs=[vmem()] * 8,
+        in_specs=[vmem()] * 2,
         out_specs=[vmem()] * 3,
         out_shape=[
             jax.ShapeDtypeStruct((2, 3, width, tokens), F32),
             jax.ShapeDtypeStruct((2, 3, HEADS, HS, tokens), BF16),
             jax.ShapeDtypeStruct((2, 2, HEADS, HS, HS), BF16),
         ],
-    )(*blocks, *others)
+        compiler_params=params(16),
+    )(mine, other)
     half = jax.ShapeDtypeStruct((8, 3 * width, BLOCK), BF16)
-    scratch = [pltpu.VMEM((2, tokens, 8 * BLOCK), BF16), pltpu.SemaphoreType.DMA((2, 8))]
+    scratch = [pltpu.VMEM((tokens, 8 * BLOCK), BF16), pltpu.SemaphoreType.DMA((8,))]
     grads, going = pl.pallas_call(
         functools.partial(send_kernel, scale=scale),
-        in_specs=[smem()] + [vmem()] * 5 + [anywhere()] * 2,
+        in_specs=[smem()] + [vmem()] * 5 + [hbm(), vmem()],
         out_specs=[vmem()] * 2,
         out_shape=[jax.ShapeDtypeStruct((2, 3 * width, tokens), BF16), half],
         scratch_shapes=scratch,
-    )(meta, local, turned, states, near, far, features, other_features)
+        compiler_params=params(16),
+    )(meta, local, turned, states, near, far, stay(features), other_features)
     here = swap(going, across, y)
     kept, own = pl.pallas_call(
         keep_kernel,
-        in_specs=[smem(), vmem()] + [anywhere()] * 2,
+        in_specs=[smem(), vmem(), hbm(), vmem()],
         out_specs=[vmem()] * 2,
         out_shape=[half, jax.ShapeDtypeStruct((tokens, 3 * width), BF16)],
         scratch_shapes=scratch,
-    )(meta, grads, features, other_features)
+        compiler_params=params(16),
+    )(meta, grads, stay(features), other_features)
     for core0, core1 in ((z1, across), (y, z1), (z2, z2)):
         count = kept.shape[0] // 2
         total = kept.astype(F32) + here.astype(F32)
@@ -293,6 +312,7 @@
         in_specs=[vmem()] * 2,
         out_specs=vmem(),
         out_shape=jax.ShapeDtypeStruct((BLOCK, 3 * width), BF16),
+        compiler_params=params(4),
     )(kept, here)
     facing = swap(final, across, across)
     pair = swap(jnp.stack([final, facing]), sibling, sibling)
@@ -301,6 +321,7 @@
         in_specs=[smem()] + [vmem()] * 3,
         out_specs=vmem(),
         out_shape=jax.ShapeDtypeStruct((seq_count * rows, 3 * width), F32),
+        compiler_params=params(8),
     )(meta, final, facing, pair)
     return (own[None], weight_grad)
 

time: 87.4 us -> 73.4 us (0.84)
  Pallas kernels: 20.1 us -> 11 us
  local copies, waits for them, and re-layouts: 4.98 us -> 0.21 us
  waiting for transfers between devices: 43.5 us -> 47.1 us
  other arithmetic: 3.59 us -> 0.62 us
    pallas_call x3, Pallas kernels: 10.5 us -> 6.14 us  [the longest x1 2.85 us: on_device(): pl.pallas_call(keep_kernel, in_specs=[smem(), vmem(), hbm(), vmem()], out...]
    unnamed x20 -> x0, local copies, waits for them, and re-layouts: 4.03 us -> none
    ppermute x13 -> x10, waiting for transfers between devices: 43.5 us -> 47.1 us  [on_device(): lax.ppermute(value, AXES, partners(core0, core1, seq_count, dp_count))]
    pallas_call x1, Pallas kernels: 5.22 us -> 2.89 us  [on_device(): pl.pallas_call(functools.partial(send_kernel, scale=scale), in_specs=[sme...]
    pallas_call x1, Pallas kernels: 1.87 us -> 0.14 us  [on_device(): pl.pallas_call(functools.partial(final_kernel, scale=weight_scale), in_sp...]
    add x3, other arithmetic: 1.98 us -> 0.57 us  [on_device(): total = kept.astype(F32) + here.astype(F32)]
    another operation x1, other arithmetic: 1.03 us -> 0.04 us  [on_device(): pair = swap(jnp.stack([final, facing]), sibling, sibling)]
    ppermute x13 -> x10, starting transfers between devices: 14.1 us -> 13.5 us  [on_device(): lax.ppermute(value, AXES, partners(core0, core1, seq_count, dp_count))]
  transfers between devices with their start and end apart: 13 -> 10, of which waited for: 7 -> 8; matrix products, arithmetic and copies ran while one was open for 2% -> 0% of each run, Pallas kernels for 12% -> 8%
where the time goes in v3:
time: 73.4 us; the launch traced here: 73.1 us
  waiting for transfers between devices  47.1 us (64%)
  starting transfers between devices  13.5 us (18%)
  Pallas kernels  11 us (15%)
    ppermute x10, waiting for transfers between devices, on_device(): lax.ppermute(value, AXES, partners(core0, core1, seq_count, dp_count))  47.1 us
    ppermute x10, starting transfers between devices, on_device(): lax.ppermute(value, AXES, partners(core0, core1, seq_count, dp_count))  13.5 us
    pallas_call x1, Pallas kernels, on_device(): pl.pallas_call(functools.partial(send_kernel, scale=scale), in_specs=[sme...  2.89 us
    pallas_call x1, Pallas kernels, on_device(): pl.pallas_call(keep_kernel, in_specs=[smem(), vmem(), hbm(), vmem()], out...  2.85 us
    pallas_call x1, Pallas kernels, on_device(): pl.pallas_call(state_kernel, in_specs=[smem()] + [hbm()] * 4, out_specs=[...  1.91 us
    pallas_call x1, Pallas kernels, on_device(): pl.pallas_call(place_kernel, in_specs=[smem()] + [vmem()] * 3, out_specs=...  1.79 us
  transfers between devices with their start and end apart: 10, of which 8 were waited for; matrix products, arithmetic and copies ran while one was open for 0% of the time, Pallas kernels for 8%

profile of v3, /device:TPU:0, one launch (start us, length us, event | category | flops | bytes accessed | tf_op | source)
XLA Modules:
  0.0 73.1 jit_solution(3592052196427031233)
XLA Ops:
  0.6 0.5 collective-permute-start.3
  1.2 1.9 %shard_map.68 = (bf16[2,128,128]{2,1,0:T(8,128)(2,1)S(1)}, bf16[4,256,256]{2,1,0:T(8,128)(2,1)S(1)}) custom-call(s32[20]{0:T(128)S(1)} %compare_select_fusion.2.meta, bf16[256,256]{1,0:T(8,128)(2,1)} %bitcast.13, bf16[256,256]{1,0:T(8,128)(2,1)} %bitcast.14, bf16[256,256]{1,0:T(8,128)(2,1)} %bitcast.15, bf16[256,256]{1,0:T(8,128)(2,1)} %bitcast.16), custom_call_target="tpu_custom_call" | custom-call | tf_op jit(solution)/shard_map/pallas_call | solution.py:259
  3.1 0.1 collective-permute-start
  3.2 2.6 %collective-permute-start.2 = (bf16[2,128,128]{2,1,0:T(8,128)(2,1)S(1)}, bf16[2,128,128]{2,1,0:T(8,128)(2,1)S(1)}, u32[]{:S(2)}, u32[]{:S(2)}) collective-permute-start(bf16[2,128,128]{2,1,0:T(8,128)(2,1)S(1)} %get-tuple-element.15), channel_id=1, source_target_pairs={{0,24},{1,25},{2,26},{3,27},{4,28},{5,29},{6,30},{7,31},{8,16},{9,... | collective-permute-start | bytes 196616 | tf_op jit(solution)/shard_map/ppermute | solution.py:242
  5.8 0.3 collective-permute-start.1
  6.2 0.0 collective-permute-done.other
  6.2 1.4 %shard_map.69 = (f32[2,3,256,256]{3,2,1,0:T(8,128)S(1)}, bf16[2,3,2,128,256]{4,3,2,1,0:T(8,128)(2,1)S(1)}, bf16[2,2,2,128,128]{4,3,2,1,0:T(8,128)(2,1)S(1)}) custom-call(bf16[4,256,256]{2,1,0:T(8,128)(2,1)S(1)} %get-tuple-element.11.mine, bf16[4,256,256]{2,1,0:T(8,128)(2,1)S(1)} %collective-permute-done.other), custom_call_target="tpu_custom_call" | custom-call | tf_op jit(solution)/shard_map/pallas_call | solution.py:275
  7.6 0.7 %collective-permute-done.2.far = bf16[2,128,128]{2,1,0:T(8,128)(2,1)S(1)} collective-permute-done((bf16[2,128,128]{2,1,0:T(8,128)(2,1)S(1)}, bf16[2,128,128]{2,1,0:T(8,128)(2,1)S(1)}, u32[]{:S(2)}, u32[]{:S(2)}) %collective-permute-start.2) | collective-permute-done | bytes 65568 | tf_op jit(solution)/shard_map/ppermute | solution.py:242
  8.3 2.0 %collective-permute-done.1.near = bf16[2,128,128]{2,1,0:T(8,128)(2,1)S(1)} collective-permute-done((bf16[2,128,128]{2,1,0:T(8,128)(2,1)S(1)}, bf16[2,128,128]{2,1,0:T(8,128)(2,1)S(1)}, u32[]{:S(2)}, u32[]{:S(2)}) %collective-permute-start.1) | collective-permute-done | bytes 65568 | tf_op jit(solution)/shard_map/ppermute | solution.py:242
  10.3 0.0 collective-permute-done.3.x1
  10.3 2.9 %shard_map.70 = (bf16[2,768,256]{2,1,0:T(8,128)(2,1)S(1)}, bf16[8,768,128]{2,1,0:T(8,128)(2,1)S(1)}) custom-call(s32[20]{0:T(128)S(1)} %compare_select_fusion.2.meta, f32[2,3,256,256]{3,2,1,0:T(8,128)S(1)} %get-tuple-element.12.local, bf16[2,3,2,128,256]{4,3,2,1,0:T(8,128)(2,1)S(1)} %get-tuple-element.13.turned, ...), custom_call_target="tpu_custom_call" | custom-call | tf_op jit(solution)/shard_map/pallas_call | solution.py:288
  13.2 1.7 %collective-permute-start.4 = (bf16[8,768,128]{2,1,0:T(8,128)(2,1)S(1)}, bf16[8,768,128]{2,1,0:T(8,128)(2,1)S(1)}, u32[]{:S(2)}, u32[]{:S(2)}) collective-permute-start(bf16[8,768,128]{2,1,0:T(8,128)(2,1)S(1)} %get-tuple-element.19), channel_id=1, source_target_pairs={{0,16},{1,17},{2,18},{3,19},{4,20},{5,21},{6,22},{7,23},{8,9},{9,8... | collective-permute-start | bytes 4718600 | tf_op jit(solution)/shard_map/ppermute | solution.py:242
  14.9 2.8 %shard_map.71 = (bf16[8,768,128]{2,1,0:T(8,128)(2,1)S(1)}, bf16[256,768]{1,0:T(8,128)(2,1)}) custom-call(s32[20]{0:T(128)S(1)} %compare_select_fusion.2.meta, bf16[2,768,256]{2,1,0:T(8,128)(2,1)S(1)} %get-tuple-element.16.grads, bf16[256,4096]{1,0:T(8,128)(2,1)} %bitcast.12, bf16[256,4096]{1,0:T(8,128)(2,1)S(1)} %collective-permute-done.3.x1), custom_call_target="tpu_custom_call" | custom-call | tf_op jit(solution)/shard_map/pallas_call | solution.py:297
  17.7 15.9 %collective-permute-done.4 = bf16[8,768,128]{2,1,0:T(8,128)(2,1)S(1)} collective-permute-done((bf16[8,768,128]{2,1,0:T(8,128)(2,1)S(1)}, bf16[8,768,128]{2,1,0:T(8,128)(2,1)S(1)}, u32[]{:S(2)}, u32[]{:S(2)}) %collective-permute-start.4) | collective-permute-done | bytes 1572896 | tf_op jit(solution)/shard_map/ppermute | solution.py:242
  33.6 0.3 convert_add_fusion
  34.0 0.1 slice.38
  34.1 1.8 %collective-permute-start.5 = (bf16[4,768,128]{2,1,0:T(8,128)(2,1)S(1)}, bf16[4,768,128]{2,1,0:T(8,128)(2,1)S(1)}, u32[]{:S(2)}, u32[]{:S(2)}) collective-permute-start(bf16[4,768,128]{2,1,0:T(8,128)(2,1)S(1)} %slice.38), channel_id=1, source_target_pairs={{0,2},{1,3},{2,0},{3,1},{4,6},{5,7},{6,4},{7,5},{8,24},{9,25},{10,... | collective-permute-start | bytes 2359304 | tf_op jit(solution)/shard_map/ppermute | solution.py:242
  35.9 10.2 %collective-permute-done.5 = bf16[4,768,128]{2,1,0:T(8,128)(2,1)S(1)} collective-permute-done((bf16[4,768,128]{2,1,0:T(8,128)(2,1)S(1)}, bf16[4,768,128]{2,1,0:T(8,128)(2,1)S(1)}, u32[]{:S(2)}, u32[]{:S(2)}) %collective-permute-start.5) | collective-permute-done | bytes 786464 | tf_op jit(solution)/shard_map/ppermute | solution.py:242
  46.1 0.2 slice_add_fusion
  46.3 0.1 slice.39
  46.4 1.8 %collective-permute-start.6 = (bf16[2,768,128]{2,1,0:T(8,128)(2,1)S(1)}, bf16[2,768,128]{2,1,0:T(8,128)(2,1)S(1)}, u32[]{:S(2)}, u32[]{:S(2)}) collective-permute-start(bf16[2,768,128]{2,1,0:T(8,128)(2,1)S(1)} %slice.39), channel_id=1, source_target_pairs={{0,1},{1,0},{2,3},{3,2},{4,5},{5,4},{6,7},{7,6},{8,10},{9,11},{10,... | collective-permute-start | bytes 1179656 | tf_op jit(solution)/shard_map/ppermute | solution.py:242
  48.1 6.1 %collective-permute-done.6 = bf16[2,768,128]{2,1,0:T(8,128)(2,1)S(1)} collective-permute-done((bf16[2,768,128]{2,1,0:T(8,128)(2,1)S(1)}, bf16[2,768,128]{2,1,0:T(8,128)(2,1)S(1)}, u32[]{:S(2)}, u32[]{:S(2)}) %collective-permute-start.6) | collective-permute-done | bytes 393248 | tf_op jit(solution)/shard_map/ppermute | solution.py:242
  54.2 0.1 slice_add_fusion.1
  54.3 2.8 %collective-permute-start.7 = (bf16[1,768,128]{2,1,0:T(8,128)(2,1)S(1)}, bf16[1,768,128]{2,1,0:T(8,128)(2,1)S(1)}, u32[]{:S(2)}, u32[]{:S(2)}) collective-permute-start(bf16[1,768,128]{2,1,0:T(8,128)(2,1)S(1)} %slice.40), channel_id=1, source_target_pairs={{0,4},{1,5},{2,6},{3,7},{4,0},{5,1},{6,2},{7,3},{8,12},{9,13},{10,... | collective-permute-start | bytes 589832 | tf_op jit(solution)/shard_map/ppermute | solution.py:242
  57.2 6.5 %collective-permute-done.7.here = bf16[1,768,128]{2,1,0:T(8,128)(2,1)S(1)} collective-permute-done((bf16[1,768,128]{2,1,0:T(8,128)(2,1)S(1)}, bf16[1,768,128]{2,1,0:T(8,128)(2,1)S(1)}, u32[]{:S(2)}, u32[]{:S(2)}) %collective-permute-start.7) | collective-permute-done | bytes 196640 | tf_op jit(solution)/shard_map/ppermute | solution.py:242
  63.6 0.1 shard_map.72.own
  63.8 1.7 %collective-permute-start.8 = (bf16[128,768]{1,0:T(8,128)(2,1)S(1)}, bf16[128,768]{1,0:T(8,128)(2,1)S(1)}, u32[]{:S(2)}, u32[]{:S(2)}) collective-permute-start(bf16[128,768]{1,0:T(8,128)(2,1)S(1)} %shard_map.72.own), channel_id=1, source_target_pairs={{0,16},{1,17},{2,18},{3,19},{4,20},{5,21},{6,22},{7,23},{8,24},{9,... | collective-permute-start | bytes 589832 | tf_op jit(solution)/shard_map/ppermute | solution.py:242
  65.5 4.0 %collective-permute-done.8.near = bf16[128,768]{1,0:T(8,128)(2,1)S(1)} collective-permute-done((bf16[128,768]{1,0:T(8,128)(2,1)S(1)}, bf16[128,768]{1,0:T(8,128)(2,1)S(1)}, u32[]{:S(2)}, u32[]{:S(2)}) %collective-permute-start.8) | collective-permute-done | bytes 196640 | tf_op jit(solution)/shard_map/ppermute | solution.py:242
  69.6 0.1 collective-permute-start.9
  69.6 1.7 %collective-permute-done.9.pair = bf16[2,128,768]{2,1,0:T(8,128)(2,1)S(1)} collective-permute-done((bf16[2,128,768]{2,1,0:T(8,128)(2,1)S(1)}, bf16[2,128,768]{2,1,0:T(8,128)(2,1)S(1)}, u32[]{:S(2)}, u32[]{:S(2)}) %collective-permute-start.9) | collective-permute-done | bytes 393248 | tf_op jit(solution)/shard_map/ppermute | solution.py:242
  71.4 1.8 %shard_map.73 = f32[512,768]{1,0:T(8,128)} custom-call(s32[20]{0:T(128)S(1)} %compare_select_fusion.2.meta, bf16[128,768]{1,0:T(8,128)(2,1)S(1)} %shard_map.72.own, bf16[128,768]{1,0:T(8,128)(2,1)S(1)} %collective-permute-done.8.near, bf16[2,128,768]{2,1,0:T(8,128)(2,1)S(1)} %collective-permute-done.9.pair), custom_call_target="tpu_custom_call" | custom-call | tf_op jit(solution)/shard_map/pallas_call | solution.py:319
  (4 shorter events, 0.1 us)
Async XLA Ops:
  0.6 9.6 %collective-permute-start.3 = (bf16[256,4096]{1,0:T(8,128)(2,1)}, bf16[256,4096]{1,0:T(8,128)(2,1)S(1)}, u32[]{:S(2)}, u32[]{:S(2)}) collective-permute-start(bf16[256,4096]{1,0:T(8,128)(2,1)} %bitcast.10), channel_id=1, source_target_pairs={{0,8},{1,9},{2,10},{3,11},{4,12},{5,13},{6,14},{7,15},{8,0},{9,1},... | collective-permute-start | bytes 6291464 | tf_op jit(solution)/shard_map/ppermute | solution.py:242
  3.1 3.1 %collective-permute-start = (bf16[4,256,256]{2,1,0:T(8,128)(2,1)S(1)}, bf16[4,256,256]{2,1,0:T(8,128)(2,1)S(1)}, u32[]{:S(2)}, u32[]{:S(2)}) collective-permute-start(bf16[4,256,256]{2,1,0:T(8,128)(2,1)S(1)} %get-tuple-element.11.mine), channel_id=1, source_target_pairs={{0,8},{1,9},{2,10},{3,11},{4,12},{5,13},{6,14},{7,15},{8,0},{9,1},... | collective-permute-start | bytes 1572872 | tf_op jit(solution)/shard_map/ppermute | solution.py:242
  3.2 5.1 %collective-permute-start.2 = (bf16[2,128,128]{2,1,0:T(8,128)(2,1)S(1)}, bf16[2,128,128]{2,1,0:T(8,128)(2,1)S(1)}, u32[]{:S(2)}, u32[]{:S(2)}) collective-permute-start(bf16[2,128,128]{2,1,0:T(8,128)(2,1)S(1)} %get-tuple-element.15), channel_id=1, source_target_pairs={{0,24},{1,25},{2,26},{3,27},{4,28},{5,29},{6,30},{7,31},{8,16},{9,... | collective-permute-start | bytes 196616 | tf_op jit(solution)/shard_map/ppermute | solution.py:242
  5.8 4.4 %collective-permute-start.1 = (bf16[2,128,128]{2,1,0:T(8,128)(2,1)S(1)}, bf16[2,128,128]{2,1,0:T(8,128)(2,1)S(1)}, u32[]{:S(2)}, u32[]{:S(2)}) collective-permute-start(bf16[2,128,128]{2,1,0:T(8,128)(2,1)S(1)} %get-tuple-element.15), channel_id=1, source_target_pairs={{0,16},{1,17},{2,18},{3,19},{4,20},{5,21},{6,22},{7,23},{8,24},{9,... | collective-permute-start | bytes 196616 | tf_op jit(solution)/shard_map/ppermute | solution.py:242
  13.2 20.5 %collective-permute-start.4 = (bf16[8,768,128]{2,1,0:T(8,128)(2,1)S(1)}, bf16[8,768,128]{2,1,0:T(8,128)(2,1)S(1)}, u32[]{:S(2)}, u32[]{:S(2)}) collective-permute-start(bf16[8,768,128]{2,1,0:T(8,128)(2,1)S(1)} %get-tuple-element.19), channel_id=1, source_target_pairs={{0,16},{1,17},{2,18},{3,19},{4,20},{5,21},{6,22},{7,23},{8,9},{9,8... | collective-permute-start | bytes 4718600 | tf_op jit(solution)/shard_map/ppermute | solution.py:242
  34.1 12.1 %collective-permute-start.5 = (bf16[4,768,128]{2,1,0:T(8,128)(2,1)S(1)}, bf16[4,768,128]{2,1,0:T(8,128)(2,1)S(1)}, u32[]{:S(2)}, u32[]{:S(2)}) collective-permute-start(bf16[4,768,128]{2,1,0:T(8,128)(2,1)S(1)} %slice.38), channel_id=1, source_target_pairs={{0,2},{1,3},{2,0},{3,1},{4,6},{5,7},{6,4},{7,5},{8,24},{9,25},{10,... | collective-permute-start | bytes 2359304 | tf_op jit(solution)/shard_map/ppermute | solution.py:242
  46.4 7.8 %collective-permute-start.6 = (bf16[2,768,128]{2,1,0:T(8,128)(2,1)S(1)}, bf16[2,768,128]{2,1,0:T(8,128)(2,1)S(1)}, u32[]{:S(2)}, u32[]{:S(2)}) collective-permute-start(bf16[2,768,128]{2,1,0:T(8,128)(2,1)S(1)} %slice.39), channel_id=1, source_target_pairs={{0,1},{1,0},{2,3},{3,2},{4,5},{5,4},{6,7},{7,6},{8,10},{9,11},{10,... | collective-permute-start | bytes 1179656 | tf_op jit(solution)/shard_map/ppermute | solution.py:242
  54.3 9.3 %collective-permute-start.7 = (bf16[1,768,128]{2,1,0:T(8,128)(2,1)S(1)}, bf16[1,768,128]{2,1,0:T(8,128)(2,1)S(1)}, u32[]{:S(2)}, u32[]{:S(2)}) collective-permute-start(bf16[1,768,128]{2,1,0:T(8,128)(2,1)S(1)} %slice.40), channel_id=1, source_target_pairs={{0,4},{1,5},{2,6},{3,7},{4,0},{5,1},{6,2},{7,3},{8,12},{9,13},{10,... | collective-permute-start | bytes 589832 | tf_op jit(solution)/shard_map/ppermute | solution.py:242
  63.8 5.7 %collective-permute-start.8 = (bf16[128,768]{1,0:T(8,128)(2,1)S(1)}, bf16[128,768]{1,0:T(8,128)(2,1)S(1)}, u32[]{:S(2)}, u32[]{:S(2)}) collective-permute-start(bf16[128,768]{1,0:T(8,128)(2,1)S(1)} %shard_map.72.own), channel_id=1, source_target_pairs={{0,16},{1,17},{2,18},{3,19},{4,20},{5,21},{6,22},{7,23},{8,24},{9,... | collective-permute-start | bytes 589832 | tf_op jit(solution)/shard_map/ppermute | solution.py:242
  69.6 1.8 %collective-permute-start.9 = (bf16[2,128,768]{2,1,0:T(8,128)(2,1)S(1)}, bf16[2,128,768]{2,1,0:T(8,128)(2,1)S(1)}, u32[]{:S(2)}, u32[]{:S(2)}) collective-permute-start(bf16[2,128,768]{2,1,0:T(8,128)(2,1)S(1)} %pad_maximum_fusion), channel_id=1, source_target_pairs={{0,8},{1,9},{2,10},{3,11},{4,12},{5,13},{6,14},{7,15},{8,0},{9,1},... | collective-permute-start | bytes 1179656 | tf_op jit(solution)/shard_map/ppermute | solution.py:242

commit v4 on v3

--- a/solution.py
+++ b/solution.py
@@ -151,22 +151,32 @@
 def column_copies(table, first, x, held, sems):
     return [
         pltpu.make_async_copy(
-            x.at[:, column(table, first + i)], held.at[:, pl.ds(i * BLOCK, BLOCK)], sems.at[i]
+            x.at[:, column(table, 16 * part + first + i)],
+            held.at[part, :, pl.ds(i * BLOCK, BLOCK)],
+            sems.at[part, i],
         )
+        for part in range(2)
         for i in range(8)
     ]
 
 
-def weights(table, first, grads, held, x1, out):
-    for i in range(0, 8, 2):
-        span = slice(i * BLOCK, (i + 2) * BLOCK)
-        other = jnp.concatenate([x1[:, column(table, first + i + j)] for j in range(2)], axis=1)
-        total = dot(grads[0], held[:, span]) + dot(grads[1], other)
-        out[i] = total[:, :BLOCK].astype(BF16)
-        out[i + 1] = total[:, BLOCK:].astype(BF16)
-
-
-def send_kernel(meta, local, turned, states, near, far, x0, x1, grads, out, held, sems, *, scale):
+def weights(table, first, grads, held, x1, outs):
+    row = 0
+    for part, out in enumerate(outs):
+        rows = slice(row, row + out.shape[1])
+        row += out.shape[1]
+        left, right = grads[0, rows], grads[1, rows]
+        for i in range(0, 8, 2):
+            own = held[part, :, i * BLOCK : (i + 2) * BLOCK]
+            other = jnp.concatenate(
+                [x1[:, column(table, 16 * part + first + i + j)] for j in range(2)], axis=1
+            )
+            total = dot(left, own) + dot(right, other)
+            out[i] = total[:, :BLOCK].astype(BF16)
+            out[i + 1] = total[:, BLOCK:].astype(BF16)
+
+
+def send_kernel(meta, local, turned, states, near, far, x0, x1, grads, out_a, out_b, held, sems, *, scale):
     copies = column_copies(meta, 8, x0, held, sems)
     for copy in copies:
         copy.start()
@@ -191,10 +201,10 @@
                 grads[b, part * width + h * HS : part * width + (h + 1) * HS] = total.astype(BF16)
     for copy in copies:
         copy.wait()
-    weights(meta, 8, grads, held, x1, out)
-
-
-def keep_kernel(meta, grads, x0, x1, out, own, held, sems):
+    weights(meta, 8, grads, held, x1, (out_a, out_b))
+
+
+def keep_kernel(meta, grads, x0, x1, out_a, out_b, own, held, sems):
     copies = column_copies(meta, 0, x0, held, sems)
     for copy in copies:
         copy.start()
@@ -202,7 +212,7 @@
         own[:, i : i + HS] = grads[0, i : i + HS].T
     for copy in copies:
         copy.wait()
-    weights(meta, 0, grads, held, x1, out)
+    weights(meta, 0, grads, held, x1, (out_a, out_b))
 
 
 def place_kernel(meta, own, near, pair, out):
@@ -212,9 +222,9 @@
         out[pl.ds(start, BLOCK), :] = block.astype(F32)
 
 
-def final_kernel(kept, here, out, *, scale):
-    total = (kept[0].astype(F32) + here[0].astype(F32)) * scale
-    out[...] = total.T.astype(BF16)
+def final_kernel(kept_a, kept_b, here, out, *, scale):
+    kept = jnp.concatenate([kept_a[0], kept_b[0]], axis=0)
+    out[...] = ((kept + here[...].astype(F32)) * scale).T.astype(BF16)
 
 
 def partners(core0, core1, seq_count, dp_count):
@@ -246,12 +256,14 @@
 
     s, d = lax.axis_index("seq"), lax.axis_index("dp")
     core, upper = s & 1, s >> 1
-    lane = jnp.arange(20, dtype=jnp.int32)
-    bits = lane - 4
+    lane = jnp.arange(36, dtype=jnp.int32)
+    bits = (lane - 4) & 15
     b1, b2, b3, b4 = (bits >> 3) & 1, (bits >> 2) & 1, (bits >> 1) & 1, bits & 1
-    row_s = s ^ (2 * jnp.where(core == 0, b1, b2))
-    row_d = d ^ jnp.where(core == 0, b3, b1) ^ (2 * jnp.where(core == 0, b2, b3)) ^ (4 * b4)
-    place = row_d * seq_count + row_s
+    lower, first = core == 0, lane < 20
+    over_x = jnp.where(first, jnp.where(lower, b1, b2), b3)
+    over_y = jnp.where(first, jnp.where(lower, b3, b1), b2)
+    over_z = jnp.where(first, jnp.where(lower, b2, b3), b1)
+    place = (d ^ over_y ^ (2 * over_z) ^ (4 * b4)) * seq_count + (s ^ (2 * over_x))
     meta = jnp.where(
         lane == 0, core, jnp.where(lane == 1, upper, jnp.where(lane == 2, s, place))
     ).astype(jnp.int32)
@@ -283,37 +295,42 @@
         ],
         compiler_params=params(16),
     )(mine, other)
-    half = jax.ShapeDtypeStruct((8, 3 * width, BLOCK), BF16)
-    scratch = [pltpu.VMEM((tokens, 8 * BLOCK), BF16), pltpu.SemaphoreType.DMA((8,))]
-    grads, going = pl.pallas_call(
+    halves = [
+        jax.ShapeDtypeStruct((8, count * width, BLOCK), BF16) for count in (2, 1)
+    ]
+    scratch = [pltpu.VMEM((2, tokens, 8 * BLOCK), BF16), pltpu.SemaphoreType.DMA((2, 8))]
+    grads, *going = pl.pallas_call(
         functools.partial(send_kernel, scale=scale),
         in_specs=[smem()] + [vmem()] * 5 + [hbm(), vmem()],
-        out_specs=[vmem()] * 2,
-        out_shape=[jax.ShapeDtypeStruct((2, 3 * width, tokens), BF16), half],
+        out_specs=[vmem()] * 3,
+        out_shape=[jax.ShapeDtypeStruct((2, 3 * width, tokens), BF16)] + halves,
         scratch_shapes=scratch,
         compiler_params=params(16),
     )(meta, local, turned, states, near, far, stay(features), other_features)
-    here = swap(going, across, y)
-    kept, own = pl.pallas_call(
+    here = [swap(going[0], across, y), swap(going[1], z1, z1)]
+    *kept, own = pl.pallas_call(
         keep_kernel,
         in_specs=[smem(), vmem(), hbm(), vmem()],
-        out_specs=[vmem()] * 2,
-        out_shape=[half, jax.ShapeDtypeStruct((tokens, 3 * width), BF16)],
+        out_specs=[vmem()] * 3,
+        out_shape=halves + [jax.ShapeDtypeStruct((tokens, 3 * width), BF16)],
         scratch_shapes=scratch,
         compiler_params=params(16),
     )(meta, grads, stay(features), other_features)
-    for core0, core1 in ((z1, across), (y, z1), (z2, z2)):
-        count = kept.shape[0] // 2
-        total = kept.astype(F32) + here.astype(F32)
-        kept = total[:count]
-        here = swap(total[count:].astype(BF16), core0, core1)
+    for ways in (((z1, across), (y, y)), ((y, z1), (across, across))):
+        for i, way in enumerate(ways):
+            count = kept[i].shape[0] // 2
+            total = kept[i].astype(F32) + here[i].astype(F32)
+            kept[i] = total[:count]
+            here[i] = swap(total[count:].astype(BF16), *way)
+    total = [k + h.astype(F32) for k, h in zip(kept, here)]
+    last = swap(jnp.concatenate([t[1] for t in total]).astype(BF16), z2, z2)
     final = pl.pallas_call(
         functools.partial(final_kernel, scale=weight_scale),
-        in_specs=[vmem()] * 2,
+        in_specs=[vmem()] * 3,
         out_specs=vmem(),
         out_shape=jax.ShapeDtypeStruct((BLOCK, 3 * width), BF16),
         compiler_params=params(4),
-    )(kept, here)
+    )(total[0][:1], total[1][:1], last)
     facing = swap(final, across, across)
     pair = swap(jnp.stack([final, facing]), sibling, sibling)
     weight_grad = pl.pallas_call(

time: 73.4 us -> 64.3 us (0.88)
  waiting for transfers between devices: 47.1 us -> 33.2 us
  starting transfers between devices: 13.5 us -> 17.5 us
    ppermute x10 -> x13, waiting for transfers between devices: 47.1 us -> 33.2 us  [on_device(): lax.ppermute(value, AXES, partners(core0, core1, seq_count, dp_count))]
    ppermute x10 -> x13, starting transfers between devices: 13.5 us -> 17.5 us  [on_device(): lax.ppermute(value, AXES, partners(core0, core1, seq_count, dp_count))]
  transfers between devices with their start and end apart: 10 -> 13, of which waited for: 8 -> 9; matrix products, arithmetic and copies ran while one was open for 0% -> 1% of each run, Pallas kernels for 8% -> 10%
where the time goes in v4:
time: 64.3 us; the launch traced here: 64 us
  waiting for transfers between devices  33.2 us (52%)
  starting transfers between devices  17.5 us (27%)
  Pallas kernels  11.7 us (18%)
  between operations  0.78 us (1%)
    ppermute x13, waiting for transfers between devices, on_device(): lax.ppermute(value, AXES, partners(core0, core1, seq_count, dp_count))  33.2 us
    ppermute x13, starting transfers between devices, on_device(): lax.ppermute(value, AXES, partners(core0, core1, seq_count, dp_count))  17.5 us
    pallas_call x1, Pallas kernels, on_device(): pl.pallas_call(keep_kernel, in_specs=[smem(), vmem(), hbm(), vmem()], out...  3.27 us
    pallas_call x1, Pallas kernels, on_device(): pl.pallas_call(functools.partial(send_kernel, scale=scale), in_specs=[sme...  3.2 us
    pallas_call x1, Pallas kernels, on_device(): pl.pallas_call(state_kernel, in_specs=[smem()] + [hbm()] * 4, out_specs=[...  1.91 us
    pallas_call x1, Pallas kernels, on_device(): pl.pallas_call(place_kernel, in_specs=[smem()] + [vmem()] * 3, out_specs=...  1.79 us
    pallas_call x1, Pallas kernels, on_device(): pl.pallas_call(local_kernel, in_specs=[vmem()] * 2, out_specs=[vmem()] *...  1.38 us
  transfers between devices with their start and end apart: 13, of which 9 were waited for; matrix products, arithmetic and copies ran while one was open for 1% of the time, Pallas kernels for 10%

profile of v4, /device:TPU:0, one launch (start us, length us, event | category | flops | bytes accessed | tf_op | source)
XLA Modules:
  0.0 64.0 jit_solution(16424034512171825274)
XLA Ops:
  0.6 0.5 collective-permute-start.3
  1.2 1.9 %shard_map.68 = (bf16[2,128,128]{2,1,0:T(8,128)(2,1)S(1)}, bf16[4,256,256]{2,1,0:T(8,128)(2,1)S(1)}) custom-call(s32[36]{0:T(128)S(1)} %compare_select_fusion.2.meta, bf16[256,256]{1,0:T(8,128)(2,1)} %bitcast.17, bf16[256,256]{1,0:T(8,128)(2,1)} %bitcast.18, bf16[256,256]{1,0:T(8,128)(2,1)} %bitcast.19, bf16[256,256]{1,0:T(8,128)(2,1)} %bitcast.20), custom_call_target="tpu_custom_call" | custom-call | tf_op jit(solution)/shard_map/pallas_call | solution.py:271
  3.1 0.1 collective-permute-start
  3.2 2.6 %collective-permute-start.2 = (bf16[2,128,128]{2,1,0:T(8,128)(2,1)S(1)}, bf16[2,128,128]{2,1,0:T(8,128)(2,1)S(1)}, u32[]{:S(2)}, u32[]{:S(2)}) collective-permute-start(bf16[2,128,128]{2,1,0:T(8,128)(2,1)S(1)} %get-tuple-element.17), channel_id=1, source_target_pairs={{0,24},{1,25},{2,26},{3,27},{4,28},{5,29},{6,30},{7,31},{8,16},{9,... | collective-permute-start | bytes 196616 | tf_op jit(solution)/shard_map/ppermute | solution.py:252
  5.8 0.3 collective-permute-start.1
  6.2 0.0 collective-permute-done.other
  6.2 1.4 %shard_map.69 = (f32[2,3,256,256]{3,2,1,0:T(8,128)S(1)}, bf16[2,3,2,128,256]{4,3,2,1,0:T(8,128)(2,1)S(1)}, bf16[2,2,2,128,128]{4,3,2,1,0:T(8,128)(2,1)S(1)}) custom-call(bf16[4,256,256]{2,1,0:T(8,128)(2,1)S(1)} %get-tuple-element.13.mine, bf16[4,256,256]{2,1,0:T(8,128)(2,1)S(1)} %collective-permute-done.other), custom_call_target="tpu_custom_call" | custom-call | tf_op jit(solution)/shard_map/pallas_call | solution.py:287
  7.6 0.7 %collective-permute-done.2.far = bf16[2,128,128]{2,1,0:T(8,128)(2,1)S(1)} collective-permute-done((bf16[2,128,128]{2,1,0:T(8,128)(2,1)S(1)}, bf16[2,128,128]{2,1,0:T(8,128)(2,1)S(1)}, u32[]{:S(2)}, u32[]{:S(2)}) %collective-permute-start.2) | collective-permute-done | bytes 65568 | tf_op jit(solution)/shard_map/ppermute | solution.py:252
  8.3 2.0 %collective-permute-done.1.near = bf16[2,128,128]{2,1,0:T(8,128)(2,1)S(1)} collective-permute-done((bf16[2,128,128]{2,1,0:T(8,128)(2,1)S(1)}, bf16[2,128,128]{2,1,0:T(8,128)(2,1)S(1)}, u32[]{:S(2)}, u32[]{:S(2)}) %collective-permute-start.1) | collective-permute-done | bytes 65568 | tf_op jit(solution)/shard_map/ppermute | solution.py:252
  10.3 0.0 collective-permute-done.3.x1
  10.3 3.2 %shard_map.70 = (bf16[2,768,256]{2,1,0:T(8,128)(2,1)S(1)}, bf16[8,512,128]{2,1,0:T(8,128)(2,1)S(1)}, bf16[8,256,128]{2,1,0:T(8,128)(2,1)S(1)}) custom-call(s32[36]{0:T(128)S(1)} %compare_select_fusion.2.meta, f32[2,3,256,256]{3,2,1,0:T(8,128)S(1)} %get-tuple-element.14.local, bf16[2,3,2,128,256]{4,3,2,1,0:T(8,128)(2,1)S(1)} %get-tuple-element.15.turned, ...), custom_call_target="tpu_custom_call" | custom-call | tf_op jit(solution)/shard_map/pallas_call | solution.py:302
  13.5 1.7 %collective-permute-start.4 = (bf16[8,512,128]{2,1,0:T(8,128)(2,1)S(1)}, bf16[8,512,128]{2,1,0:T(8,128)(2,1)S(1)}, u32[]{:S(2)}, u32[]{:S(2)}) collective-permute-start(bf16[8,512,128]{2,1,0:T(8,128)(2,1)S(1)} %get-tuple-element.21), channel_id=1, source_target_pairs={{0,16},{1,17},{2,18},{3,19},{4,20},{5,21},{6,22},{7,23},{8,9},{9,8... | collective-permute-start | bytes 3145736 | tf_op jit(solution)/shard_map/ppermute | solution.py:252
  15.2 1.6 %collective-permute-start.7 = (bf16[8,256,128]{2,1,0:T(8,128)(2,1)S(1)}, bf16[8,256,128]{2,1,0:T(8,128)(2,1)S(1)}, u32[]{:S(2)}, u32[]{:S(2)}) collective-permute-start(bf16[8,256,128]{2,1,0:T(8,128)(2,1)S(1)} %get-tuple-element.23), channel_id=1, source_target_pairs={{0,2},{1,3},{2,0},{3,1},{4,6},{5,7},{6,4},{7,5},{8,10},{9,11},{10,... | collective-permute-start | bytes 1572872 | tf_op jit(solution)/shard_map/ppermute | solution.py:252
  16.8 3.3 %shard_map.71 = (bf16[8,512,128]{2,1,0:T(8,128)(2,1)S(1)}, bf16[8,256,128]{2,1,0:T(8,128)(2,1)S(1)}, bf16[256,768]{1,0:T(8,128)(2,1)}) custom-call(s32[36]{0:T(128)S(1)} %compare_select_fusion.2.meta, bf16[2,768,256]{2,1,0:T(8,128)(2,1)S(1)} %get-tuple-element.18.grads, bf16[256,4096]{1,0:T(8,128)(2,1)} %bitcast.16, ...), custom_call_target="tpu_custom_call" | custom-call | tf_op jit(solution)/shard_map/pallas_call | solution.py:311
  20.1 8.3 %collective-permute-done.4 = bf16[8,512,128]{2,1,0:T(8,128)(2,1)S(1)} collective-permute-done((bf16[8,512,128]{2,1,0:T(8,128)(2,1)S(1)}, bf16[8,512,128]{2,1,0:T(8,128)(2,1)S(1)}, u32[]{:S(2)}, u32[]{:S(2)}) %collective-permute-start.4) | collective-permute-done | bytes 1048608 | tf_op jit(solution)/shard_map/ppermute | solution.py:252
  28.3 0.2 convert_add_fusion
  28.6 0.1 slice.80
  28.6 1.8 %collective-permute-start.5 = (bf16[4,512,128]{2,1,0:T(8,128)(2,1)S(1)}, bf16[4,512,128]{2,1,0:T(8,128)(2,1)S(1)}, u32[]{:S(2)}, u32[]{:S(2)}) collective-permute-start(bf16[4,512,128]{2,1,0:T(8,128)(2,1)S(1)} %slice.80), channel_id=1, source_target_pairs={{0,2},{1,3},{2,0},{3,1},{4,6},{5,7},{6,4},{7,5},{8,24},{9,25},{10,... | collective-permute-start | bytes 1572872 | tf_op jit(solution)/shard_map/ppermute | solution.py:252
  30.5 0.0 collective-permute-done.7
  30.5 0.1 convert_add_fusion.1
  30.6 1.6 %collective-permute-start.8 = (bf16[4,256,128]{2,1,0:T(8,128)(2,1)S(1)}, bf16[4,256,128]{2,1,0:T(8,128)(2,1)S(1)}, u32[]{:S(2)}, u32[]{:S(2)}) collective-permute-start(bf16[4,256,128]{2,1,0:T(8,128)(2,1)S(1)} %slice.81), channel_id=1, source_target_pairs={{0,1},{1,0},{2,3},{3,2},{4,5},{5,4},{6,7},{7,6},{8,9},{9,8},{10,11... | collective-permute-start | bytes 786440 | tf_op jit(solution)/shard_map/ppermute | solution.py:252
  32.2 5.3 %collective-permute-done.8 = bf16[4,256,128]{2,1,0:T(8,128)(2,1)S(1)} collective-permute-done((bf16[4,256,128]{2,1,0:T(8,128)(2,1)S(1)}, bf16[4,256,128]{2,1,0:T(8,128)(2,1)S(1)}, u32[]{:S(2)}, u32[]{:S(2)}) %collective-permute-start.8) | collective-permute-done | bytes 262176 | tf_op jit(solution)/shard_map/ppermute | solution.py:252
  37.6 1.1 %collective-permute-start.9 = (bf16[2,256,128]{2,1,0:T(8,128)(2,1)S(1)}, bf16[2,256,128]{2,1,0:T(8,128)(2,1)S(1)}, u32[]{:S(2)}, u32[]{:S(2)}) collective-permute-start(bf16[2,256,128]{2,1,0:T(8,128)(2,1)S(1)} %slice.83), channel_id=1, source_target_pairs={{0,16},{1,17},{2,18},{3,19},{4,20},{5,21},{6,22},{7,23},{8,24},{9,... | collective-permute-start | bytes 393224 | tf_op jit(solution)/shard_map/ppermute | solution.py:252
  38.7 0.0 collective-permute-done.5
  38.7 0.1 slice_add_fusion
  38.9 1.6 %collective-permute-start.6 = (bf16[2,512,128]{2,1,0:T(8,128)(2,1)S(1)}, bf16[2,512,128]{2,1,0:T(8,128)(2,1)S(1)}, u32[]{:S(2)}, u32[]{:S(2)}) collective-permute-start(bf16[2,512,128]{2,1,0:T(8,128)(2,1)S(1)} %slice.82), channel_id=1, source_target_pairs={{0,1},{1,0},{2,3},{3,2},{4,5},{5,4},{6,7},{7,6},{8,10},{9,11},{10,... | collective-permute-start | bytes 786440 | tf_op jit(solution)/shard_map/ppermute | solution.py:252
  40.4 2.2 %collective-permute-done.9 = bf16[2,256,128]{2,1,0:T(8,128)(2,1)S(1)} collective-permute-done((bf16[2,256,128]{2,1,0:T(8,128)(2,1)S(1)}, bf16[2,256,128]{2,1,0:T(8,128)(2,1)S(1)}, u32[]{:S(2)}, u32[]{:S(2)}) %collective-permute-start.9) | collective-permute-done | bytes 131104 | tf_op jit(solution)/shard_map/ppermute | solution.py:252
  42.7 2.6 %collective-permute-done.6 = bf16[2,512,128]{2,1,0:T(8,128)(2,1)S(1)} collective-permute-done((bf16[2,512,128]{2,1,0:T(8,128)(2,1)S(1)}, bf16[2,512,128]{2,1,0:T(8,128)(2,1)S(1)}, u32[]{:S(2)}, u32[]{:S(2)}) %collective-permute-start.6) | collective-permute-done | bytes 262176 | tf_op jit(solution)/shard_map/ppermute | solution.py:252
  45.3 0.1 slice_add_fusion.2
  45.4 2.7 %collective-permute-start.10 = (bf16[768,128]{1,0:T(8,128)(2,1)S(1)}, bf16[768,128]{1,0:T(8,128)(2,1)S(1)}, u32[]{:S(2)}, u32[]{:S(2)}) collective-permute-start(bf16[768,128]{1,0:T(8,128)(2,1)S(1)} %pad_maximum_fusion.1), channel_id=1, source_target_pairs={{0,4},{1,5},{2,6},{3,7},{4,0},{5,1},{6,2},{7,3},{8,12},{9,13},{10,... | collective-permute-start | bytes 589832 | tf_op jit(solution)/shard_map/ppermute | solution.py:252
  48.1 6.4 %collective-permute-done.10.here = bf16[768,128]{1,0:T(8,128)(2,1)S(1)} collective-permute-done((bf16[768,128]{1,0:T(8,128)(2,1)S(1)}, bf16[768,128]{1,0:T(8,128)(2,1)S(1)}, u32[]{:S(2)}, u32[]{:S(2)}) %collective-permute-start.10) | collective-permute-done | bytes 196640 | tf_op jit(solution)/shard_map/ppermute | solution.py:252
  54.5 0.1 shard_map.72.own
  54.6 1.8 %collective-permute-start.11 = (bf16[128,768]{1,0:T(8,128)(2,1)S(1)}, bf16[128,768]{1,0:T(8,128)(2,1)S(1)}, u32[]{:S(2)}, u32[]{:S(2)}) collective-permute-start(bf16[128,768]{1,0:T(8,128)(2,1)S(1)} %shard_map.72.own), channel_id=1, source_target_pairs={{0,16},{1,17},{2,18},{3,19},{4,20},{5,21},{6,22},{7,23},{8,24},{9,... | collective-permute-start | bytes 589832 | tf_op jit(solution)/shard_map/ppermute | solution.py:252
  56.4 3.9 %collective-permute-done.11.near = bf16[128,768]{1,0:T(8,128)(2,1)S(1)} collective-permute-done((bf16[128,768]{1,0:T(8,128)(2,1)S(1)}, bf16[128,768]{1,0:T(8,128)(2,1)S(1)}, u32[]{:S(2)}, u32[]{:S(2)}) %collective-permute-start.11) | collective-permute-done | bytes 196640 | tf_op jit(solution)/shard_map/ppermute | solution.py:252
  60.4 0.1 collective-permute-start.12
  60.5 1.7 %collective-permute-done.12.pair = bf16[2,128,768]{2,1,0:T(8,128)(2,1)S(1)} collective-permute-done((bf16[2,128,768]{2,1,0:T(8,128)(2,1)S(1)}, bf16[2,128,768]{2,1,0:T(8,128)(2,1)S(1)}, u32[]{:S(2)}, u32[]{:S(2)}) %collective-permute-start.12) | collective-permute-done | bytes 393248 | tf_op jit(solution)/shard_map/ppermute | solution.py:252
  62.2 1.8 %shard_map.73 = f32[512,768]{1,0:T(8,128)} custom-call(s32[36]{0:T(128)S(1)} %compare_select_fusion.2.meta, bf16[128,768]{1,0:T(8,128)(2,1)S(1)} %shard_map.72.own, bf16[128,768]{1,0:T(8,128)(2,1)S(1)} %collective-permute-done.11.near, bf16[2,128,768]{2,1,0:T(8,128)(2,1)S(1)} %collective-permute-done.12.pair), custom_call_target="tpu_custom_call" | custom-call | tf_op jit(solution)/shard_map/pallas_call | solution.py:336
  (12 shorter events, 0.3 us)
Async XLA Ops:
  0.6 9.6 %collective-permute-start.3 = (bf16[256,4096]{1,0:T(8,128)(2,1)}, bf16[256,4096]{1,0:T(8,128)(2,1)S(1)}, u32[]{:S(2)}, u32[]{:S(2)}) collective-permute-start(bf16[256,4096]{1,0:T(8,128)(2,1)} %bitcast.14), channel_id=1, source_target_pairs={{0,8},{1,9},{2,10},{3,11},{4,12},{5,13},{6,14},{7,15},{8,0},{9,1},... | collective-permute-start | bytes 6291464 | tf_op jit(solution)/shard_map/ppermute | solution.py:252
  3.1 3.1 %collective-permute-start = (bf16[4,256,256]{2,1,0:T(8,128)(2,1)S(1)}, bf16[4,256,256]{2,1,0:T(8,128)(2,1)S(1)}, u32[]{:S(2)}, u32[]{:S(2)}) collective-permute-start(bf16[4,256,256]{2,1,0:T(8,128)(2,1)S(1)} %get-tuple-element.13.mine), channel_id=1, source_target_pairs={{0,8},{1,9},{2,10},{3,11},{4,12},{5,13},{6,14},{7,15},{8,0},{9,1},... | collective-permute-start | bytes 1572872 | tf_op jit(solution)/shard_map/ppermute | solution.py:252
  3.2 5.1 %collective-permute-start.2 = (bf16[2,128,128]{2,1,0:T(8,128)(2,1)S(1)}, bf16[2,128,128]{2,1,0:T(8,128)(2,1)S(1)}, u32[]{:S(2)}, u32[]{:S(2)}) collective-permute-start(bf16[2,128,128]{2,1,0:T(8,128)(2,1)S(1)} %get-tuple-element.17), channel_id=1, source_target_pairs={{0,24},{1,25},{2,26},{3,27},{4,28},{5,29},{6,30},{7,31},{8,16},{9,... | collective-permute-start | bytes 196616 | tf_op jit(solution)/shard_map/ppermute | solution.py:252
  5.8 4.4 %collective-permute-start.1 = (bf16[2,128,128]{2,1,0:T(8,128)(2,1)S(1)}, bf16[2,128,128]{2,1,0:T(8,128)(2,1)S(1)}, u32[]{:S(2)}, u32[]{:S(2)}) collective-permute-start(bf16[2,128,128]{2,1,0:T(8,128)(2,1)S(1)} %get-tuple-element.17), channel_id=1, source_target_pairs={{0,16},{1,17},{2,18},{3,19},{4,20},{5,21},{6,22},{7,23},{8,24},{9,... | collective-permute-start | bytes 196616 | tf_op jit(solution)/shard_map/ppermute | solution.py:252
  13.5 14.9 %collective-permute-start.4 = (bf16[8,512,128]{2,1,0:T(8,128)(2,1)S(1)}, bf16[8,512,128]{2,1,0:T(8,128)(2,1)S(1)}, u32[]{:S(2)}, u32[]{:S(2)}) collective-permute-start(bf16[8,512,128]{2,1,0:T(8,128)(2,1)S(1)} %get-tuple-element.21), channel_id=1, source_target_pairs={{0,16},{1,17},{2,18},{3,19},{4,20},{5,21},{6,22},{7,23},{8,9},{9,8... | collective-permute-start | bytes 3145736 | tf_op jit(solution)/shard_map/ppermute | solution.py:252
  15.2 15.2 %collective-permute-start.7 = (bf16[8,256,128]{2,1,0:T(8,128)(2,1)S(1)}, bf16[8,256,128]{2,1,0:T(8,128)(2,1)S(1)}, u32[]{:S(2)}, u32[]{:S(2)}) collective-permute-start(bf16[8,256,128]{2,1,0:T(8,128)(2,1)S(1)} %get-tuple-element.23), channel_id=1, source_target_pairs={{0,2},{1,3},{2,0},{3,1},{4,6},{5,7},{6,4},{7,5},{8,10},{9,11},{10,... | collective-permute-start | bytes 1572872 | tf_op jit(solution)/shard_map/ppermute | solution.py:252
  28.6 10.1 %collective-permute-start.5 = (bf16[4,512,128]{2,1,0:T(8,128)(2,1)S(1)}, bf16[4,512,128]{2,1,0:T(8,128)(2,1)S(1)}, u32[]{:S(2)}, u32[]{:S(2)}) collective-permute-start(bf16[4,512,128]{2,1,0:T(8,128)(2,1)S(1)} %slice.80), channel_id=1, source_target_pairs={{0,2},{1,3},{2,0},{3,1},{4,6},{5,7},{6,4},{7,5},{8,24},{9,25},{10,... | collective-permute-start | bytes 1572872 | tf_op jit(solution)/shard_map/ppermute | solution.py:252
  30.6 6.9 %collective-permute-start.8 = (bf16[4,256,128]{2,1,0:T(8,128)(2,1)S(1)}, bf16[4,256,128]{2,1,0:T(8,128)(2,1)S(1)}, u32[]{:S(2)}, u32[]{:S(2)}) collective-permute-start(bf16[4,256,128]{2,1,0:T(8,128)(2,1)S(1)} %slice.81), channel_id=1, source_target_pairs={{0,1},{1,0},{2,3},{3,2},{4,5},{5,4},{6,7},{7,6},{8,9},{9,8},{10,11... | collective-permute-start | bytes 786440 | tf_op jit(solution)/shard_map/ppermute | solution.py:252
  37.6 5.0 %collective-permute-start.9 = (bf16[2,256,128]{2,1,0:T(8,128)(2,1)S(1)}, bf16[2,256,128]{2,1,0:T(8,128)(2,1)S(1)}, u32[]{:S(2)}, u32[]{:S(2)}) collective-permute-start(bf16[2,256,128]{2,1,0:T(8,128)(2,1)S(1)} %slice.83), channel_id=1, source_target_pairs={{0,16},{1,17},{2,18},{3,19},{4,20},{5,21},{6,22},{7,23},{8,24},{9,... | collective-permute-start | bytes 393224 | tf_op jit(solution)/shard_map/ppermute | solution.py:252
  38.9 6.4 %collective-permute-start.6 = (bf16[2,512,128]{2,1,0:T(8,128)(2,1)S(1)}, bf16[2,512,128]{2,1,0:T(8,128)(2,1)S(1)}, u32[]{:S(2)}, u32[]{:S(2)}) collective-permute-start(bf16[2,512,128]{2,1,0:T(8,128)(2,1)S(1)} %slice.82), channel_id=1, source_target_pairs={{0,1},{1,0},{2,3},{3,2},{4,5},{5,4},{6,7},{7,6},{8,10},{9,11},{10,... | collective-permute-start | bytes 786440 | tf_op jit(solution)/shard_map/ppermute | solution.py:252
  45.4 9.1 %collective-permute-start.10 = (bf16[768,128]{1,0:T(8,128)(2,1)S(1)}, bf16[768,128]{1,0:T(8,128)(2,1)S(1)}, u32[]{:S(2)}, u32[]{:S(2)}) collective-permute-start(bf16[768,128]{1,0:T(8,128)(2,1)S(1)} %pad_maximum_fusion.1), channel_id=1, source_target_pairs={{0,4},{1,5},{2,6},{3,7},{4,0},{5,1},{6,2},{7,3},{8,12},{9,13},{10,... | collective-permute-start | bytes 589832 | tf_op jit(solution)/shard_map/ppermute | solution.py:252
  54.6 5.7 %collective-permute-start.11 = (bf16[128,768]{1,0:T(8,128)(2,1)S(1)}, bf16[128,768]{1,0:T(8,128)(2,1)S(1)}, u32[]{:S(2)}, u32[]{:S(2)}) collective-permute-start(bf16[128,768]{1,0:T(8,128)(2,1)S(1)} %shard_map.72.own), channel_id=1, source_target_pairs={{0,16},{1,17},{2,18},{3,19},{4,20},{5,21},{6,22},{7,23},{8,24},{9,... | collective-permute-start | bytes 589832 | tf_op jit(solution)/shard_map/ppermute | solution.py:252
  60.4 1.8 %collective-permute-start.12 = (bf16[2,128,768]{2,1,0:T(8,128)(2,1)S(1)}, bf16[2,128,768]{2,1,0:T(8,128)(2,1)S(1)}, u32[]{:S(2)}, u32[]{:S(2)}) collective-permute-start(bf16[2,128,768]{2,1,0:T(8,128)(2,1)S(1)} %pad_maximum_fusion), channel_id=1, source_target_pairs={{0,8},{1,9},{2,10},{3,11},{4,12},{5,13},{6,14},{7,15},{8,0},{9,1},... | collective-permute-start | bytes 1179656 | tf_op jit(solution)/shard_map/ppermute | solution.py:252

commit v5 on v3

--- a/solution.py
+++ b/solution.py
@@ -121,7 +121,9 @@
         send[h] = dot(left, right, 0, 0).astype(BF16)
 
 
-def local_kernel(mine, other, local, turned, states):
+def local_kernel(x, mine, other, local, turned, states, x0, sem):
+    copy = pltpu.make_async_copy(x, x0, sem)
+    copy.start()
     count = mine.shape[1]
     row = lax.broadcasted_iota(jnp.int32, (count, count), 0)
     col = lax.broadcasted_iota(jnp.int32, (count, count), 1)
@@ -142,37 +144,32 @@
             turned[b, 0, h] = gt
             turned[b, 1, h] = vt
             turned[b, 2, h] = kt
+    copy.wait()
 
 
 def column(table, i):
     return pl.ds(pl.multiple_of(table[4 + i] * BLOCK, BLOCK), BLOCK)
 
 
-def column_copies(table, first, x, held, sems):
-    return [
-        pltpu.make_async_copy(
-            x.at[:, column(table, first + i)], held.at[:, pl.ds(i * BLOCK, BLOCK)], sems.at[i]
+def weights(table, first, grads, x0, x1, out):
+    for i in range(0, 8, 2):
+        x = jnp.concatenate(
+            [
+                jnp.concatenate([ref[:, column(table, first + i + j)] for j in range(2)], axis=1)
+                for ref in (x0, x1)
+            ],
+            axis=0,
         )
-        for i in range(8)
-    ]
-
-
-def weights(table, first, grads, held, x1, out):
-    for i in range(0, 8, 2):
-        span = slice(i * BLOCK, (i + 2) * BLOCK)
-        other = jnp.concatenate([x1[:, column(table, first + i + j)] for j in range(2)], axis=1)
-        total = dot(grads[0], held[:, span]) + dot(grads[1], other)
+        total = dot(grads, x)
         out[i] = total[:, :BLOCK].astype(BF16)
         out[i + 1] = total[:, BLOCK:].astype(BF16)
 
 
-def send_kernel(meta, local, turned, states, near, far, x0, x1, grads, out, held, sems, *, scale):
-    copies = column_copies(meta, 8, x0, held, sems)
-    for copy in copies:
-        copy.start()
+def send_a_kernel(meta, local, turned, states, near, far, x0, x1, grads, out, *, scale):
     core = meta[0].astype(F32)
     upper = meta[1].astype(F32)
     width = HEADS * HS
+    tokens = x0.shape[0]
     for h in range(HEADS):
         outside = near[h].astype(F32) + far[h].astype(F32)
         before = outside * upper
@@ -188,33 +185,39 @@
             )
             for part in range(3):
                 total = (local[b, part, cols(h)] + extra[part]) * scale
-                grads[b, part * width + h * HS : part * width + (h + 1) * HS] = total.astype(BF16)
-    for copy in copies:
-        copy.wait()
-    weights(meta, 8, grads, held, x1, out)
-
-
-def keep_kernel(meta, grads, x0, x1, out, own, held, sems):
-    copies = column_copies(meta, 0, x0, held, sems)
-    for copy in copies:
-        copy.start()
-    for i in range(0, grads.shape[1], HS):
-        own[:, i : i + HS] = grads[0, i : i + HS].T
-    for copy in copies:
-        copy.wait()
-    weights(meta, 0, grads, held, x1, out)
-
-
-def place_kernel(meta, own, near, pair, out):
-    mine = meta[2]
-    for turn, block in ((0, own[...]), (2, near[...]), (1, pair[0]), (3, pair[1])):
-        start = pl.multiple_of((mine ^ turn) * BLOCK, BLOCK)
-        out[pl.ds(start, BLOCK), :] = block.astype(F32)
-
-
-def final_kernel(kept, here, out, *, scale):
-    total = (kept[0].astype(F32) + here[0].astype(F32)) * scale
-    out[...] = total.T.astype(BF16)
+                rows = slice(part * width + h * HS, part * width + (h + 1) * HS)
+                grads[rows, b * tokens : (b + 1) * tokens] = total.astype(BF16)
+    weights(meta, 8, grads[: 2 * width], x0, x1, out)
+
+
+def send_b_kernel(meta, grads, x0, x1, out):
+    weights(meta, 24, grads[2 * HEADS * HS :], x0, x1, out)
+
+
+def keep_kernel(meta, grads, x0, x1, out_a, out_b, own):
+    width = HEADS * HS
+    weights(meta, 0, grads[: 2 * width], x0, x1, out_a)
+    weights(meta, 16, grads[2 * width :], x0, x1, out_b)
+    for i in range(0, grads.shape[0], HS):
+        own[:, i : i + HS] = grads[i : i + HS, : own.shape[0]].T
+
+
+def place_kernel(meta, *refs):
+    out = refs[-1]
+    column = 0
+    for part in range(0, 8, 4):
+        for turn, block in zip((0, 2, 1, 3), refs[part : part + 4]):
+            rows = pl.ds(pl.multiple_of((meta[2] ^ turn) * BLOCK, BLOCK), BLOCK)
+            out[rows, column : column + block.shape[1]] = block[...].astype(F32)
+        column += refs[part].shape[1]
+
+
+def final_kernel(total, here, out, *, scale):
+    out[...] = ((total[0] + here[0].astype(F32)) * scale).T.astype(BF16)
+
+
+def after(value, *others):
+    return lax.optimization_barrier((value, *others))[0]
 
 
 def partners(core0, core1, seq_count, dp_count):
@@ -246,14 +249,16 @@
 
     s, d = lax.axis_index("seq"), lax.axis_index("dp")
     core, upper = s & 1, s >> 1
-    lane = jnp.arange(20, dtype=jnp.int32)
-    bits = lane - 4
+    lane = jnp.arange(36, dtype=jnp.int32)
+    bits = (lane - 4) & 15
     b1, b2, b3, b4 = (bits >> 3) & 1, (bits >> 2) & 1, (bits >> 1) & 1, bits & 1
-    row_s = s ^ (2 * jnp.where(core == 0, b1, b2))
-    row_d = d ^ jnp.where(core == 0, b3, b1) ^ (2 * jnp.where(core == 0, b2, b3)) ^ (4 * b4)
-    place = row_d * seq_count + row_s
+    lower, first = core == 0, lane < 20
+    over_x = jnp.where(first, jnp.where(lower, b1, b2), b3)
+    over_y = jnp.where(first, jnp.where(lower, b3, b1), b2)
+    over_z = jnp.where(first, jnp.where(lower, b2, b3), b1)
+    spot = (d ^ over_y ^ (2 * over_z) ^ (4 * b4)) * seq_count + (s ^ (2 * over_x))
     meta = jnp.where(
-        lane == 0, core, jnp.where(lane == 1, upper, jnp.where(lane == 2, s, place))
+        lane == 0, core, jnp.where(lane == 1, upper, jnp.where(lane == 2, s, spot))
     ).astype(jnp.int32)
 
     send, mine = pl.pallas_call(
@@ -268,61 +273,85 @@
         compiler_params=params(4),
     )(meta, *map(stay, blocks))
     near = swap(send, across, across)
-    far = swap(send, (3, 0), (3, 0))
     other = swap(mine, sibling, sibling)
-    other_features = swap(features, sibling, sibling)
-
-    local, turned, states = pl.pallas_call(
+    other_x = swap(features, sibling, sibling)
+
+    local, turned, states, mine_x = pl.pallas_call(
         local_kernel,
-        in_specs=[vmem()] * 2,
-        out_specs=[vmem()] * 3,
+        in_specs=[hbm()] + [vmem()] * 2,
+        out_specs=[vmem()] * 4,
         out_shape=[
             jax.ShapeDtypeStruct((2, 3, width, tokens), F32),
             jax.ShapeDtypeStruct((2, 3, HEADS, HS, tokens), BF16),
             jax.ShapeDtypeStruct((2, 2, HEADS, HS, HS), BF16),
+            jax.ShapeDtypeStruct(features.shape, BF16),
         ],
+        scratch_shapes=[pltpu.SemaphoreType.DMA],
         compiler_params=params(16),
-    )(mine, other)
-    half = jax.ShapeDtypeStruct((8, 3 * width, BLOCK), BF16)
-    scratch = [pltpu.VMEM((tokens, 8 * BLOCK), BF16), pltpu.SemaphoreType.DMA((8,))]
-    grads, going = pl.pallas_call(
-        functools.partial(send_kernel, scale=scale),
-        in_specs=[smem()] + [vmem()] * 5 + [hbm(), vmem()],
+    )(stay(features), mine, other)
+    near = after(near, states)
+    far = swap(near, sibling, sibling)
+    halves = [
+        jax.ShapeDtypeStruct((8, count * width, BLOCK), BF16) for count in (2, 1)
+    ]
+    grads, going_a = pl.pallas_call(
+        functools.partial(send_a_kernel, scale=scale),
+        in_specs=[smem()] + [vmem()] * 7,
         out_specs=[vmem()] * 2,
-        out_shape=[jax.ShapeDtypeStruct((2, 3 * width, tokens), BF16), half],
-        scratch_shapes=scratch,
+        out_shape=[jax.ShapeDtypeStruct((3 * width, 2 * tokens), BF16), halves[0]],
         compiler_params=params(16),
-    )(meta, local, turned, states, near, far, stay(features), other_features)
-    here = swap(going, across, y)
-    kept, own = pl.pallas_call(
+    )(meta, local, turned, states, near, far, mine_x, other_x)
+    here_a = swap(going_a, across, y)
+    going_b = pl.pallas_call(
+        send_b_kernel,
+        in_specs=[smem()] + [vmem()] * 3,
+        out_specs=vmem(),
+        out_shape=halves[1],
+        compiler_params=params(16),
+    )(meta, grads, mine_x, other_x)
+    here = [here_a, swap(going_b, z1, z1)]
+    *kept, own = pl.pallas_call(
         keep_kernel,
-        in_specs=[smem(), vmem(), hbm(), vmem()],
-        out_specs=[vmem()] * 2,
-        out_shape=[half, jax.ShapeDtypeStruct((tokens, 3 * width), BF16)],
-        scratch_shapes=scratch,
+        in_specs=[smem()] + [vmem()] * 3,
+        out_specs=[vmem()] * 3,
+        out_shape=halves + [jax.ShapeDtypeStruct((tokens, 3 * width), BF16)],
         compiler_params=params(16),
-    )(meta, grads, stay(features), other_features)
-    for core0, core1 in ((z1, across), (y, z1), (z2, z2)):
+    )(meta, grads, mine_x, other_x)
+
+    def step(kept, here, way):
         count = kept.shape[0] // 2
         total = kept.astype(F32) + here.astype(F32)
-        kept = total[:count]
-        here = swap(total[count:].astype(BF16), core0, core1)
-    final = pl.pallas_call(
-        functools.partial(final_kernel, scale=weight_scale),
-        in_specs=[vmem()] * 2,
-        out_specs=vmem(),
-        out_shape=jax.ShapeDtypeStruct((BLOCK, 3 * width), BF16),
-        compiler_params=params(4),
-    )(kept, here)
-    facing = swap(final, across, across)
-    pair = swap(jnp.stack([final, facing]), sibling, sibling)
+        going = total[count:].astype(BF16)
+        return total[:count], going, swap(going, *way)
+
+    def finish(kept, here):
+        final = pl.pallas_call(
+            functools.partial(final_kernel, scale=weight_scale),
+            in_specs=[vmem()] * 2,
+            out_specs=vmem(),
+            out_shape=jax.ShapeDtypeStruct((BLOCK, kept.shape[1]), BF16),
+            compiler_params=params(4),
+        )(kept, here)
+        facing = swap(final, across, across)
+        return final, facing, swap(final, sibling, sibling), swap(facing, sibling, sibling)
+
+    kept_a, kept_b = kept
+    here_a, here_b = here
+    kept_a, going_a, here_a = step(kept_a, after(here_a, going_b, kept_a), (z1, across))
+    kept_b, going_b, here_b = step(kept_b, after(here_b, going_a), (y, y))
+    kept_b, going_b, here_b = step(kept_b, here_b, (across, across))
+    kept_a, going_a, here_a = step(kept_a, after(here_a, going_b), (y, z1))
+    kept_b, going_b, here_b = step(kept_b, after(here_b, going_a), (z2, z2))
+    kept_a, going_a, here_a = step(kept_a, after(here_a, going_b), (z2, z2))
+    part_b = finish(kept_b, after(here_b, going_a))
+    part_a = finish(kept_a, after(here_a, part_b[1]))
     weight_grad = pl.pallas_call(
         place_kernel,
-        in_specs=[smem()] + [vmem()] * 3,
+        in_specs=[smem()] + [vmem()] * 8,
         out_specs=vmem(),
         out_shape=jax.ShapeDtypeStruct((seq_count * rows, 3 * width), F32),
         compiler_params=params(8),
-    )(meta, final, facing, pair)
+    )(meta, *part_a, *part_b)
     return (own[None], weight_grad)
 
 

time: 73.4 us -> 62.8 us (0.86)
  waiting for transfers between devices: 47.1 us -> 25 us
  starting transfers between devices: 13.5 us -> 25.6 us
    ppermute x10 -> x18, waiting for transfers between devices: 47.1 us -> 25 us  [on_device(): lax.ppermute(value, AXES, partners(core0, core1, seq_count, dp_count))]
    ppermute x10 -> x18, starting transfers between devices: 13.5 us -> 25.6 us  [on_device(): lax.ppermute(value, AXES, partners(core0, core1, seq_count, dp_count))]
    pallas_call x5 -> x7, Pallas kernels: 9.05 us -> 8.63 us  [the longest x1 2.38 us: on_device(): pl.pallas_call(keep_kernel, in_specs=[smem()] + [vmem()] * 3, out_specs=[...]
  transfers between devices with their start and end apart: 10 -> 18, of which waited for: 8 -> 10; matrix products, arithmetic and copies ran while one was open for 0% -> 1% of each run, Pallas kernels for 8% -> 11%
where the time goes in v5:
time: 62.8 us; the launch traced here: 62.6 us
  starting transfers between devices  25.6 us (41%)
  waiting for transfers between devices  25 us (40%)
  Pallas kernels  10.5 us (17%)
  between operations  0.77 us (1%)
    ppermute x18, starting transfers between devices, on_device(): lax.ppermute(value, AXES, partners(core0, core1, seq_count, dp_count))  25.6 us
    ppermute x18, waiting for transfers between devices, on_device(): lax.ppermute(value, AXES, partners(core0, core1, seq_count, dp_count))  25 us
    pallas_call x1, Pallas kernels, on_device(): pl.pallas_call(keep_kernel, in_specs=[smem()] + [vmem()] * 3, out_specs=[...  2.38 us
    pallas_call x1, Pallas kernels, on_device(): pl.pallas_call(state_kernel, in_specs=[smem()] + [hbm()] * 4, out_specs=[...  1.91 us
    pallas_call x1, Pallas kernels, on_device(): pl.pallas_call(place_kernel, in_specs=[smem()] + [vmem()] * 8, out_specs=...  1.79 us
    pallas_call x1, Pallas kernels, on_device(): pl.pallas_call(local_kernel, in_specs=[hbm()] + [vmem()] * 2, out_specs=[...  1.6 us
    pallas_call x1, Pallas kernels, on_device(): pl.pallas_call(functools.partial(send_a_kernel, scale=scale), in_specs=[s...  1.56 us
  transfers between devices with their start and end apart: 18, of which 10 were waited for; matrix products, arithmetic and copies ran while one was open for 1% of the time, Pallas kernels for 11%

profile of v5, /device:TPU:0, one launch (start us, length us, event | category | flops | bytes accessed | tf_op | source)
XLA Modules:
  0.0 62.6 jit_solution(9607336731197882560)
XLA Ops:
  0.6 0.5 collective-permute-start.3
  1.2 1.9 %shard_map.68 = (bf16[2,128,128]{2,1,0:T(8,128)(2,1)S(1)}, bf16[4,256,256]{2,1,0:T(8,128)(2,1)S(1)}) custom-call(s32[36]{0:T(128)S(1)} %compare_select_fusion.2.meta, bf16[256,256]{1,0:T(8,128)(2,1)} %bitcast.8, bf16[256,256]{1,0:T(8,128)(2,1)} %bitcast.9, bf16[256,256]{1,0:T(8,128)(2,1)} %bitcast.10, bf16[256,256]{1,0:T(8,128)(2,1)} %bitcast.11), custom_call_target="tpu_custom_call" | custom-call | tf_op jit(solution)/shard_map/pallas_call | solution.py:264
  3.1 0.1 collective-permute-start
  3.2 2.9 %collective-permute-start.1 = (bf16[2,128,128]{2,1,0:T(8,128)(2,1)S(1)}, bf16[2,128,128]{2,1,0:T(8,128)(2,1)S(1)}, u32[]{:S(2)}, u32[]{:S(2)}) collective-permute-start(bf16[2,128,128]{2,1,0:T(8,128)(2,1)S(1)} %get-tuple-element.25), channel_id=1, source_target_pairs={{0,16},{1,17},{2,18},{3,19},{4,20},{5,21},{6,22},{7,23},{8,24},{9,... | collective-permute-start | bytes 196616 | tf_op jit(solution)/shard_map/ppermute | solution.py:245
  6.1 0.0 collective-permute-done.other
  6.1 1.6 %shard_map.69 = (f32[2,3,256,256]{3,2,1,0:T(8,128)S(1)}, bf16[2,3,2,128,256]{4,3,2,1,0:T(8,128)(2,1)S(1)}, bf16[2,2,2,128,128]{4,3,2,1,0:T(8,128)(2,1)S(1)}, bf16[256,4096]{1,0:T(8,128)(2,1)S(1)}) custom-call(bf16[256,4096]{1,0:T(8,128)(2,1)} %bitcast.7, bf16[4,256,256]{2,1,0:T(8,128)(2,1)S(1)} %get-tuple-element.21.mine, ...), custom_call_target="tpu_custom_call" | custom-call | tf_op jit(solution)/shard_map/pallas_call | solution.py:279
  7.7 0.7 %collective-permute-done.1.near = bf16[2,128,128]{2,1,0:T(8,128)(2,1)S(1)} collective-permute-done((bf16[2,128,128]{2,1,0:T(8,128)(2,1)S(1)}, bf16[2,128,128]{2,1,0:T(8,128)(2,1)S(1)}, u32[]{:S(2)}, u32[]{:S(2)}) %collective-permute-start.1) | collective-permute-done | bytes 65568 | tf_op jit(solution)/shard_map/ppermute | solution.py:245
  8.5 0.0 collective-permute-start.2
  8.5 1.3 %collective-permute-done.2.far = bf16[2,128,128]{2,1,0:T(8,128)(2,1)S(1)} collective-permute-done((bf16[2,128,128]{2,1,0:T(8,128)(2,1)S(1)}, bf16[2,128,128]{2,1,0:T(8,128)(2,1)S(1)}, u32[]{:S(2)}, u32[]{:S(2)}) %collective-permute-start.2) | collective-permute-done | bytes 65568 | tf_op jit(solution)/shard_map/ppermute | solution.py:245
  9.7 0.0 collective-permute-done.3.x1
  9.7 1.6 %shard_map.70 = (bf16[768,512]{1,0:T(8,128)(2,1)S(1)}, bf16[8,512,128]{2,1,0:T(8,128)(2,1)S(1)}) custom-call(s32[36]{0:T(128)S(1)} %compare_select_fusion.2.meta, f32[2,3,256,256]{3,2,1,0:T(8,128)S(1)} %get-tuple-element.22.local, bf16[2,3,2,128,256]{4,3,2,1,0:T(8,128)(2,1)S(1)} %get-tuple-element.23.turned, ...), custom_call_target="tpu_custom_call" | custom-call | tf_op jit(solution)/shard_map/pallas_call | solution.py:297
  11.3 2.0 %collective-permute-start.4 = (bf16[8,512,128]{2,1,0:T(8,128)(2,1)S(1)}, bf16[8,512,128]{2,1,0:T(8,128)(2,1)S(1)}, u32[]{:S(2)}, u32[]{:S(2)}) collective-permute-start(bf16[8,512,128]{2,1,0:T(8,128)(2,1)S(1)} %get-tuple-element.31), channel_id=1, source_target_pairs={{0,16},{1,17},{2,18},{3,19},{4,20},{5,21},{6,22},{7,23},{8,9},{9,8... | collective-permute-start | bytes 3145736 | tf_op jit(solution)/shard_map/ppermute | solution.py:245
  13.3 1.1 %shard_map.72 = bf16[8,256,128]{2,1,0:T(8,128)(2,1)S(1)} custom-call(s32[36]{0:T(128)S(1)} %compare_select_fusion.2.meta, bf16[768,512]{1,0:T(8,128)(2,1)S(1)} %get-tuple-element.28.grads, bf16[256,4096]{1,0:T(8,128)(2,1)S(1)} %get-tuple-element.27.x0, bf16[256,4096]{1,0:T(8,128)(2,1)S(1)} %collective-permute-done.3.x1), custom_call_target="tpu_custom_call" | custom-call | tf_op jit(solution)/shard_map/pallas_call | solution.py:305
  14.4 1.7 %collective-permute-start.6 = (bf16[8,256,128]{2,1,0:T(8,128)(2,1)S(1)}, bf16[8,256,128]{2,1,0:T(8,128)(2,1)S(1)}, u32[]{:S(2)}, u32[]{:S(2)}) collective-permute-start(bf16[8,256,128]{2,1,0:T(8,128)(2,1)S(1)} %shard_map.72), channel_id=1, source_target_pairs={{0,2},{1,3},{2,0},{3,1},{4,6},{5,7},{6,4},{7,5},{8,10},{9,11},{10,... | collective-permute-start | bytes 1572872 | tf_op jit(solution)/shard_map/ppermute | solution.py:245
  16.0 2.4 %shard_map.71 = (bf16[8,512,128]{2,1,0:T(8,128)(2,1)S(1)}, bf16[8,256,128]{2,1,0:T(8,128)(2,1)S(1)}, bf16[256,768]{1,0:T(8,128)(2,1)}) custom-call(s32[36]{0:T(128)S(1)} %compare_select_fusion.2.meta, bf16[768,512]{1,0:T(8,128)(2,1)S(1)} %get-tuple-element.28.grads, bf16[256,4096]{1,0:T(8,128)(2,1)S(1)} %get-tuple-element.27.x0, ...), custom_call_target="tpu_custom_call" | custom-call | tf_op jit(solution)/shard_map/pallas_call | solution.py:313
  18.4 7.8 %collective-permute-done.4 = bf16[8,512,128]{2,1,0:T(8,128)(2,1)S(1)} collective-permute-done((bf16[8,512,128]{2,1,0:T(8,128)(2,1)S(1)}, bf16[8,512,128]{2,1,0:T(8,128)(2,1)S(1)}, u32[]{:S(2)}, u32[]{:S(2)}) %collective-permute-start.4) | collective-permute-done | bytes 1048608 | tf_op jit(solution)/shard_map/ppermute | solution.py:245
  26.2 0.2 convert_add_fusion
  26.4 0.1 slice.76
  26.4 2.1 %collective-permute-start.5 = (bf16[4,512,128]{2,1,0:T(8,128)(2,1)S(1)}, bf16[4,512,128]{2,1,0:T(8,128)(2,1)S(1)}, u32[]{:S(2)}, u32[]{:S(2)}) collective-permute-start(bf16[4,512,128]{2,1,0:T(8,128)(2,1)S(1)} %slice.76), channel_id=1, source_target_pairs={{0,2},{1,3},{2,0},{3,1},{4,6},{5,7},{6,4},{7,5},{8,24},{9,25},{10,... | collective-permute-start | bytes 1572872 | tf_op jit(solution)/shard_map/ppermute | solution.py:245
  28.5 0.0 collective-permute-done.6
  28.5 0.1 convert_add_fusion.1
  28.7 1.6 %collective-permute-start.7 = (bf16[4,256,128]{2,1,0:T(8,128)(2,1)S(1)}, bf16[4,256,128]{2,1,0:T(8,128)(2,1)S(1)}, u32[]{:S(2)}, u32[]{:S(2)}) collective-permute-start(bf16[4,256,128]{2,1,0:T(8,128)(2,1)S(1)} %slice.78), channel_id=1, source_target_pairs={{0,1},{1,0},{2,3},{3,2},{4,5},{5,4},{6,7},{7,6},{8,9},{9,8},{10,11... | collective-permute-start | bytes 786440 | tf_op jit(solution)/shard_map/ppermute | solution.py:245
  30.3 5.6 %collective-permute-done.7 = bf16[4,256,128]{2,1,0:T(8,128)(2,1)S(1)} collective-permute-done((bf16[4,256,128]{2,1,0:T(8,128)(2,1)S(1)}, bf16[4,256,128]{2,1,0:T(8,128)(2,1)S(1)}, u32[]{:S(2)}, u32[]{:S(2)}) %collective-permute-start.7) | collective-permute-done | bytes 262176 | tf_op jit(solution)/shard_map/ppermute | solution.py:245
  36.0 1.8 %collective-permute-start.9 = (bf16[2,256,128]{2,1,0:T(8,128)(2,1)S(1)}, bf16[2,256,128]{2,1,0:T(8,128)(2,1)S(1)}, u32[]{:S(2)}, u32[]{:S(2)}) collective-permute-start(bf16[2,256,128]{2,1,0:T(8,128)(2,1)S(1)} %slice.80), channel_id=1, source_target_pairs={{0,16},{1,17},{2,18},{3,19},{4,20},{5,21},{6,22},{7,23},{8,24},{9,... | collective-permute-start | bytes 393224 | tf_op jit(solution)/shard_map/ppermute | solution.py:245
  37.8 0.0 collective-permute-done.5
  37.8 0.1 slice_add_fusion
  37.9 0.6 collective-permute-start.8
  38.5 2.5 %collective-permute-done.9 = bf16[2,256,128]{2,1,0:T(8,128)(2,1)S(1)} collective-permute-done((bf16[2,256,128]{2,1,0:T(8,128)(2,1)S(1)}, bf16[2,256,128]{2,1,0:T(8,128)(2,1)S(1)}, u32[]{:S(2)}, u32[]{:S(2)}) %collective-permute-start.9) | collective-permute-done | bytes 131104 | tf_op jit(solution)/shard_map/ppermute | solution.py:245
  41.1 2.8 %collective-permute-start.11 = (bf16[1,256,128]{2,1,0:T(8,128)(2,1)S(1)}, bf16[1,256,128]{2,1,0:T(8,128)(2,1)S(1)}, u32[]{:S(2)}, u32[]{:S(2)}) collective-permute-start(bf16[1,256,128]{2,1,0:T(8,128)(2,1)S(1)} %slice.81), channel_id=1, source_target_pairs={{0,4},{1,5},{2,6},{3,7},{4,0},{5,1},{6,2},{7,3},{8,12},{9,13},{10,... | collective-permute-start | bytes 196616 | tf_op jit(solution)/shard_map/ppermute | solution.py:245
  43.9 0.5 collective-permute-done.8
  44.4 0.1 slice_add_fusion.1
  44.5 3.1 %collective-permute-start.10 = (bf16[1,512,128]{2,1,0:T(8,128)(2,1)S(1)}, bf16[1,512,128]{2,1,0:T(8,128)(2,1)S(1)}, u32[]{:S(2)}, u32[]{:S(2)}) collective-permute-start(bf16[1,512,128]{2,1,0:T(8,128)(2,1)S(1)} %slice.79), channel_id=1, source_target_pairs={{0,4},{1,5},{2,6},{3,7},{4,0},{5,1},{6,2},{7,3},{8,12},{9,13},{10,... | collective-permute-start | bytes 393224 | tf_op jit(solution)/shard_map/ppermute | solution.py:245
  47.6 0.0 collective-permute-done.11.here
  47.6 0.1 shard_map.73.refs_4_
  47.7 3.4 %collective-permute-start.12 = (bf16[128,256]{1,0:T(8,128)(2,1)S(1)}, bf16[128,256]{1,0:T(8,128)(2,1)S(1)}, u32[]{:S(2)}, u32[]{:S(2)}) collective-permute-start(bf16[128,256]{1,0:T(8,128)(2,1)S(1)} %shard_map.73.refs_4_), channel_id=1, source_target_pairs={{0,16},{1,17},{2,18},{3,19},{4,20},{5,21},{6,22},{7,23},{8,24},{9,... | collective-permute-start | bytes 196616 | tf_op jit(solution)/shard_map/ppermute | solution.py:245
  51.1 2.4 %collective-permute-done.12.refs_5_ = bf16[128,256]{1,0:T(8,128)(2,1)S(1)} collective-permute-done((bf16[128,256]{1,0:T(8,128)(2,1)S(1)}, bf16[128,256]{1,0:T(8,128)(2,1)S(1)}, u32[]{:S(2)}, u32[]{:S(2)}) %collective-permute-start.12) | collective-permute-done | bytes 65568 | tf_op jit(solution)/shard_map/ppermute | solution.py:245
  53.5 0.0 collective-permute-done.10.here
  53.5 0.1 shard_map.74.refs_0_
  53.6 2.5 %collective-permute-start.13 = (bf16[128,512]{1,0:T(8,128)(2,1)S(1)}, bf16[128,512]{1,0:T(8,128)(2,1)S(1)}, u32[]{:S(2)}, u32[]{:S(2)}) collective-permute-start(bf16[128,512]{1,0:T(8,128)(2,1)S(1)} %shard_map.74.refs_0_), channel_id=1, source_target_pairs={{0,16},{1,17},{2,18},{3,19},{4,20},{5,21},{6,22},{7,23},{8,24},{9,... | collective-permute-start | bytes 393224 | tf_op jit(solution)/shard_map/ppermute | solution.py:245
  56.1 0.0 collective-permute-start.14
  56.1 2.9 %collective-permute-done.13.refs_1_ = bf16[128,512]{1,0:T(8,128)(2,1)S(1)} collective-permute-done((bf16[128,512]{1,0:T(8,128)(2,1)S(1)}, bf16[128,512]{1,0:T(8,128)(2,1)S(1)}, u32[]{:S(2)}, u32[]{:S(2)}) %collective-permute-start.13) | collective-permute-done | bytes 131104 | tf_op jit(solution)/shard_map/ppermute | solution.py:245
  59.1 0.0 collective-permute-start.15
  59.1 0.5 collective-permute-start.16
  59.6 0.0 collective-permute-start.17
  59.6 0.9 %collective-permute-done.16.refs_6_ = bf16[128,256]{1,0:T(8,128)(2,1)S(1)} collective-permute-done((bf16[128,256]{1,0:T(8,128)(2,1)S(1)}, bf16[128,256]{1,0:T(8,128)(2,1)S(1)}, u32[]{:S(2)}, u32[]{:S(2)}) %collective-permute-start.16) | collective-permute-done | bytes 65568 | tf_op jit(solution)/shard_map/ppermute | solution.py:245
  60.5 0.3 collective-permute-done.17.refs_7_
  60.8 0.0 collective-permute-done.14.refs_2_
  60.9 0.0 collective-permute-done.15.refs_3_
  60.9 1.8 %shard_map.75 = f32[512,768]{1,0:T(8,128)} custom-call(s32[36]{0:T(128)S(1)} %compare_select_fusion.2.meta, bf16[128,512]{1,0:T(8,128)(2,1)S(1)} %shard_map.74.refs_0_, bf16[128,512]{1,0:T(8,128)(2,1)S(1)} %collective-permute-done.13.refs_1_, bf16[128,512]{1,0:T(8,128)(2,1)S(1)} %collective-permute-done.14.refs_2_, ...), custom_call_target="tpu_custom_call" | custom-call | tf_op jit(solution)/shard_map/pallas_call | solution.py:348
  (10 shorter events, 0.2 us)
Async XLA Ops:
  0.6 9.1 %collective-permute-start.3 = (bf16[256,4096]{1,0:T(8,128)(2,1)}, bf16[256,4096]{1,0:T(8,128)(2,1)S(1)}, u32[]{:S(2)}, u32[]{:S(2)}) collective-permute-start(bf16[256,4096]{1,0:T(8,128)(2,1)} %bitcast.6), channel_id=1, source_target_pairs={{0,8},{1,9},{2,10},{3,11},{4,12},{5,13},{6,14},{7,15},{8,0},{9,1},... | collective-permute-start | bytes 6291464 | tf_op jit(solution)/shard_map/ppermute | solution.py:245
  3.1 3.1 %collective-permute-start = (bf16[4,256,256]{2,1,0:T(8,128)(2,1)S(1)}, bf16[4,256,256]{2,1,0:T(8,128)(2,1)S(1)}, u32[]{:S(2)}, u32[]{:S(2)}) collective-permute-start(bf16[4,256,256]{2,1,0:T(8,128)(2,1)S(1)} %get-tuple-element.21.mine), channel_id=1, source_target_pairs={{0,8},{1,9},{2,10},{3,11},{4,12},{5,13},{6,14},{7,15},{8,0},{9,1},... | collective-permute-start | bytes 1572872 | tf_op jit(solution)/shard_map/ppermute | solution.py:245
  3.2 5.3 %collective-permute-start.1 = (bf16[2,128,128]{2,1,0:T(8,128)(2,1)S(1)}, bf16[2,128,128]{2,1,0:T(8,128)(2,1)S(1)}, u32[]{:S(2)}, u32[]{:S(2)}) collective-permute-start(bf16[2,128,128]{2,1,0:T(8,128)(2,1)S(1)} %get-tuple-element.25), channel_id=1, source_target_pairs={{0,16},{1,17},{2,18},{3,19},{4,20},{5,21},{6,22},{7,23},{8,24},{9,... | collective-permute-start | bytes 196616 | tf_op jit(solution)/shard_map/ppermute | solution.py:245
  8.5 1.3 %collective-permute-start.2 = (bf16[2,128,128]{2,1,0:T(8,128)(2,1)S(1)}, bf16[2,128,128]{2,1,0:T(8,128)(2,1)S(1)}, u32[]{:S(2)}, u32[]{:S(2)}) collective-permute-start(bf16[2,128,128]{2,1,0:T(8,128)(2,1)S(1)} %collective-permute-done.1.near), channel_id=1, source_target_pairs={{0,8},{1,9},{2,10},{3,11},{4,12},{5,13},{6,14},{7,15},{8,0},{9,1},... | collective-permute-start | bytes 196616 | tf_op jit(solution)/shard_map/ppermute | solution.py:245
  11.3 14.9 %collective-permute-start.4 = (bf16[8,512,128]{2,1,0:T(8,128)(2,1)S(1)}, bf16[8,512,128]{2,1,0:T(8,128)(2,1)S(1)}, u32[]{:S(2)}, u32[]{:S(2)}) collective-permute-start(bf16[8,512,128]{2,1,0:T(8,128)(2,1)S(1)} %get-tuple-element.31), channel_id=1, source_target_pairs={{0,16},{1,17},{2,18},{3,19},{4,20},{5,21},{6,22},{7,23},{8,9},{9,8... | collective-permute-start | bytes 3145736 | tf_op jit(solution)/shard_map/ppermute | solution.py:245
  14.4 14.2 %collective-permute-start.6 = (bf16[8,256,128]{2,1,0:T(8,128)(2,1)S(1)}, bf16[8,256,128]{2,1,0:T(8,128)(2,1)S(1)}, u32[]{:S(2)}, u32[]{:S(2)}) collective-permute-start(bf16[8,256,128]{2,1,0:T(8,128)(2,1)S(1)} %shard_map.72), channel_id=1, source_target_pairs={{0,2},{1,3},{2,0},{3,1},{4,6},{5,7},{6,4},{7,5},{8,10},{9,11},{10,... | collective-permute-start | bytes 1572872 | tf_op jit(solution)/shard_map/ppermute | solution.py:245
  26.4 11.3 %collective-permute-start.5 = (bf16[4,512,128]{2,1,0:T(8,128)(2,1)S(1)}, bf16[4,512,128]{2,1,0:T(8,128)(2,1)S(1)}, u32[]{:S(2)}, u32[]{:S(2)}) collective-permute-start(bf16[4,512,128]{2,1,0:T(8,128)(2,1)S(1)} %slice.76), channel_id=1, source_target_pairs={{0,2},{1,3},{2,0},{3,1},{4,6},{5,7},{6,4},{7,5},{8,24},{9,25},{10,... | collective-permute-start | bytes 1572872 | tf_op jit(solution)/shard_map/ppermute | solution.py:245
  28.7 7.2 %collective-permute-start.7 = (bf16[4,256,128]{2,1,0:T(8,128)(2,1)S(1)}, bf16[4,256,128]{2,1,0:T(8,128)(2,1)S(1)}, u32[]{:S(2)}, u32[]{:S(2)}) collective-permute-start(bf16[4,256,128]{2,1,0:T(8,128)(2,1)S(1)} %slice.78), channel_id=1, source_target_pairs={{0,1},{1,0},{2,3},{3,2},{4,5},{5,4},{6,7},{7,6},{8,9},{9,8},{10,11... | collective-permute-start | bytes 786440 | tf_op jit(solution)/shard_map/ppermute | solution.py:245
  36.0 5.0 %collective-permute-start.9 = (bf16[2,256,128]{2,1,0:T(8,128)(2,1)S(1)}, bf16[2,256,128]{2,1,0:T(8,128)(2,1)S(1)}, u32[]{:S(2)}, u32[]{:S(2)}) collective-permute-start(bf16[2,256,128]{2,1,0:T(8,128)(2,1)S(1)} %slice.80), channel_id=1, source_target_pairs={{0,16},{1,17},{2,18},{3,19},{4,20},{5,21},{6,22},{7,23},{8,24},{9,... | collective-permute-start | bytes 393224 | tf_op jit(solution)/shard_map/ppermute | solution.py:245
  37.9 6.4 %collective-permute-start.8 = (bf16[2,512,128]{2,1,0:T(8,128)(2,1)S(1)}, bf16[2,512,128]{2,1,0:T(8,128)(2,1)S(1)}, u32[]{:S(2)}, u32[]{:S(2)}) collective-permute-start(bf16[2,512,128]{2,1,0:T(8,128)(2,1)S(1)} %slice.77), channel_id=1, source_target_pairs={{0,1},{1,0},{2,3},{3,2},{4,5},{5,4},{6,7},{7,6},{8,10},{9,11},{10,... | collective-permute-start | bytes 786440 | tf_op jit(solution)/shard_map/ppermute | solution.py:245
  41.1 6.5 %collective-permute-start.11 = (bf16[1,256,128]{2,1,0:T(8,128)(2,1)S(1)}, bf16[1,256,128]{2,1,0:T(8,128)(2,1)S(1)}, u32[]{:S(2)}, u32[]{:S(2)}) collective-permute-start(bf16[1,256,128]{2,1,0:T(8,128)(2,1)S(1)} %slice.81), channel_id=1, source_target_pairs={{0,4},{1,5},{2,6},{3,7},{4,0},{5,1},{6,2},{7,3},{8,12},{9,13},{10,... | collective-permute-start | bytes 196616 | tf_op jit(solution)/shard_map/ppermute | solution.py:245
  44.5 9.0 %collective-permute-start.10 = (bf16[1,512,128]{2,1,0:T(8,128)(2,1)S(1)}, bf16[1,512,128]{2,1,0:T(8,128)(2,1)S(1)}, u32[]{:S(2)}, u32[]{:S(2)}) collective-permute-start(bf16[1,512,128]{2,1,0:T(8,128)(2,1)S(1)} %slice.79), channel_id=1, source_target_pairs={{0,4},{1,5},{2,6},{3,7},{4,0},{5,1},{6,2},{7,3},{8,12},{9,13},{10,... | collective-permute-start | bytes 393224 | tf_op jit(solution)/shard_map/ppermute | solution.py:245
  47.7 5.8 %collective-permute-start.12 = (bf16[128,256]{1,0:T(8,128)(2,1)S(1)}, bf16[128,256]{1,0:T(8,128)(2,1)S(1)}, u32[]{:S(2)}, u32[]{:S(2)}) collective-permute-start(bf16[128,256]{1,0:T(8,128)(2,1)S(1)} %shard_map.73.refs_4_), channel_id=1, source_target_pairs={{0,16},{1,17},{2,18},{3,19},{4,20},{5,21},{6,22},{7,23},{8,24},{9,... | collective-permute-start | bytes 196616 | tf_op jit(solution)/shard_map/ppermute | solution.py:245
  53.6 5.5 %collective-permute-start.13 = (bf16[128,512]{1,0:T(8,128)(2,1)S(1)}, bf16[128,512]{1,0:T(8,128)(2,1)S(1)}, u32[]{:S(2)}, u32[]{:S(2)}) collective-permute-start(bf16[128,512]{1,0:T(8,128)(2,1)S(1)} %shard_map.74.refs_0_), channel_id=1, source_target_pairs={{0,16},{1,17},{2,18},{3,19},{4,20},{5,21},{6,22},{7,23},{8,24},{9,... | collective-permute-start | bytes 393224 | tf_op jit(solution)/shard_map/ppermute | solution.py:245
  56.1 4.7 %collective-permute-start.14 = (bf16[128,512]{1,0:T(8,128)(2,1)S(1)}, bf16[128,512]{1,0:T(8,128)(2,1)S(1)}, u32[]{:S(2)}, u32[]{:S(2)}) collective-permute-start(bf16[128,512]{1,0:T(8,128)(2,1)S(1)} %shard_map.74.refs_0_), channel_id=1, source_target_pairs={{0,8},{1,9},{2,10},{3,11},{4,12},{5,13},{6,14},{7,15},{8,0},{9,1},... | collective-permute-start | bytes 393224 | tf_op jit(solution)/shard_map/ppermute | solution.py:245
  59.1 1.8 %collective-permute-start.15 = (bf16[128,512]{1,0:T(8,128)(2,1)S(1)}, bf16[128,512]{1,0:T(8,128)(2,1)S(1)}, u32[]{:S(2)}, u32[]{:S(2)}) collective-permute-start(bf16[128,512]{1,0:T(8,128)(2,1)S(1)} %collective-permute-done.13.refs_1_), channel_id=1, source_target_pairs={{0,8},{1,9},{2,10},{3,11},{4,12},{5,13},{6,14},{7,15},{8,0},{9,1},... | collective-permute-start | bytes 393224 | tf_op jit(solution)/shard_map/ppermute | solution.py:245
  59.1 1.4 %collective-permute-start.16 = (bf16[128,256]{1,0:T(8,128)(2,1)S(1)}, bf16[128,256]{1,0:T(8,128)(2,1)S(1)}, u32[]{:S(2)}, u32[]{:S(2)}) collective-permute-start(bf16[128,256]{1,0:T(8,128)(2,1)S(1)} %shard_map.73.refs_4_), channel_id=1, source_target_pairs={{0,8},{1,9},{2,10},{3,11},{4,12},{5,13},{6,14},{7,15},{8,0},{9,1},... | collective-permute-start | bytes 196616 | tf_op jit(solution)/shard_map/ppermute | solution.py:245
  59.6 1.3 %collective-permute-start.17 = (bf16[128,256]{1,0:T(8,128)(2,1)S(1)}, bf16[128,256]{1,0:T(8,128)(2,1)S(1)}, u32[]{:S(2)}, u32[]{:S(2)}) collective-permute-start(bf16[128,256]{1,0:T(8,128)(2,1)S(1)} %collective-permute-done.12.refs_5_), channel_id=1, source_target_pairs={{0,8},{1,9},{2,10},{3,11},{4,12},{5,13},{6,14},{7,15},{8,0},{9,1},... | collective-permute-start | bytes 196616 | tf_op jit(solution)/shard_map/ppermute | solution.py:245

commit v6 on v5

--- a/solution.py
+++ b/solution.py
@@ -165,7 +165,7 @@
         out[i + 1] = total[:, BLOCK:].astype(BF16)
 
 
-def send_a_kernel(meta, local, turned, states, near, far, x0, x1, grads, out, *, scale):
+def first_kernel(meta, local, turned, states, near, far, x0, x1, grads, out, *, scale):
     core = meta[0].astype(F32)
     upper = meta[1].astype(F32)
     width = HEADS * HS
@@ -187,17 +187,18 @@
                 total = (local[b, part, cols(h)] + extra[part]) * scale
                 rows = slice(part * width + h * HS, part * width + (h + 1) * HS)
                 grads[rows, b * tokens : (b + 1) * tokens] = total.astype(BF16)
-    weights(meta, 8, grads[: 2 * width], x0, x1, out)
-
-
-def send_b_kernel(meta, grads, x0, x1, out):
-    weights(meta, 24, grads[2 * HEADS * HS :], x0, x1, out)
-
-
-def keep_kernel(meta, grads, x0, x1, out_a, out_b, own):
+    weights(meta, 8, grads[:width], x0, x1, out)
+
+
+def other_kernel(meta, grads, x0, x1, out, *, part):
     width = HEADS * HS
-    weights(meta, 0, grads[: 2 * width], x0, x1, out_a)
-    weights(meta, 16, grads[2 * width :], x0, x1, out_b)
+    weights(meta, 16 * part + 8, grads[part * width : (part + 1) * width], x0, x1, out)
+
+
+def keep_kernel(meta, grads, x0, x1, out_0, out_1, out_2, own):
+    width = HEADS * HS
+    for part, out in enumerate((out_0, out_1, out_2)):
+        weights(meta, 16 * part, grads[part * width : (part + 1) * width], x0, x1, out)
     for i in range(0, grads.shape[0], HS):
         own[:, i : i + HS] = grads[i : i + HS, : own.shape[0]].T
 
@@ -205,7 +206,7 @@
 def place_kernel(meta, *refs):
     out = refs[-1]
     column = 0
-    for part in range(0, 8, 4):
+    for part in range(0, len(refs) - 1, 4):
         for turn, block in zip((0, 2, 1, 3), refs[part : part + 4]):
             rows = pl.ds(pl.multiple_of((meta[2] ^ turn) * BLOCK, BLOCK), BLOCK)
             out[rows, column : column + block.shape[1]] = block[...].astype(F32)
@@ -249,14 +250,21 @@
 
     s, d = lax.axis_index("seq"), lax.axis_index("dp")
     core, upper = s & 1, s >> 1
-    lane = jnp.arange(36, dtype=jnp.int32)
-    bits = (lane - 4) & 15
-    b1, b2, b3, b4 = (bits >> 3) & 1, (bits >> 2) & 1, (bits >> 1) & 1, bits & 1
-    lower, first = core == 0, lane < 20
-    over_x = jnp.where(first, jnp.where(lower, b1, b2), b3)
-    over_y = jnp.where(first, jnp.where(lower, b3, b1), b2)
-    over_z = jnp.where(first, jnp.where(lower, b2, b3), b1)
-    spot = (d ^ over_y ^ (2 * over_z) ^ (4 * b4)) * seq_count + (s ^ (2 * over_x))
+    orders = (
+        ((across, y), (y, across), (z1, z1), (z2, z2)),
+        ((across, y), (y, across), (z1, z1), (z2, z2)),
+        ((z1, z1), (across, y), (y, across), (z2, z2)),
+    )
+    lane = jnp.arange(4 + 16 * len(orders), dtype=jnp.int32)
+    bits = lane - 4
+    spot = jnp.zeros_like(lane)
+    for part, order in enumerate(orders):
+        for i, way in enumerate(order):
+            bit = (bits >> (3 - i)) & 1
+            jump = [ds | dd * seq_count for ds, dd in way]
+            flip = bit * jnp.where(core == 0, jump[0], jump[1])
+            spot = spot ^ jnp.where(bits >> 4 == part, flip, 0)
+    spot = spot ^ (d * seq_count + s)
     meta = jnp.where(
         lane == 0, core, jnp.where(lane == 1, upper, jnp.where(lane == 2, s, spot))
     ).astype(jnp.int32)
@@ -291,32 +299,31 @@
     )(stay(features), mine, other)
     near = after(near, states)
     far = swap(near, sibling, sibling)
-    halves = [
-        jax.ShapeDtypeStruct((8, count * width, BLOCK), BF16) for count in (2, 1)
-    ]
-    grads, going_a = pl.pallas_call(
-        functools.partial(send_a_kernel, scale=scale),
+    half = jax.ShapeDtypeStruct((8, width, BLOCK), BF16)
+    grads, going = pl.pallas_call(
+        functools.partial(first_kernel, scale=scale),
         in_specs=[smem()] + [vmem()] * 7,
         out_specs=[vmem()] * 2,
-        out_shape=[jax.ShapeDtypeStruct((3 * width, 2 * tokens), BF16), halves[0]],
+        out_shape=[jax.ShapeDtypeStruct((3 * width, 2 * tokens), BF16), half],
         compiler_params=params(16),
     )(meta, local, turned, states, near, far, mine_x, other_x)
-    here_a = swap(going_a, across, y)
-    going_b = pl.pallas_call(
-        send_b_kernel,
-        in_specs=[smem()] + [vmem()] * 3,
-        out_specs=vmem(),
-        out_shape=halves[1],
-        compiler_params=params(16),
-    )(meta, grads, mine_x, other_x)
-    here = [here_a, swap(going_b, z1, z1)]
+    here = [swap(going, *orders[0][0]), None, None]
+    for part in (2, 1):
+        going = pl.pallas_call(
+            functools.partial(other_kernel, part=part),
+            in_specs=[smem()] + [vmem()] * 3,
+            out_specs=vmem(),
+            out_shape=half,
+            compiler_params=params(16),
+        )(meta, after(grads, going), mine_x, other_x)
+        here[part] = swap(going, *orders[part][0])
     *kept, own = pl.pallas_call(
         keep_kernel,
         in_specs=[smem()] + [vmem()] * 3,
-        out_specs=[vmem()] * 3,
-        out_shape=halves + [jax.ShapeDtypeStruct((tokens, 3 * width), BF16)],
+        out_specs=[vmem()] * 4,
+        out_shape=[half] * 3 + [jax.ShapeDtypeStruct((tokens, 3 * width), BF16)],
         compiler_params=params(16),
-    )(meta, grads, mine_x, other_x)
+    )(meta, after(grads, going), mine_x, other_x)
 
     def step(kept, here, way):
         count = kept.shape[0] // 2
@@ -335,23 +342,22 @@
         facing = swap(final, across, across)
         return final, facing, swap(final, sibling, sibling), swap(facing, sibling, sibling)
 
-    kept_a, kept_b = kept
-    here_a, here_b = here
-    kept_a, going_a, here_a = step(kept_a, after(here_a, going_b, kept_a), (z1, across))
-    kept_b, going_b, here_b = step(kept_b, after(here_b, going_a), (y, y))
-    kept_b, going_b, here_b = step(kept_b, here_b, (across, across))
-    kept_a, going_a, here_a = step(kept_a, after(here_a, going_b), (y, z1))
-    kept_b, going_b, here_b = step(kept_b, after(here_b, going_a), (z2, z2))
-    kept_a, going_a, here_a = step(kept_a, after(here_a, going_b), (z2, z2))
-    part_b = finish(kept_b, after(here_b, going_a))
-    part_a = finish(kept_a, after(here_a, part_b[1]))
+    latest = kept[0]
+    for part, level in ((0, 1), (1, 1), (2, 1), (0, 2), (1, 2), (2, 2), (0, 3), (1, 3), (2, 3)):
+        kept[part], latest, here[part] = step(
+            kept[part], after(here[part], latest), orders[part][level]
+        )
+    parts = {}
+    parts[0] = finish(kept[0], after(here[0], latest))
+    parts[1] = finish(kept[1], after(here[1], parts[0][0]))
+    parts[2] = finish(kept[2], after(here[2], parts[1][0], parts[0][1]))
     weight_grad = pl.pallas_call(
         place_kernel,
-        in_specs=[smem()] + [vmem()] * 8,
+        in_specs=[smem()] + [vmem()] * 12,
         out_specs=vmem(),
         out_shape=jax.ShapeDtypeStruct((seq_count * rows, 3 * width), F32),
         compiler_params=params(8),
-    )(meta, *part_a, *part_b)
+    )(meta, *parts[0], *parts[1], *parts[2])
     return (own[None], weight_grad)
 
 

time: 62.8 us -> 58.5 us (0.932)
  waiting for transfers between devices: 25 us -> 15.3 us
  starting transfers between devices: 25.6 us -> 29.7 us
  Pallas kernels: 10.5 us -> 11.6 us
    ppermute x18 -> x25, waiting for transfers between devices: 25 us -> 15.3 us  [on_device(): lax.ppermute(value, AXES, partners(core0, core1, seq_count, dp_count))]
    ppermute x18 -> x25, starting transfers between devices: 25.6 us -> 29.7 us  [on_device(): lax.ppermute(value, AXES, partners(core0, core1, seq_count, dp_count))]
    pallas_call x3 -> x4, Pallas kernels: 4.44 us -> 5.33 us  [the longest x2 2.2 us: on_device(): pl.pallas_call(functools.partial(other_kernel, part=part), in_specs=[smem...]
  transfers between devices with their start and end apart: 18 -> 25, of which waited for: 10 -> 11; matrix products, arithmetic and copies ran while one was open for 1% -> 1% of each run, Pallas kernels for 11% -> 15%
where the time goes in v6:
time: 58.5 us; the launch traced here: 58.3 us
  starting transfers between devices  29.7 us (51%)
  waiting for transfers between devices  15.3 us (26%)
  Pallas kernels  11.6 us (20%)
  between operations  0.88 us (2%)
    ppermute x25, starting transfers between devices, on_device(): lax.ppermute(value, AXES, partners(core0, core1, seq_count, dp_count))  29.7 us
    ppermute x25, waiting for transfers between devices, on_device(): lax.ppermute(value, AXES, partners(core0, core1, seq_count, dp_count))  15.3 us
    pallas_call x1, Pallas kernels, on_device(): pl.pallas_call(keep_kernel, in_specs=[smem()] + [vmem()] * 3, out_specs=[...  2.47 us
    pallas_call x2, Pallas kernels, on_device(): pl.pallas_call(functools.partial(other_kernel, part=part), in_specs=[smem...  2.2 us
    pallas_call x1, Pallas kernels, on_device(): pl.pallas_call(state_kernel, in_specs=[smem()] + [hbm()] * 4, out_specs=[...  1.9 us
    pallas_call x1, Pallas kernels, on_device(): pl.pallas_call(place_kernel, in_specs=[smem()] + [vmem()] * 12, out_specs...  1.79 us
    pallas_call x1, Pallas kernels, on_device(): pl.pallas_call(local_kernel, in_specs=[hbm()] + [vmem()] * 2, out_specs=[...  1.6 us
    pallas_call x1, Pallas kernels, on_device(): pl.pallas_call(functools.partial(first_kernel, scale=scale), in_specs=[sm...  1.34 us
  transfers between devices with their start and end apart: 25, of which 11 were waited for; matrix products, arithmetic and copies ran while one was open for 1% of the time, Pallas kernels for 15%

profile of v6, /device:TPU:0, one launch (start us, length us, event | category | flops | bytes accessed | tf_op | source)
XLA Modules:
  0.0 58.3 jit_solution(792502102845945370)
XLA Ops:
  0.6 0.5 collective-permute-start.3
  1.2 1.9 %shard_map.68 = (bf16[2,128,128]{2,1,0:T(8,128)(2,1)S(1)}, bf16[4,256,256]{2,1,0:T(8,128)(2,1)S(1)}) custom-call(s32[52]{0:T(128)S(1)} %compare_select_fusion.2.meta, bf16[256,256]{1,0:T(8,128)(2,1)} %bitcast.8, bf16[256,256]{1,0:T(8,128)(2,1)} %bitcast.9, bf16[256,256]{1,0:T(8,128)(2,1)} %bitcast.10, bf16[256,256]{1,0:T(8,128)(2,1)} %bitcast.11), custom_call_target="tpu_custom_call" | custom-call | tf_op jit(solution)/shard_map/pallas_call | solution.py:272
  3.1 0.1 collective-permute-start
  3.2 2.9 %collective-permute-start.1 = (bf16[2,128,128]{2,1,0:T(8,128)(2,1)S(1)}, bf16[2,128,128]{2,1,0:T(8,128)(2,1)S(1)}, u32[]{:S(2)}, u32[]{:S(2)}) collective-permute-start(bf16[2,128,128]{2,1,0:T(8,128)(2,1)S(1)} %get-tuple-element.34), channel_id=1, source_target_pairs={{0,16},{1,17},{2,18},{3,19},{4,20},{5,21},{6,22},{7,23},{8,24},{9,... | collective-permute-start | bytes 196616 | tf_op jit(solution)/shard_map/ppermute | solution.py:246
  6.1 0.0 collective-permute-done.other
  6.1 1.6 %shard_map.69 = (f32[2,3,256,256]{3,2,1,0:T(8,128)S(1)}, bf16[2,3,2,128,256]{4,3,2,1,0:T(8,128)(2,1)S(1)}, bf16[2,2,2,128,128]{4,3,2,1,0:T(8,128)(2,1)S(1)}, bf16[256,4096]{1,0:T(8,128)(2,1)S(1)}) custom-call(bf16[256,4096]{1,0:T(8,128)(2,1)} %bitcast.7, bf16[4,256,256]{2,1,0:T(8,128)(2,1)S(1)} %get-tuple-element.30.mine, ...), custom_call_target="tpu_custom_call" | custom-call | tf_op jit(solution)/shard_map/pallas_call | solution.py:287
  7.8 0.7 %collective-permute-done.1.near = bf16[2,128,128]{2,1,0:T(8,128)(2,1)S(1)} collective-permute-done((bf16[2,128,128]{2,1,0:T(8,128)(2,1)S(1)}, bf16[2,128,128]{2,1,0:T(8,128)(2,1)S(1)}, u32[]{:S(2)}, u32[]{:S(2)}) %collective-permute-start.1) | collective-permute-done | bytes 65568 | tf_op jit(solution)/shard_map/ppermute | solution.py:246
  8.5 0.0 collective-permute-start.2
  8.5 1.3 %collective-permute-done.2.far = bf16[2,128,128]{2,1,0:T(8,128)(2,1)S(1)} collective-permute-done((bf16[2,128,128]{2,1,0:T(8,128)(2,1)S(1)}, bf16[2,128,128]{2,1,0:T(8,128)(2,1)S(1)}, u32[]{:S(2)}, u32[]{:S(2)}) %collective-permute-start.2) | collective-permute-done | bytes 65568 | tf_op jit(solution)/shard_map/ppermute | solution.py:246
  9.7 0.0 collective-permute-done.3.x1
  9.7 1.3 %shard_map.70 = (bf16[768,512]{1,0:T(8,128)(2,1)S(1)}, bf16[8,256,128]{2,1,0:T(8,128)(2,1)S(1)}) custom-call(s32[52]{0:T(128)S(1)} %compare_select_fusion.2.meta, f32[2,3,256,256]{3,2,1,0:T(8,128)S(1)} %get-tuple-element.31.local, bf16[2,3,2,128,256]{4,3,2,1,0:T(8,128)(2,1)S(1)} %get-tuple-element.32.turned, ...), custom_call_target="tpu_custom_call" | custom-call | tf_op jit(solution)/shard_map/pallas_call | solution.py:303
  11.1 2.0 %collective-permute-start.4 = (bf16[8,256,128]{2,1,0:T(8,128)(2,1)S(1)}, bf16[8,256,128]{2,1,0:T(8,128)(2,1)S(1)}, u32[]{:S(2)}, u32[]{:S(2)}) collective-permute-start(bf16[8,256,128]{2,1,0:T(8,128)(2,1)S(1)} %get-tuple-element.42), channel_id=1, source_target_pairs={{0,16},{1,17},{2,18},{3,19},{4,20},{5,21},{6,22},{7,23},{8,9},{9,8... | collective-permute-start | bytes 1572872 | tf_op jit(solution)/shard_map/ppermute | solution.py:246
  13.1 1.1 %shard_map.71 = bf16[8,256,128]{2,1,0:T(8,128)(2,1)S(1)} custom-call(s32[52]{0:T(128)S(1)} %compare_select_fusion.2.meta, bf16[768,512]{1,0:T(8,128)(2,1)S(1)} %get-tuple-element.39.grads, bf16[256,4096]{1,0:T(8,128)(2,1)S(1)} %get-tuple-element.36.x0, bf16[256,4096]{1,0:T(8,128)(2,1)S(1)} %collective-permute-done.3.x1), custom_call_target="tpu_custom_call" | custom-call | tf_op jit(solution)/shard_map/pallas_call | solution.py:312
  14.2 1.1 %shard_map.72 = bf16[8,256,128]{2,1,0:T(8,128)(2,1)S(1)} custom-call(s32[52]{0:T(128)S(1)} %compare_select_fusion.2.meta, bf16[768,512]{1,0:T(8,128)(2,1)S(1)} %get-tuple-element.39.grads, bf16[256,4096]{1,0:T(8,128)(2,1)S(1)} %get-tuple-element.36.x0, bf16[256,4096]{1,0:T(8,128)(2,1)S(1)} %collective-permute-done.3.x1), custom_call_target="tpu_custom_call" | custom-call | tf_op jit(solution)/shard_map/pallas_call | solution.py:312
  15.3 0.2 collective-permute-start.7
  15.5 2.0 %collective-permute-start.6 = (bf16[8,256,128]{2,1,0:T(8,128)(2,1)S(1)}, bf16[8,256,128]{2,1,0:T(8,128)(2,1)S(1)}, u32[]{:S(2)}, u32[]{:S(2)}) collective-permute-start(bf16[8,256,128]{2,1,0:T(8,128)(2,1)S(1)} %shard_map.71), channel_id=1, source_target_pairs={{0,2},{1,3},{2,0},{3,1},{4,6},{5,7},{6,4},{7,5},{8,10},{9,11},{10,... | collective-permute-start | bytes 1572872 | tf_op jit(solution)/shard_map/ppermute | solution.py:246
  17.5 2.5 %shard_map.73 = (bf16[8,256,128]{2,1,0:T(8,128)(2,1)S(1)}, bf16[8,256,128]{2,1,0:T(8,128)(2,1)S(1)}, bf16[8,256,128]{2,1,0:T(8,128)(2,1)S(1)}, bf16[256,768]{1,0:T(8,128)(2,1)}) custom-call(s32[52]{0:T(128)S(1)} %compare_select_fusion.2.meta, bf16[768,512]{1,0:T(8,128)(2,1)S(1)} %get-tuple-element.39.grads, bf16[256,4096]{1,0:T(8,128)(2,1)S(1)} %get-tuple-element.36.x0, ...), custom_call_target="tpu_custom_call" | custom-call | tf_op jit(solution)/shard_map/pallas_call | solution.py:320
  19.9 0.4 collective-permute-done.4
  20.3 0.1 convert_add_fusion.2
  20.5 2.0 %collective-permute-start.5 = (bf16[4,256,128]{2,1,0:T(8,128)(2,1)S(1)}, bf16[4,256,128]{2,1,0:T(8,128)(2,1)S(1)}, u32[]{:S(2)}, u32[]{:S(2)}) collective-permute-start(bf16[4,256,128]{2,1,0:T(8,128)(2,1)S(1)} %slice.116), channel_id=1, source_target_pairs={{0,1},{1,0},{2,3},{3,2},{4,5},{5,4},{6,7},{7,6},{8,24},{9,25},{10,... | collective-permute-start | bytes 786440 | tf_op jit(solution)/shard_map/ppermute | solution.py:246
  22.5 6.2 %collective-permute-done.7 = bf16[8,256,128]{2,1,0:T(8,128)(2,1)S(1)} collective-permute-done((bf16[8,256,128]{2,1,0:T(8,128)(2,1)S(1)}, bf16[8,256,128]{2,1,0:T(8,128)(2,1)S(1)}, u32[]{:S(2)}, u32[]{:S(2)}) %collective-permute-start.7) | collective-permute-done | bytes 524320 | tf_op jit(solution)/shard_map/ppermute | solution.py:246
  28.8 0.1 convert_add_fusion.1
  28.9 2.0 %collective-permute-start.10 = (bf16[4,256,128]{2,1,0:T(8,128)(2,1)S(1)}, bf16[4,256,128]{2,1,0:T(8,128)(2,1)S(1)}, u32[]{:S(2)}, u32[]{:S(2)}) collective-permute-start(bf16[4,256,128]{2,1,0:T(8,128)(2,1)S(1)} %slice.115), channel_id=1, source_target_pairs={{0,1},{1,0},{2,3},{3,2},{4,5},{5,4},{6,7},{7,6},{8,24},{9,25},{10,... | collective-permute-start | bytes 786440 | tf_op jit(solution)/shard_map/ppermute | solution.py:246
  31.0 0.0 collective-permute-done.6
  31.0 0.1 convert_add_fusion
  31.1 1.5 %collective-permute-start.9 = (bf16[4,256,128]{2,1,0:T(8,128)(2,1)S(1)}, bf16[4,256,128]{2,1,0:T(8,128)(2,1)S(1)}, u32[]{:S(2)}, u32[]{:S(2)}) collective-permute-start(bf16[4,256,128]{2,1,0:T(8,128)(2,1)S(1)} %slice.114), channel_id=1, source_target_pairs={{0,16},{1,17},{2,18},{3,19},{4,20},{5,21},{6,22},{7,23},{8,9},{9,8... | collective-permute-start | bytes 786440 | tf_op jit(solution)/shard_map/ppermute | solution.py:246
  32.7 0.0 collective-permute-done.5
  32.7 1.6 %collective-permute-start.8 = (bf16[2,256,128]{2,1,0:T(8,128)(2,1)S(1)}, bf16[2,256,128]{2,1,0:T(8,128)(2,1)S(1)}, u32[]{:S(2)}, u32[]{:S(2)}) collective-permute-start(bf16[2,256,128]{2,1,0:T(8,128)(2,1)S(1)} %slice.119), channel_id=1, source_target_pairs={{0,2},{1,3},{2,0},{3,1},{4,6},{5,7},{6,4},{7,5},{8,10},{9,11},{10,... | collective-permute-start | bytes 393224 | tf_op jit(solution)/shard_map/ppermute | solution.py:246
  34.4 2.2 %collective-permute-done.10 = bf16[4,256,128]{2,1,0:T(8,128)(2,1)S(1)} collective-permute-done((bf16[4,256,128]{2,1,0:T(8,128)(2,1)S(1)}, bf16[4,256,128]{2,1,0:T(8,128)(2,1)S(1)}, u32[]{:S(2)}, u32[]{:S(2)}) %collective-permute-start.10) | collective-permute-done | bytes 262176 | tf_op jit(solution)/shard_map/ppermute | solution.py:246
  36.6 0.1 slice_add_fusion
  36.7 1.6 %collective-permute-start.13 = (bf16[2,256,128]{2,1,0:T(8,128)(2,1)S(1)}, bf16[2,256,128]{2,1,0:T(8,128)(2,1)S(1)}, u32[]{:S(2)}, u32[]{:S(2)}) collective-permute-start(bf16[2,256,128]{2,1,0:T(8,128)(2,1)S(1)} %slice.118), channel_id=1, source_target_pairs={{0,2},{1,3},{2,0},{3,1},{4,6},{5,7},{6,4},{7,5},{8,10},{9,11},{10,... | collective-permute-start | bytes 393224 | tf_op jit(solution)/shard_map/ppermute | solution.py:246
  38.3 0.0 collective-permute-done.9
  38.3 0.1 slice_add_fusion.1
  38.4 1.6 %collective-permute-start.12 = (bf16[2,256,128]{2,1,0:T(8,128)(2,1)S(1)}, bf16[2,256,128]{2,1,0:T(8,128)(2,1)S(1)}, u32[]{:S(2)}, u32[]{:S(2)}) collective-permute-start(bf16[2,256,128]{2,1,0:T(8,128)(2,1)S(1)} %slice.117), channel_id=1, source_target_pairs={{0,1},{1,0},{2,3},{3,2},{4,5},{5,4},{6,7},{7,6},{8,24},{9,25},{10,... | collective-permute-start | bytes 393224 | tf_op jit(solution)/shard_map/ppermute | solution.py:246
  39.9 0.0 collective-permute-done.8
  40.0 2.6 %collective-permute-start.11 = (bf16[1,256,128]{2,1,0:T(8,128)(2,1)S(1)}, bf16[1,256,128]{2,1,0:T(8,128)(2,1)S(1)}, u32[]{:S(2)}, u32[]{:S(2)}) collective-permute-start(bf16[1,256,128]{2,1,0:T(8,128)(2,1)S(1)} %slice.122), channel_id=1, source_target_pairs={{0,4},{1,5},{2,6},{3,7},{4,0},{5,1},{6,2},{7,3},{8,12},{9,13},{10,... | collective-permute-start | bytes 196616 | tf_op jit(solution)/shard_map/ppermute | solution.py:246
  42.6 0.0 collective-permute-done.13
  42.7 2.8 %collective-permute-start.17 = (bf16[1,256,128]{2,1,0:T(8,128)(2,1)S(1)}, bf16[1,256,128]{2,1,0:T(8,128)(2,1)S(1)}, u32[]{:S(2)}, u32[]{:S(2)}) collective-permute-start(bf16[1,256,128]{2,1,0:T(8,128)(2,1)S(1)} %slice.121), channel_id=1, source_target_pairs={{0,4},{1,5},{2,6},{3,7},{4,0},{5,1},{6,2},{7,3},{8,12},{9,13},{10,... | collective-permute-start | bytes 196616 | tf_op jit(solution)/shard_map/ppermute | solution.py:246
  45.4 0.0 collective-permute-done.12
  45.5 0.6 %collective-permute-start.21 = (bf16[1,256,128]{2,1,0:T(8,128)(2,1)S(1)}, bf16[1,256,128]{2,1,0:T(8,128)(2,1)S(1)}, u32[]{:S(2)}, u32[]{:S(2)}) collective-permute-start(bf16[1,256,128]{2,1,0:T(8,128)(2,1)S(1)} %slice.120), channel_id=1, source_target_pairs={{0,4},{1,5},{2,6},{3,7},{4,0},{5,1},{6,2},{7,3},{8,12},{9,13},{10,... | collective-permute-start | bytes 196616 | tf_op jit(solution)/shard_map/ppermute | solution.py:246
  46.1 0.3 collective-permute-done.11.here
  46.4 0.1 shard_map.74.refs_0_
  46.5 1.6 %collective-permute-start.14 = (bf16[128,256]{1,0:T(8,128)(2,1)S(1)}, bf16[128,256]{1,0:T(8,128)(2,1)S(1)}, u32[]{:S(2)}, u32[]{:S(2)}) collective-permute-start(bf16[128,256]{1,0:T(8,128)(2,1)S(1)} %shard_map.74.refs_0_), channel_id=1, source_target_pairs={{0,16},{1,17},{2,18},{3,19},{4,20},{5,21},{6,22},{7,23},{8,24},{9,... | collective-permute-start | bytes 196616 | tf_op jit(solution)/shard_map/ppermute | solution.py:246
  48.1 0.0 collective-permute-done.17.here
  48.1 0.1 shard_map.75.refs_4_
  48.2 0.1 collective-permute-start.19
  48.3 1.3 %collective-permute-start.18 = (bf16[128,256]{1,0:T(8,128)(2,1)S(1)}, bf16[128,256]{1,0:T(8,128)(2,1)S(1)}, u32[]{:S(2)}, u32[]{:S(2)}) collective-permute-start(bf16[128,256]{1,0:T(8,128)(2,1)S(1)} %shard_map.75.refs_4_), channel_id=1, source_target_pairs={{0,16},{1,17},{2,18},{3,19},{4,20},{5,21},{6,22},{7,23},{8,24},{9,... | collective-permute-start | bytes 196616 | tf_op jit(solution)/shard_map/ppermute | solution.py:246
  49.6 1.2 %collective-permute-done.21.here = bf16[1,256,128]{2,1,0:T(8,128)(2,1)S(1)} collective-permute-done((bf16[1,256,128]{2,1,0:T(8,128)(2,1)S(1)}, bf16[1,256,128]{2,1,0:T(8,128)(2,1)S(1)}, u32[]{:S(2)}, u32[]{:S(2)}) %collective-permute-start.21) | collective-permute-done | bytes 65568 | tf_op jit(solution)/shard_map/ppermute | solution.py:246
  50.7 0.1 collective-permute-done.14.refs_1_
  50.8 0.1 shard_map.76.refs_8_
  50.9 1.6 %collective-permute-start.22 = (bf16[128,256]{1,0:T(8,128)(2,1)S(1)}, bf16[128,256]{1,0:T(8,128)(2,1)S(1)}, u32[]{:S(2)}, u32[]{:S(2)}) collective-permute-start(bf16[128,256]{1,0:T(8,128)(2,1)S(1)} %shard_map.76.refs_8_), channel_id=1, source_target_pairs={{0,16},{1,17},{2,18},{3,19},{4,20},{5,21},{6,22},{7,23},{8,24},{9,... | collective-permute-start | bytes 196616 | tf_op jit(solution)/shard_map/ppermute | solution.py:246
  52.5 0.0 collective-permute-start.15
  52.5 0.5 collective-permute-start.23
  53.0 0.2 collective-permute-done.18.refs_5_
  53.2 0.0 collective-permute-done.19.refs_6_
  53.2 0.5 collective-permute-start.16
  53.7 1.5 %collective-permute-done.22.refs_9_ = bf16[128,256]{1,0:T(8,128)(2,1)S(1)} collective-permute-done((bf16[128,256]{1,0:T(8,128)(2,1)S(1)}, bf16[128,256]{1,0:T(8,128)(2,1)S(1)}, u32[]{:S(2)}, u32[]{:S(2)}) %collective-permute-start.22) | collective-permute-done | bytes 65568 | tf_op jit(solution)/shard_map/ppermute | solution.py:246
  55.2 0.0 collective-permute-start.24
  55.2 0.0 collective-permute-done.15.refs_2_
  55.2 0.0 collective-permute-done.20.refs_7_
  55.3 0.0 collective-permute-done.23.refs_10_
  55.3 0.0 collective-permute-done.16.refs_3_
  55.3 1.2 %collective-permute-done.24.refs_11_ = bf16[128,256]{1,0:T(8,128)(2,1)S(1)} collective-permute-done((bf16[128,256]{1,0:T(8,128)(2,1)S(1)}, bf16[128,256]{1,0:T(8,128)(2,1)S(1)}, u32[]{:S(2)}, u32[]{:S(2)}) %collective-permute-start.24) | collective-permute-done | bytes 65568 | tf_op jit(solution)/shard_map/ppermute | solution.py:246
  56.5 1.8 %shard_map.77 = f32[512,768]{1,0:T(8,128)} custom-call(s32[52]{0:T(128)S(1)} %compare_select_fusion.2.meta, bf16[128,256]{1,0:T(8,128)(2,1)S(1)} %shard_map.74.refs_0_, bf16[128,256]{1,0:T(8,128)(2,1)S(1)} %collective-permute-done.14.refs_1_, bf16[128,256]{1,0:T(8,128)(2,1)S(1)} %collective-permute-done.15.refs_2_, ...), custom_call_target="tpu_custom_call" | custom-call | tf_op jit(solution)/shard_map/pallas_call | solution.py:354
  (18 shorter events, 0.4 us)
Async XLA Ops:
  0.6 9.1 %collective-permute-start.3 = (bf16[256,4096]{1,0:T(8,128)(2,1)}, bf16[256,4096]{1,0:T(8,128)(2,1)S(1)}, u32[]{:S(2)}, u32[]{:S(2)}) collective-permute-start(bf16[256,4096]{1,0:T(8,128)(2,1)} %bitcast.6), channel_id=1, source_target_pairs={{0,8},{1,9},{2,10},{3,11},{4,12},{5,13},{6,14},{7,15},{8,0},{9,1},... | collective-permute-start | bytes 6291464 | tf_op jit(solution)/shard_map/ppermute | solution.py:246
  3.1 3.1 %collective-permute-start = (bf16[4,256,256]{2,1,0:T(8,128)(2,1)S(1)}, bf16[4,256,256]{2,1,0:T(8,128)(2,1)S(1)}, u32[]{:S(2)}, u32[]{:S(2)}) collective-permute-start(bf16[4,256,256]{2,1,0:T(8,128)(2,1)S(1)} %get-tuple-element.30.mine), channel_id=1, source_target_pairs={{0,8},{1,9},{2,10},{3,11},{4,12},{5,13},{6,14},{7,15},{8,0},{9,1},... | collective-permute-start | bytes 1572872 | tf_op jit(solution)/shard_map/ppermute | solution.py:246
  3.2 5.3 %collective-permute-start.1 = (bf16[2,128,128]{2,1,0:T(8,128)(2,1)S(1)}, bf16[2,128,128]{2,1,0:T(8,128)(2,1)S(1)}, u32[]{:S(2)}, u32[]{:S(2)}) collective-permute-start(bf16[2,128,128]{2,1,0:T(8,128)(2,1)S(1)} %get-tuple-element.34), channel_id=1, source_target_pairs={{0,16},{1,17},{2,18},{3,19},{4,20},{5,21},{6,22},{7,23},{8,24},{9,... | collective-permute-start | bytes 196616 | tf_op jit(solution)/shard_map/ppermute | solution.py:246
  8.5 1.3 %collective-permute-start.2 = (bf16[2,128,128]{2,1,0:T(8,128)(2,1)S(1)}, bf16[2,128,128]{2,1,0:T(8,128)(2,1)S(1)}, u32[]{:S(2)}, u32[]{:S(2)}) collective-permute-start(bf16[2,128,128]{2,1,0:T(8,128)(2,1)S(1)} %collective-permute-done.1.near), channel_id=1, source_target_pairs={{0,8},{1,9},{2,10},{3,11},{4,12},{5,13},{6,14},{7,15},{8,0},{9,1},... | collective-permute-start | bytes 196616 | tf_op jit(solution)/shard_map/ppermute | solution.py:246
  11.1 9.2 %collective-permute-start.4 = (bf16[8,256,128]{2,1,0:T(8,128)(2,1)S(1)}, bf16[8,256,128]{2,1,0:T(8,128)(2,1)S(1)}, u32[]{:S(2)}, u32[]{:S(2)}) collective-permute-start(bf16[8,256,128]{2,1,0:T(8,128)(2,1)S(1)} %get-tuple-element.42), channel_id=1, source_target_pairs={{0,16},{1,17},{2,18},{3,19},{4,20},{5,21},{6,22},{7,23},{8,9},{9,8... | collective-permute-start | bytes 1572872 | tf_op jit(solution)/shard_map/ppermute | solution.py:246
  15.3 13.5 %collective-permute-start.7 = (bf16[8,256,128]{2,1,0:T(8,128)(2,1)S(1)}, bf16[8,256,128]{2,1,0:T(8,128)(2,1)S(1)}, u32[]{:S(2)}, u32[]{:S(2)}) collective-permute-start(bf16[8,256,128]{2,1,0:T(8,128)(2,1)S(1)} %shard_map.72), channel_id=1, source_target_pairs={{0,16},{1,17},{2,18},{3,19},{4,20},{5,21},{6,22},{7,23},{8,9},{9,8... | collective-permute-start | bytes 1572872 | tf_op jit(solution)/shard_map/ppermute | solution.py:246
  15.5 15.5 %collective-permute-start.6 = (bf16[8,256,128]{2,1,0:T(8,128)(2,1)S(1)}, bf16[8,256,128]{2,1,0:T(8,128)(2,1)S(1)}, u32[]{:S(2)}, u32[]{:S(2)}) collective-permute-start(bf16[8,256,128]{2,1,0:T(8,128)(2,1)S(1)} %shard_map.71), channel_id=1, source_target_pairs={{0,2},{1,3},{2,0},{3,1},{4,6},{5,7},{6,4},{7,5},{8,10},{9,11},{10,... | collective-permute-start | bytes 1572872 | tf_op jit(solution)/shard_map/ppermute | solution.py:246
  20.5 12.2 %collective-permute-start.5 = (bf16[4,256,128]{2,1,0:T(8,128)(2,1)S(1)}, bf16[4,256,128]{2,1,0:T(8,128)(2,1)S(1)}, u32[]{:S(2)}, u32[]{:S(2)}) collective-permute-start(bf16[4,256,128]{2,1,0:T(8,128)(2,1)S(1)} %slice.116), channel_id=1, source_target_pairs={{0,1},{1,0},{2,3},{3,2},{4,5},{5,4},{6,7},{7,6},{8,24},{9,25},{10,... | collective-permute-start | bytes 786440 | tf_op jit(solution)/shard_map/ppermute | solution.py:246
  28.9 7.7 %collective-permute-start.10 = (bf16[4,256,128]{2,1,0:T(8,128)(2,1)S(1)}, bf16[4,256,128]{2,1,0:T(8,128)(2,1)S(1)}, u32[]{:S(2)}, u32[]{:S(2)}) collective-permute-start(bf16[4,256,128]{2,1,0:T(8,128)(2,1)S(1)} %slice.115), channel_id=1, source_target_pairs={{0,1},{1,0},{2,3},{3,2},{4,5},{5,4},{6,7},{7,6},{8,24},{9,25},{10,... | collective-permute-start | bytes 786440 | tf_op jit(solution)/shard_map/ppermute | solution.py:246
  31.1 7.2 %collective-permute-start.9 = (bf16[4,256,128]{2,1,0:T(8,128)(2,1)S(1)}, bf16[4,256,128]{2,1,0:T(8,128)(2,1)S(1)}, u32[]{:S(2)}, u32[]{:S(2)}) collective-permute-start(bf16[4,256,128]{2,1,0:T(8,128)(2,1)S(1)} %slice.114), channel_id=1, source_target_pairs={{0,16},{1,17},{2,18},{3,19},{4,20},{5,21},{6,22},{7,23},{8,9},{9,8... | collective-permute-start | bytes 786440 | tf_op jit(solution)/shard_map/ppermute | solution.py:246
  32.7 7.2 %collective-permute-start.8 = (bf16[2,256,128]{2,1,0:T(8,128)(2,1)S(1)}, bf16[2,256,128]{2,1,0:T(8,128)(2,1)S(1)}, u32[]{:S(2)}, u32[]{:S(2)}) collective-permute-start(bf16[2,256,128]{2,1,0:T(8,128)(2,1)S(1)} %slice.119), channel_id=1, source_target_pairs={{0,2},{1,3},{2,0},{3,1},{4,6},{5,7},{6,4},{7,5},{8,10},{9,11},{10,... | collective-permute-start | bytes 393224 | tf_op jit(solution)/shard_map/ppermute | solution.py:246
  36.7 5.9 %collective-permute-start.13 = (bf16[2,256,128]{2,1,0:T(8,128)(2,1)S(1)}, bf16[2,256,128]{2,1,0:T(8,128)(2,1)S(1)}, u32[]{:S(2)}, u32[]{:S(2)}) collective-permute-start(bf16[2,256,128]{2,1,0:T(8,128)(2,1)S(1)} %slice.118), channel_id=1, source_target_pairs={{0,2},{1,3},{2,0},{3,1},{4,6},{5,7},{6,4},{7,5},{8,10},{9,11},{10,... | collective-permute-start | bytes 393224 | tf_op jit(solution)/shard_map/ppermute | solution.py:246
  38.4 7.1 %collective-permute-start.12 = (bf16[2,256,128]{2,1,0:T(8,128)(2,1)S(1)}, bf16[2,256,128]{2,1,0:T(8,128)(2,1)S(1)}, u32[]{:S(2)}, u32[]{:S(2)}) collective-permute-start(bf16[2,256,128]{2,1,0:T(8,128)(2,1)S(1)} %slice.117), channel_id=1, source_target_pairs={{0,1},{1,0},{2,3},{3,2},{4,5},{5,4},{6,7},{7,6},{8,24},{9,25},{10,... | collective-permute-start | bytes 393224 | tf_op jit(solution)/shard_map/ppermute | solution.py:246
  40.0 6.4 %collective-permute-start.11 = (bf16[1,256,128]{2,1,0:T(8,128)(2,1)S(1)}, bf16[1,256,128]{2,1,0:T(8,128)(2,1)S(1)}, u32[]{:S(2)}, u32[]{:S(2)}) collective-permute-start(bf16[1,256,128]{2,1,0:T(8,128)(2,1)S(1)} %slice.122), channel_id=1, source_target_pairs={{0,4},{1,5},{2,6},{3,7},{4,0},{5,1},{6,2},{7,3},{8,12},{9,13},{10,... | collective-permute-start | bytes 196616 | tf_op jit(solution)/shard_map/ppermute | solution.py:246
  42.7 5.4 %collective-permute-start.17 = (bf16[1,256,128]{2,1,0:T(8,128)(2,1)S(1)}, bf16[1,256,128]{2,1,0:T(8,128)(2,1)S(1)}, u32[]{:S(2)}, u32[]{:S(2)}) collective-permute-start(bf16[1,256,128]{2,1,0:T(8,128)(2,1)S(1)} %slice.121), channel_id=1, source_target_pairs={{0,4},{1,5},{2,6},{3,7},{4,0},{5,1},{6,2},{7,3},{8,12},{9,13},{10,... | collective-permute-start | bytes 196616 | tf_op jit(solution)/shard_map/ppermute | solution.py:246
  45.5 5.2 %collective-permute-start.21 = (bf16[1,256,128]{2,1,0:T(8,128)(2,1)S(1)}, bf16[1,256,128]{2,1,0:T(8,128)(2,1)S(1)}, u32[]{:S(2)}, u32[]{:S(2)}) collective-permute-start(bf16[1,256,128]{2,1,0:T(8,128)(2,1)S(1)} %slice.120), channel_id=1, source_target_pairs={{0,4},{1,5},{2,6},{3,7},{4,0},{5,1},{6,2},{7,3},{8,12},{9,13},{10,... | collective-permute-start | bytes 196616 | tf_op jit(solution)/shard_map/ppermute | solution.py:246
  46.5 4.3 %collective-permute-start.14 = (bf16[128,256]{1,0:T(8,128)(2,1)S(1)}, bf16[128,256]{1,0:T(8,128)(2,1)S(1)}, u32[]{:S(2)}, u32[]{:S(2)}) collective-permute-start(bf16[128,256]{1,0:T(8,128)(2,1)S(1)} %shard_map.74.refs_0_), channel_id=1, source_target_pairs={{0,16},{1,17},{2,18},{3,19},{4,20},{5,21},{6,22},{7,23},{8,24},{9,... | collective-permute-start | bytes 196616 | tf_op jit(solution)/shard_map/ppermute | solution.py:246
  48.2 5.0 %collective-permute-start.19 = (bf16[128,256]{1,0:T(8,128)(2,1)S(1)}, bf16[128,256]{1,0:T(8,128)(2,1)S(1)}, u32[]{:S(2)}, u32[]{:S(2)}) collective-permute-start(bf16[128,256]{1,0:T(8,128)(2,1)S(1)} %shard_map.75.refs_4_), channel_id=1, source_target_pairs={{0,8},{1,9},{2,10},{3,11},{4,12},{5,13},{6,14},{7,15},{8,0},{9,1},... | collective-permute-start | bytes 196616 | tf_op jit(solution)/shard_map/ppermute | solution.py:246
  48.3 4.9 %collective-permute-start.18 = (bf16[128,256]{1,0:T(8,128)(2,1)S(1)}, bf16[128,256]{1,0:T(8,128)(2,1)S(1)}, u32[]{:S(2)}, u32[]{:S(2)}) collective-permute-start(bf16[128,256]{1,0:T(8,128)(2,1)S(1)} %shard_map.75.refs_4_), channel_id=1, source_target_pairs={{0,16},{1,17},{2,18},{3,19},{4,20},{5,21},{6,22},{7,23},{8,24},{9,... | collective-permute-start | bytes 196616 | tf_op jit(solution)/shard_map/ppermute | solution.py:246
  50.9 4.3 %collective-permute-start.22 = (bf16[128,256]{1,0:T(8,128)(2,1)S(1)}, bf16[128,256]{1,0:T(8,128)(2,1)S(1)}, u32[]{:S(2)}, u32[]{:S(2)}) collective-permute-start(bf16[128,256]{1,0:T(8,128)(2,1)S(1)} %shard_map.76.refs_8_), channel_id=1, source_target_pairs={{0,16},{1,17},{2,18},{3,19},{4,20},{5,21},{6,22},{7,23},{8,24},{9,... | collective-permute-start | bytes 196616 | tf_op jit(solution)/shard_map/ppermute | solution.py:246
  52.5 2.7 %collective-permute-start.15 = (bf16[128,256]{1,0:T(8,128)(2,1)S(1)}, bf16[128,256]{1,0:T(8,128)(2,1)S(1)}, u32[]{:S(2)}, u32[]{:S(2)}) collective-permute-start(bf16[128,256]{1,0:T(8,128)(2,1)S(1)} %shard_map.74.refs_0_), channel_id=1, source_target_pairs={{0,8},{1,9},{2,10},{3,11},{4,12},{5,13},{6,14},{7,15},{8,0},{9,1},... | collective-permute-start | bytes 196616 | tf_op jit(solution)/shard_map/ppermute | solution.py:246
  52.5 2.7 %collective-permute-start.23 = (bf16[128,256]{1,0:T(8,128)(2,1)S(1)}, bf16[128,256]{1,0:T(8,128)(2,1)S(1)}, u32[]{:S(2)}, u32[]{:S(2)}) collective-permute-start(bf16[128,256]{1,0:T(8,128)(2,1)S(1)} %shard_map.76.refs_8_), channel_id=1, source_target_pairs={{0,8},{1,9},{2,10},{3,11},{4,12},{5,13},{6,14},{7,15},{8,0},{9,1},... | collective-permute-start | bytes 196616 | tf_op jit(solution)/shard_map/ppermute | solution.py:246
  53.2 2.1 %collective-permute-start.20 = (bf16[128,256]{1,0:T(8,128)(2,1)S(1)}, bf16[128,256]{1,0:T(8,128)(2,1)S(1)}, u32[]{:S(2)}, u32[]{:S(2)}) collective-permute-start(bf16[128,256]{1,0:T(8,128)(2,1)S(1)} %collective-permute-done.18.refs_5_), channel_id=1, source_target_pairs={{0,8},{1,9},{2,10},{3,11},{4,12},{5,13},{6,14},{7,15},{8,0},{9,1},... | collective-permute-start | bytes 196616 | tf_op jit(solution)/shard_map/ppermute | solution.py:246
  53.2 2.1 %collective-permute-start.16 = (bf16[128,256]{1,0:T(8,128)(2,1)S(1)}, bf16[128,256]{1,0:T(8,128)(2,1)S(1)}, u32[]{:S(2)}, u32[]{:S(2)}) collective-permute-start(bf16[128,256]{1,0:T(8,128)(2,1)S(1)} %collective-permute-done.14.refs_1_), channel_id=1, source_target_pairs={{0,8},{1,9},{2,10},{3,11},{4,12},{5,13},{6,14},{7,15},{8,0},{9,1},... | collective-permute-start | bytes 196616 | tf_op jit(solution)/shard_map/ppermute | solution.py:246
  55.2 1.3 %collective-permute-start.24 = (bf16[128,256]{1,0:T(8,128)(2,1)S(1)}, bf16[128,256]{1,0:T(8,128)(2,1)S(1)}, u32[]{:S(2)}, u32[]{:S(2)}) collective-permute-start(bf16[128,256]{1,0:T(8,128)(2,1)S(1)} %collective-permute-done.22.refs_9_), channel_id=1, source_target_pairs={{0,8},{1,9},{2,10},{3,11},{4,12},{5,13},{6,14},{7,15},{8,0},{9,1},... | collective-permute-start | bytes 196616 | tf_op jit(solution)/shard_map/ppermute | solution.py:246

commit v7 on v6

--- a/solution.py
+++ b/solution.py
@@ -203,14 +203,36 @@
         own[:, i : i + HS] = grads[i : i + HS, : own.shape[0]].T
 
 
-def place_kernel(meta, *refs):
-    out = refs[-1]
-    column = 0
-    for part in range(0, len(refs) - 1, 4):
-        for turn, block in zip((0, 2, 1, 3), refs[part : part + 4]):
+def place_kernel(meta, *refs, parts, first):
+    out, wide, sems = refs[-3:]
+    copies = []
+    size = wide.shape[3]
+    for part in range(parts):
+        columns = pl.ds((first + part) * size, size)
+        for i, (turn, block) in enumerate(zip((0, 2, 1, 3), refs[4 * part : 4 * part + 4])):
+            wide[part, i] = block[...].astype(F32)
             rows = pl.ds(pl.multiple_of((meta[2] ^ turn) * BLOCK, BLOCK), BLOCK)
-            out[rows, column : column + block.shape[1]] = block[...].astype(F32)
-        column += refs[part].shape[1]
+            copy = pltpu.make_async_copy(wide.at[part, i], out.at[rows, columns], sems.at[part, i])
+            copy.start()
+            copies.append(copy)
+    for copy in copies:
+        copy.wait()
+
+
+def place(meta, blocks, first, shape, before=()):
+    parts = len(blocks) // 4
+    return pl.pallas_call(
+        functools.partial(place_kernel, parts=parts, first=first),
+        in_specs=[smem()] + [vmem()] * len(blocks) + [hbm()] * len(before),
+        out_specs=hbm(),
+        out_shape=jax.ShapeDtypeStruct(shape, F32),
+        scratch_shapes=[
+            pltpu.VMEM((parts, 4, *blocks[0].shape), F32),
+            pltpu.SemaphoreType.DMA((parts, 4)),
+        ],
+        input_output_aliases={len(blocks) + 1: 0} if before else {},
+        compiler_params=params(8),
+    )(meta, *blocks, *before)
 
 
 def final_kernel(total, here, out, *, scale):
@@ -251,9 +273,9 @@
     s, d = lax.axis_index("seq"), lax.axis_index("dp")
     core, upper = s & 1, s >> 1
     orders = (
+        ((across, y), (y, z1), (z1, across), (z2, z2)),
         ((across, y), (y, across), (z1, z1), (z2, z2)),
-        ((across, y), (y, across), (z1, z1), (z2, z2)),
-        ((z1, z1), (across, y), (y, across), (z2, z2)),
+        ((z1, z1), (y, across), (across, y), (z2, z2)),
     )
     lane = jnp.arange(4 + 16 * len(orders), dtype=jnp.int32)
     bits = lane - 4
@@ -351,13 +373,8 @@
     parts[0] = finish(kept[0], after(here[0], latest))
     parts[1] = finish(kept[1], after(here[1], parts[0][0]))
     parts[2] = finish(kept[2], after(here[2], parts[1][0], parts[0][1]))
-    weight_grad = pl.pallas_call(
-        place_kernel,
-        in_specs=[smem()] + [vmem()] * 12,
-        out_specs=vmem(),
-        out_shape=jax.ShapeDtypeStruct((seq_count * rows, 3 * width), F32),
-        compiler_params=params(8),
-    )(meta, *parts[0], *parts[1], *parts[2])
+    shape = (seq_count * rows, 3 * width)
+    weight_grad = place(meta, parts[0] + parts[1] + parts[2], 0, shape)
     return (own[None], weight_grad)
 
 

time: 58.5 us -> 58.4 us (level)
  waiting for transfers between devices: 15.3 us -> 14.5 us
  starting transfers between devices: 29.7 us -> 30.4 us
    ppermute x25, waiting for transfers between devices: 15.3 us -> 14.5 us  [on_device(): lax.ppermute(value, AXES, partners(core0, core1, seq_count, dp_count))]
    ppermute x25, starting transfers between devices: 29.7 us -> 30.4 us  [on_device(): lax.ppermute(value, AXES, partners(core0, core1, seq_count, dp_count))]
where the time goes in v7:
time: 58.4 us; the launch traced here: 58.2 us
  starting transfers between devices  30.4 us (52%)
  waiting for transfers between devices  14.5 us (25%)
  Pallas kernels  11.6 us (20%)
  between operations  0.87 us (1%)
    ppermute x25, starting transfers between devices, on_device(): lax.ppermute(value, AXES, partners(core0, core1, seq_count, dp_count))  30.4 us
    ppermute x25, waiting for transfers between devices, on_device(): lax.ppermute(value, AXES, partners(core0, core1, seq_count, dp_count))  14.5 us
    pallas_call x1, Pallas kernels, on_device(): pl.pallas_call(keep_kernel, in_specs=[smem()] + [vmem()] * 3, out_specs=[...  2.49 us
    pallas_call x2, Pallas kernels, on_device(): pl.pallas_call(functools.partial(other_kernel, part=part), in_specs=[smem...  2.2 us
    pallas_call x1, Pallas kernels, on_device(): pl.pallas_call(state_kernel, in_specs=[smem()] + [hbm()] * 4, out_specs=[...  1.9 us
    pallas_call x1, Pallas kernels, place(): pl.pallas_call(functools.partial(place_kernel, parts=parts, first=first),...  1.78 us
    pallas_call x1, Pallas kernels, on_device(): pl.pallas_call(local_kernel, in_specs=[hbm()] + [vmem()] * 2, out_specs=[...  1.6 us
    pallas_call x1, Pallas kernels, on_device(): pl.pallas_call(functools.partial(first_kernel, scale=scale), in_specs=[sm...  1.34 us
  transfers between devices with their start and end apart: 25, of which 11 were waited for; matrix products, arithmetic and copies ran while one was open for 1% of the time, Pallas kernels for 15%

profile of v7, /device:TPU:0, one launch (start us, length us, event | category | flops | bytes accessed | tf_op | source)
XLA Modules:
  0.0 58.2 jit_solution(2938768240031998684)
XLA Ops:
  0.6 0.5 collective-permute-start.3
  1.2 1.9 %shard_map.68 = (bf16[2,128,128]{2,1,0:T(8,128)(2,1)S(1)}, bf16[4,256,256]{2,1,0:T(8,128)(2,1)S(1)}) custom-call(s32[52]{0:T(128)S(1)} %compare_select_fusion.2.meta, bf16[256,256]{1,0:T(8,128)(2,1)} %bitcast.8, bf16[256,256]{1,0:T(8,128)(2,1)} %bitcast.9, bf16[256,256]{1,0:T(8,128)(2,1)} %bitcast.10, bf16[256,256]{1,0:T(8,128)(2,1)} %bitcast.11), custom_call_target="tpu_custom_call" | custom-call | tf_op jit(solution)/shard_map/pallas_call | solution.py:294
  3.1 0.1 collective-permute-start
  3.2 2.9 %collective-permute-start.1 = (bf16[2,128,128]{2,1,0:T(8,128)(2,1)S(1)}, bf16[2,128,128]{2,1,0:T(8,128)(2,1)S(1)}, u32[]{:S(2)}, u32[]{:S(2)}) collective-permute-start(bf16[2,128,128]{2,1,0:T(8,128)(2,1)S(1)} %get-tuple-element.34), channel_id=1, source_target_pairs={{0,16},{1,17},{2,18},{3,19},{4,20},{5,21},{6,22},{7,23},{8,24},{9,... | collective-permute-start | bytes 196616 | tf_op jit(solution)/shard_map/ppermute | solution.py:268
  6.1 0.0 collective-permute-done.other
  6.1 1.6 %shard_map.69 = (f32[2,3,256,256]{3,2,1,0:T(8,128)S(1)}, bf16[2,3,2,128,256]{4,3,2,1,0:T(8,128)(2,1)S(1)}, bf16[2,2,2,128,128]{4,3,2,1,0:T(8,128)(2,1)S(1)}, bf16[256,4096]{1,0:T(8,128)(2,1)S(1)}) custom-call(bf16[256,4096]{1,0:T(8,128)(2,1)} %bitcast.7, bf16[4,256,256]{2,1,0:T(8,128)(2,1)S(1)} %get-tuple-element.30.mine, ...), custom_call_target="tpu_custom_call" | custom-call | tf_op jit(solution)/shard_map/pallas_call | solution.py:309
  7.8 0.7 %collective-permute-done.1.near = bf16[2,128,128]{2,1,0:T(8,128)(2,1)S(1)} collective-permute-done((bf16[2,128,128]{2,1,0:T(8,128)(2,1)S(1)}, bf16[2,128,128]{2,1,0:T(8,128)(2,1)S(1)}, u32[]{:S(2)}, u32[]{:S(2)}) %collective-permute-start.1) | collective-permute-done | bytes 65568 | tf_op jit(solution)/shard_map/ppermute | solution.py:268
  8.5 0.0 collective-permute-start.2
  8.5 1.3 %collective-permute-done.2.far = bf16[2,128,128]{2,1,0:T(8,128)(2,1)S(1)} collective-permute-done((bf16[2,128,128]{2,1,0:T(8,128)(2,1)S(1)}, bf16[2,128,128]{2,1,0:T(8,128)(2,1)S(1)}, u32[]{:S(2)}, u32[]{:S(2)}) %collective-permute-start.2) | collective-permute-done | bytes 65568 | tf_op jit(solution)/shard_map/ppermute | solution.py:268
  9.7 0.0 collective-permute-done.3.x1
  9.7 1.3 %shard_map.70 = (bf16[768,512]{1,0:T(8,128)(2,1)S(1)}, bf16[8,256,128]{2,1,0:T(8,128)(2,1)S(1)}) custom-call(s32[52]{0:T(128)S(1)} %compare_select_fusion.2.meta, f32[2,3,256,256]{3,2,1,0:T(8,128)S(1)} %get-tuple-element.31.local, bf16[2,3,2,128,256]{4,3,2,1,0:T(8,128)(2,1)S(1)} %get-tuple-element.32.turned, ...), custom_call_target="tpu_custom_call" | custom-call | tf_op jit(solution)/shard_map/pallas_call | solution.py:325
  11.1 2.0 %collective-permute-start.4 = (bf16[8,256,128]{2,1,0:T(8,128)(2,1)S(1)}, bf16[8,256,128]{2,1,0:T(8,128)(2,1)S(1)}, u32[]{:S(2)}, u32[]{:S(2)}) collective-permute-start(bf16[8,256,128]{2,1,0:T(8,128)(2,1)S(1)} %get-tuple-element.42), channel_id=1, source_target_pairs={{0,16},{1,17},{2,18},{3,19},{4,20},{5,21},{6,22},{7,23},{8,9},{9,8... | collective-permute-start | bytes 1572872 | tf_op jit(solution)/shard_map/ppermute | solution.py:268
  13.1 1.1 %shard_map.71 = bf16[8,256,128]{2,1,0:T(8,128)(2,1)S(1)} custom-call(s32[52]{0:T(128)S(1)} %compare_select_fusion.2.meta, bf16[768,512]{1,0:T(8,128)(2,1)S(1)} %get-tuple-element.39.grads, bf16[256,4096]{1,0:T(8,128)(2,1)S(1)} %get-tuple-element.36.x0, bf16[256,4096]{1,0:T(8,128)(2,1)S(1)} %collective-permute-done.3.x1), custom_call_target="tpu_custom_call" | custom-call | tf_op jit(solution)/shard_map/pallas_call | solution.py:334
  14.2 1.1 %shard_map.72 = bf16[8,256,128]{2,1,0:T(8,128)(2,1)S(1)} custom-call(s32[52]{0:T(128)S(1)} %compare_select_fusion.2.meta, bf16[768,512]{1,0:T(8,128)(2,1)S(1)} %get-tuple-element.39.grads, bf16[256,4096]{1,0:T(8,128)(2,1)S(1)} %get-tuple-element.36.x0, bf16[256,4096]{1,0:T(8,128)(2,1)S(1)} %collective-permute-done.3.x1), custom_call_target="tpu_custom_call" | custom-call | tf_op jit(solution)/shard_map/pallas_call | solution.py:334
  15.3 0.2 collective-permute-start.7
  15.5 2.0 %collective-permute-start.6 = (bf16[8,256,128]{2,1,0:T(8,128)(2,1)S(1)}, bf16[8,256,128]{2,1,0:T(8,128)(2,1)S(1)}, u32[]{:S(2)}, u32[]{:S(2)}) collective-permute-start(bf16[8,256,128]{2,1,0:T(8,128)(2,1)S(1)} %shard_map.71), channel_id=1, source_target_pairs={{0,2},{1,3},{2,0},{3,1},{4,6},{5,7},{6,4},{7,5},{8,10},{9,11},{10,... | collective-permute-start | bytes 1572872 | tf_op jit(solution)/shard_map/ppermute | solution.py:268
  17.5 2.5 %shard_map.73 = (bf16[8,256,128]{2,1,0:T(8,128)(2,1)S(1)}, bf16[8,256,128]{2,1,0:T(8,128)(2,1)S(1)}, bf16[8,256,128]{2,1,0:T(8,128)(2,1)S(1)}, bf16[256,768]{1,0:T(8,128)(2,1)}) custom-call(s32[52]{0:T(128)S(1)} %compare_select_fusion.2.meta, bf16[768,512]{1,0:T(8,128)(2,1)S(1)} %get-tuple-element.39.grads, bf16[256,4096]{1,0:T(8,128)(2,1)S(1)} %get-tuple-element.36.x0, ...), custom_call_target="tpu_custom_call" | custom-call | tf_op jit(solution)/shard_map/pallas_call | solution.py:342
  20.0 0.4 collective-permute-done.4
  20.3 0.1 convert_add_fusion.2
  20.5 2.0 %collective-permute-start.5 = (bf16[4,256,128]{2,1,0:T(8,128)(2,1)S(1)}, bf16[4,256,128]{2,1,0:T(8,128)(2,1)S(1)}, u32[]{:S(2)}, u32[]{:S(2)}) collective-permute-start(bf16[4,256,128]{2,1,0:T(8,128)(2,1)S(1)} %slice.116), channel_id=1, source_target_pairs={{0,1},{1,0},{2,3},{3,2},{4,5},{5,4},{6,7},{7,6},{8,10},{9,11},{10,... | collective-permute-start | bytes 786440 | tf_op jit(solution)/shard_map/ppermute | solution.py:268
  22.5 3.4 %collective-permute-done.7 = bf16[8,256,128]{2,1,0:T(8,128)(2,1)S(1)} collective-permute-done((bf16[8,256,128]{2,1,0:T(8,128)(2,1)S(1)}, bf16[8,256,128]{2,1,0:T(8,128)(2,1)S(1)}, u32[]{:S(2)}, u32[]{:S(2)}) %collective-permute-start.7) | collective-permute-done | bytes 524320 | tf_op jit(solution)/shard_map/ppermute | solution.py:268
  26.0 0.1 convert_add_fusion.1
  26.1 2.0 %collective-permute-start.10 = (bf16[4,256,128]{2,1,0:T(8,128)(2,1)S(1)}, bf16[4,256,128]{2,1,0:T(8,128)(2,1)S(1)}, u32[]{:S(2)}, u32[]{:S(2)}) collective-permute-start(bf16[4,256,128]{2,1,0:T(8,128)(2,1)S(1)} %slice.115), channel_id=1, source_target_pairs={{0,1},{1,0},{2,3},{3,2},{4,5},{5,4},{6,7},{7,6},{8,24},{9,25},{10,... | collective-permute-start | bytes 786440 | tf_op jit(solution)/shard_map/ppermute | solution.py:268
  28.1 2.1 %collective-permute-done.6 = bf16[8,256,128]{2,1,0:T(8,128)(2,1)S(1)} collective-permute-done((bf16[8,256,128]{2,1,0:T(8,128)(2,1)S(1)}, bf16[8,256,128]{2,1,0:T(8,128)(2,1)S(1)}, u32[]{:S(2)}, u32[]{:S(2)}) %collective-permute-start.6) | collective-permute-done | bytes 524320 | tf_op jit(solution)/shard_map/ppermute | solution.py:268
  30.3 0.1 convert_add_fusion
  30.4 2.1 %collective-permute-start.9 = (bf16[4,256,128]{2,1,0:T(8,128)(2,1)S(1)}, bf16[4,256,128]{2,1,0:T(8,128)(2,1)S(1)}, u32[]{:S(2)}, u32[]{:S(2)}) collective-permute-start(bf16[4,256,128]{2,1,0:T(8,128)(2,1)S(1)} %slice.114), channel_id=1, source_target_pairs={{0,1},{1,0},{2,3},{3,2},{4,5},{5,4},{6,7},{7,6},{8,24},{9,25},{10,... | collective-permute-start | bytes 786440 | tf_op jit(solution)/shard_map/ppermute | solution.py:268
  32.5 0.0 collective-permute-done.5
  32.6 1.6 %collective-permute-start.8 = (bf16[2,256,128]{2,1,0:T(8,128)(2,1)S(1)}, bf16[2,256,128]{2,1,0:T(8,128)(2,1)S(1)}, u32[]{:S(2)}, u32[]{:S(2)}) collective-permute-start(bf16[2,256,128]{2,1,0:T(8,128)(2,1)S(1)} %slice.119), channel_id=1, source_target_pairs={{0,2},{1,3},{2,0},{3,1},{4,6},{5,7},{6,4},{7,5},{8,24},{9,25},{10,... | collective-permute-start | bytes 393224 | tf_op jit(solution)/shard_map/ppermute | solution.py:268
  34.2 0.0 collective-permute-done.10
  34.2 0.1 slice_add_fusion
  34.3 0.5 collective-permute-start.13
  34.8 2.0 %collective-permute-done.9 = bf16[4,256,128]{2,1,0:T(8,128)(2,1)S(1)} collective-permute-done((bf16[4,256,128]{2,1,0:T(8,128)(2,1)S(1)}, bf16[4,256,128]{2,1,0:T(8,128)(2,1)S(1)}, u32[]{:S(2)}, u32[]{:S(2)}) %collective-permute-start.9) | collective-permute-done | bytes 262176 | tf_op jit(solution)/shard_map/ppermute | solution.py:268
  36.9 0.1 slice_add_fusion.1
  37.0 2.0 %collective-permute-start.12 = (bf16[2,256,128]{2,1,0:T(8,128)(2,1)S(1)}, bf16[2,256,128]{2,1,0:T(8,128)(2,1)S(1)}, u32[]{:S(2)}, u32[]{:S(2)}) collective-permute-start(bf16[2,256,128]{2,1,0:T(8,128)(2,1)S(1)} %slice.117), channel_id=1, source_target_pairs={{0,16},{1,17},{2,18},{3,19},{4,20},{5,21},{6,22},{7,23},{8,9},{9,8... | collective-permute-start | bytes 393224 | tf_op jit(solution)/shard_map/ppermute | solution.py:268
  39.0 0.0 collective-permute-done.8
  39.0 2.7 %collective-permute-start.11 = (bf16[1,256,128]{2,1,0:T(8,128)(2,1)S(1)}, bf16[1,256,128]{2,1,0:T(8,128)(2,1)S(1)}, u32[]{:S(2)}, u32[]{:S(2)}) collective-permute-start(bf16[1,256,128]{2,1,0:T(8,128)(2,1)S(1)} %slice.122), channel_id=1, source_target_pairs={{0,4},{1,5},{2,6},{3,7},{4,0},{5,1},{6,2},{7,3},{8,12},{9,13},{10,... | collective-permute-start | bytes 196616 | tf_op jit(solution)/shard_map/ppermute | solution.py:268
  41.7 0.0 collective-permute-done.13
  41.8 2.0 %collective-permute-start.17 = (bf16[1,256,128]{2,1,0:T(8,128)(2,1)S(1)}, bf16[1,256,128]{2,1,0:T(8,128)(2,1)S(1)}, u32[]{:S(2)}, u32[]{:S(2)}) collective-permute-start(bf16[1,256,128]{2,1,0:T(8,128)(2,1)S(1)} %slice.121), channel_id=1, source_target_pairs={{0,4},{1,5},{2,6},{3,7},{4,0},{5,1},{6,2},{7,3},{8,12},{9,13},{10,... | collective-permute-start | bytes 196616 | tf_op jit(solution)/shard_map/ppermute | solution.py:268
  43.8 0.0 collective-permute-done.12
  43.9 1.3 %collective-permute-start.21 = (bf16[1,256,128]{2,1,0:T(8,128)(2,1)S(1)}, bf16[1,256,128]{2,1,0:T(8,128)(2,1)S(1)}, u32[]{:S(2)}, u32[]{:S(2)}) collective-permute-start(bf16[1,256,128]{2,1,0:T(8,128)(2,1)S(1)} %slice.120), channel_id=1, source_target_pairs={{0,4},{1,5},{2,6},{3,7},{4,0},{5,1},{6,2},{7,3},{8,12},{9,13},{10,... | collective-permute-start | bytes 196616 | tf_op jit(solution)/shard_map/ppermute | solution.py:268
  45.2 0.8 %collective-permute-done.11.here = bf16[1,256,128]{2,1,0:T(8,128)(2,1)S(1)} collective-permute-done((bf16[1,256,128]{2,1,0:T(8,128)(2,1)S(1)}, bf16[1,256,128]{2,1,0:T(8,128)(2,1)S(1)}, u32[]{:S(2)}, u32[]{:S(2)}) %collective-permute-start.11) | collective-permute-done | bytes 65568 | tf_op jit(solution)/shard_map/ppermute | solution.py:268
  45.9 0.1 shard_map.74.refs_0_
  46.0 1.8 %collective-permute-start.14 = (bf16[128,256]{1,0:T(8,128)(2,1)S(1)}, bf16[128,256]{1,0:T(8,128)(2,1)S(1)}, u32[]{:S(2)}, u32[]{:S(2)}) collective-permute-start(bf16[128,256]{1,0:T(8,128)(2,1)S(1)} %shard_map.74.refs_0_), channel_id=1, source_target_pairs={{0,16},{1,17},{2,18},{3,19},{4,20},{5,21},{6,22},{7,23},{8,24},{9,... | collective-permute-start | bytes 196616 | tf_op jit(solution)/shard_map/ppermute | solution.py:268
  47.8 0.6 %collective-permute-done.17.here = bf16[1,256,128]{2,1,0:T(8,128)(2,1)S(1)} collective-permute-done((bf16[1,256,128]{2,1,0:T(8,128)(2,1)S(1)}, bf16[1,256,128]{2,1,0:T(8,128)(2,1)S(1)}, u32[]{:S(2)}, u32[]{:S(2)}) %collective-permute-start.17) | collective-permute-done | bytes 65568 | tf_op jit(solution)/shard_map/ppermute | solution.py:268
  48.5 0.1 shard_map.75.refs_4_
  48.6 0.1 collective-permute-start.19
  48.7 2.0 %collective-permute-start.18 = (bf16[128,256]{1,0:T(8,128)(2,1)S(1)}, bf16[128,256]{1,0:T(8,128)(2,1)S(1)}, u32[]{:S(2)}, u32[]{:S(2)}) collective-permute-start(bf16[128,256]{1,0:T(8,128)(2,1)S(1)} %shard_map.75.refs_4_), channel_id=1, source_target_pairs={{0,16},{1,17},{2,18},{3,19},{4,20},{5,21},{6,22},{7,23},{8,24},{9,... | collective-permute-start | bytes 196616 | tf_op jit(solution)/shard_map/ppermute | solution.py:268
  50.7 0.0 collective-permute-done.21.here
  50.7 0.0 collective-permute-done.14.refs_1_
  50.7 0.1 shard_map.76.refs_8_
  50.8 1.4 %collective-permute-start.22 = (bf16[128,256]{1,0:T(8,128)(2,1)S(1)}, bf16[128,256]{1,0:T(8,128)(2,1)S(1)}, u32[]{:S(2)}, u32[]{:S(2)}) collective-permute-start(bf16[128,256]{1,0:T(8,128)(2,1)S(1)} %shard_map.76.refs_8_), channel_id=1, source_target_pairs={{0,16},{1,17},{2,18},{3,19},{4,20},{5,21},{6,22},{7,23},{8,24},{9,... | collective-permute-start | bytes 196616 | tf_op jit(solution)/shard_map/ppermute | solution.py:268
  52.3 0.0 collective-permute-start.15
  52.3 0.5 collective-permute-start.23
  52.8 0.6 %collective-permute-done.18.refs_5_ = bf16[128,256]{1,0:T(8,128)(2,1)S(1)} collective-permute-done((bf16[128,256]{1,0:T(8,128)(2,1)S(1)}, bf16[128,256]{1,0:T(8,128)(2,1)S(1)}, u32[]{:S(2)}, u32[]{:S(2)}) %collective-permute-start.18) | collective-permute-done | bytes 65568 | tf_op jit(solution)/shard_map/ppermute | solution.py:268
  53.4 0.0 collective-permute-start.20
  53.4 0.0 collective-permute-done.19.refs_6_
  53.4 0.5 collective-permute-start.16
  53.9 1.2 %collective-permute-done.22.refs_9_ = bf16[128,256]{1,0:T(8,128)(2,1)S(1)} collective-permute-done((bf16[128,256]{1,0:T(8,128)(2,1)S(1)}, bf16[128,256]{1,0:T(8,128)(2,1)S(1)}, u32[]{:S(2)}, u32[]{:S(2)}) %collective-permute-start.22) | collective-permute-done | bytes 65568 | tf_op jit(solution)/shard_map/ppermute | solution.py:268
  55.2 0.0 collective-permute-start.24
  55.2 0.0 collective-permute-done.15.refs_2_
  55.2 0.0 collective-permute-done.20.refs_7_
  55.2 0.0 collective-permute-done.16.refs_3_
  55.2 1.2 %collective-permute-done.24.refs_11_ = bf16[128,256]{1,0:T(8,128)(2,1)S(1)} collective-permute-done((bf16[128,256]{1,0:T(8,128)(2,1)S(1)}, bf16[128,256]{1,0:T(8,128)(2,1)S(1)}, u32[]{:S(2)}, u32[]{:S(2)}) %collective-permute-start.24) | collective-permute-done | bytes 65568 | tf_op jit(solution)/shard_map/ppermute | solution.py:268
  56.4 1.8 %shard_map.77 = f32[512,768]{1,0:T(8,128)} custom-call(s32[52]{0:T(128)S(1)} %compare_select_fusion.2.meta, bf16[128,256]{1,0:T(8,128)(2,1)S(1)} %shard_map.74.refs_0_, bf16[128,256]{1,0:T(8,128)(2,1)S(1)} %collective-permute-done.14.refs_1_, bf16[128,256]{1,0:T(8,128)(2,1)S(1)} %collective-permute-done.15.refs_2_, ...), custom_call_target="tpu_custom_call" | custom-call | tf_op jit(solution)/shard_map/pallas_call | solution.py:224
  (18 shorter events, 0.4 us)
Async XLA Ops:
  0.6 9.1 %collective-permute-start.3 = (bf16[256,4096]{1,0:T(8,128)(2,1)}, bf16[256,4096]{1,0:T(8,128)(2,1)S(1)}, u32[]{:S(2)}, u32[]{:S(2)}) collective-permute-start(bf16[256,4096]{1,0:T(8,128)(2,1)} %bitcast.6), channel_id=1, source_target_pairs={{0,8},{1,9},{2,10},{3,11},{4,12},{5,13},{6,14},{7,15},{8,0},{9,1},... | collective-permute-start | bytes 6291464 | tf_op jit(solution)/shard_map/ppermute | solution.py:268
  3.1 3.1 %collective-permute-start = (bf16[4,256,256]{2,1,0:T(8,128)(2,1)S(1)}, bf16[4,256,256]{2,1,0:T(8,128)(2,1)S(1)}, u32[]{:S(2)}, u32[]{:S(2)}) collective-permute-start(bf16[4,256,256]{2,1,0:T(8,128)(2,1)S(1)} %get-tuple-element.30.mine), channel_id=1, source_target_pairs={{0,8},{1,9},{2,10},{3,11},{4,12},{5,13},{6,14},{7,15},{8,0},{9,1},... | collective-permute-start | bytes 1572872 | tf_op jit(solution)/shard_map/ppermute | solution.py:268
  3.2 5.3 %collective-permute-start.1 = (bf16[2,128,128]{2,1,0:T(8,128)(2,1)S(1)}, bf16[2,128,128]{2,1,0:T(8,128)(2,1)S(1)}, u32[]{:S(2)}, u32[]{:S(2)}) collective-permute-start(bf16[2,128,128]{2,1,0:T(8,128)(2,1)S(1)} %get-tuple-element.34), channel_id=1, source_target_pairs={{0,16},{1,17},{2,18},{3,19},{4,20},{5,21},{6,22},{7,23},{8,24},{9,... | collective-permute-start | bytes 196616 | tf_op jit(solution)/shard_map/ppermute | solution.py:268
  8.5 1.3 %collective-permute-start.2 = (bf16[2,128,128]{2,1,0:T(8,128)(2,1)S(1)}, bf16[2,128,128]{2,1,0:T(8,128)(2,1)S(1)}, u32[]{:S(2)}, u32[]{:S(2)}) collective-permute-start(bf16[2,128,128]{2,1,0:T(8,128)(2,1)S(1)} %collective-permute-done.1.near), channel_id=1, source_target_pairs={{0,8},{1,9},{2,10},{3,11},{4,12},{5,13},{6,14},{7,15},{8,0},{9,1},... | collective-permute-start | bytes 196616 | tf_op jit(solution)/shard_map/ppermute | solution.py:268
  11.1 9.2 %collective-permute-start.4 = (bf16[8,256,128]{2,1,0:T(8,128)(2,1)S(1)}, bf16[8,256,128]{2,1,0:T(8,128)(2,1)S(1)}, u32[]{:S(2)}, u32[]{:S(2)}) collective-permute-start(bf16[8,256,128]{2,1,0:T(8,128)(2,1)S(1)} %get-tuple-element.42), channel_id=1, source_target_pairs={{0,16},{1,17},{2,18},{3,19},{4,20},{5,21},{6,22},{7,23},{8,9},{9,8... | collective-permute-start | bytes 1572872 | tf_op jit(solution)/shard_map/ppermute | solution.py:268
  15.3 10.7 %collective-permute-start.7 = (bf16[8,256,128]{2,1,0:T(8,128)(2,1)S(1)}, bf16[8,256,128]{2,1,0:T(8,128)(2,1)S(1)}, u32[]{:S(2)}, u32[]{:S(2)}) collective-permute-start(bf16[8,256,128]{2,1,0:T(8,128)(2,1)S(1)} %shard_map.72), channel_id=1, source_target_pairs={{0,16},{1,17},{2,18},{3,19},{4,20},{5,21},{6,22},{7,23},{8,9},{9,8... | collective-permute-start | bytes 1572872 | tf_op jit(solution)/shard_map/ppermute | solution.py:268
  15.5 14.8 %collective-permute-start.6 = (bf16[8,256,128]{2,1,0:T(8,128)(2,1)S(1)}, bf16[8,256,128]{2,1,0:T(8,128)(2,1)S(1)}, u32[]{:S(2)}, u32[]{:S(2)}) collective-permute-start(bf16[8,256,128]{2,1,0:T(8,128)(2,1)S(1)} %shard_map.71), channel_id=1, source_target_pairs={{0,2},{1,3},{2,0},{3,1},{4,6},{5,7},{6,4},{7,5},{8,10},{9,11},{10,... | collective-permute-start | bytes 1572872 | tf_op jit(solution)/shard_map/ppermute | solution.py:268
  20.5 12.0 %collective-permute-start.5 = (bf16[4,256,128]{2,1,0:T(8,128)(2,1)S(1)}, bf16[4,256,128]{2,1,0:T(8,128)(2,1)S(1)}, u32[]{:S(2)}, u32[]{:S(2)}) collective-permute-start(bf16[4,256,128]{2,1,0:T(8,128)(2,1)S(1)} %slice.116), channel_id=1, source_target_pairs={{0,1},{1,0},{2,3},{3,2},{4,5},{5,4},{6,7},{7,6},{8,10},{9,11},{10,... | collective-permute-start | bytes 786440 | tf_op jit(solution)/shard_map/ppermute | solution.py:268
  26.1 8.1 %collective-permute-start.10 = (bf16[4,256,128]{2,1,0:T(8,128)(2,1)S(1)}, bf16[4,256,128]{2,1,0:T(8,128)(2,1)S(1)}, u32[]{:S(2)}, u32[]{:S(2)}) collective-permute-start(bf16[4,256,128]{2,1,0:T(8,128)(2,1)S(1)} %slice.115), channel_id=1, source_target_pairs={{0,1},{1,0},{2,3},{3,2},{4,5},{5,4},{6,7},{7,6},{8,24},{9,25},{10,... | collective-permute-start | bytes 786440 | tf_op jit(solution)/shard_map/ppermute | solution.py:268
  30.4 6.4 %collective-permute-start.9 = (bf16[4,256,128]{2,1,0:T(8,128)(2,1)S(1)}, bf16[4,256,128]{2,1,0:T(8,128)(2,1)S(1)}, u32[]{:S(2)}, u32[]{:S(2)}) collective-permute-start(bf16[4,256,128]{2,1,0:T(8,128)(2,1)S(1)} %slice.114), channel_id=1, source_target_pairs={{0,1},{1,0},{2,3},{3,2},{4,5},{5,4},{6,7},{7,6},{8,24},{9,25},{10,... | collective-permute-start | bytes 786440 | tf_op jit(solution)/shard_map/ppermute | solution.py:268
  32.6 6.4 %collective-permute-start.8 = (bf16[2,256,128]{2,1,0:T(8,128)(2,1)S(1)}, bf16[2,256,128]{2,1,0:T(8,128)(2,1)S(1)}, u32[]{:S(2)}, u32[]{:S(2)}) collective-permute-start(bf16[2,256,128]{2,1,0:T(8,128)(2,1)S(1)} %slice.119), channel_id=1, source_target_pairs={{0,2},{1,3},{2,0},{3,1},{4,6},{5,7},{6,4},{7,5},{8,24},{9,25},{10,... | collective-permute-start | bytes 393224 | tf_op jit(solution)/shard_map/ppermute | solution.py:268
  34.3 7.4 %collective-permute-start.13 = (bf16[2,256,128]{2,1,0:T(8,128)(2,1)S(1)}, bf16[2,256,128]{2,1,0:T(8,128)(2,1)S(1)}, u32[]{:S(2)}, u32[]{:S(2)}) collective-permute-start(bf16[2,256,128]{2,1,0:T(8,128)(2,1)S(1)} %slice.118), channel_id=1, source_target_pairs={{0,2},{1,3},{2,0},{3,1},{4,6},{5,7},{6,4},{7,5},{8,10},{9,11},{10,... | collective-permute-start | bytes 393224 | tf_op jit(solution)/shard_map/ppermute | solution.py:268
  37.0 6.9 %collective-permute-start.12 = (bf16[2,256,128]{2,1,0:T(8,128)(2,1)S(1)}, bf16[2,256,128]{2,1,0:T(8,128)(2,1)S(1)}, u32[]{:S(2)}, u32[]{:S(2)}) collective-permute-start(bf16[2,256,128]{2,1,0:T(8,128)(2,1)S(1)} %slice.117), channel_id=1, source_target_pairs={{0,16},{1,17},{2,18},{3,19},{4,20},{5,21},{6,22},{7,23},{8,9},{9,8... | collective-permute-start | bytes 393224 | tf_op jit(solution)/shard_map/ppermute | solution.py:268
  39.0 6.9 %collective-permute-start.11 = (bf16[1,256,128]{2,1,0:T(8,128)(2,1)S(1)}, bf16[1,256,128]{2,1,0:T(8,128)(2,1)S(1)}, u32[]{:S(2)}, u32[]{:S(2)}) collective-permute-start(bf16[1,256,128]{2,1,0:T(8,128)(2,1)S(1)} %slice.122), channel_id=1, source_target_pairs={{0,4},{1,5},{2,6},{3,7},{4,0},{5,1},{6,2},{7,3},{8,12},{9,13},{10,... | collective-permute-start | bytes 196616 | tf_op jit(solution)/shard_map/ppermute | solution.py:268
  41.8 6.7 %collective-permute-start.17 = (bf16[1,256,128]{2,1,0:T(8,128)(2,1)S(1)}, bf16[1,256,128]{2,1,0:T(8,128)(2,1)S(1)}, u32[]{:S(2)}, u32[]{:S(2)}) collective-permute-start(bf16[1,256,128]{2,1,0:T(8,128)(2,1)S(1)} %slice.121), channel_id=1, source_target_pairs={{0,4},{1,5},{2,6},{3,7},{4,0},{5,1},{6,2},{7,3},{8,12},{9,13},{10,... | collective-permute-start | bytes 196616 | tf_op jit(solution)/shard_map/ppermute | solution.py:268
  43.9 6.8 %collective-permute-start.21 = (bf16[1,256,128]{2,1,0:T(8,128)(2,1)S(1)}, bf16[1,256,128]{2,1,0:T(8,128)(2,1)S(1)}, u32[]{:S(2)}, u32[]{:S(2)}) collective-permute-start(bf16[1,256,128]{2,1,0:T(8,128)(2,1)S(1)} %slice.120), channel_id=1, source_target_pairs={{0,4},{1,5},{2,6},{3,7},{4,0},{5,1},{6,2},{7,3},{8,12},{9,13},{10,... | collective-permute-start | bytes 196616 | tf_op jit(solution)/shard_map/ppermute | solution.py:268
  46.0 4.7 %collective-permute-start.14 = (bf16[128,256]{1,0:T(8,128)(2,1)S(1)}, bf16[128,256]{1,0:T(8,128)(2,1)S(1)}, u32[]{:S(2)}, u32[]{:S(2)}) collective-permute-start(bf16[128,256]{1,0:T(8,128)(2,1)S(1)} %shard_map.74.refs_0_), channel_id=1, source_target_pairs={{0,16},{1,17},{2,18},{3,19},{4,20},{5,21},{6,22},{7,23},{8,24},{9,... | collective-permute-start | bytes 196616 | tf_op jit(solution)/shard_map/ppermute | solution.py:268
  48.6 4.8 %collective-permute-start.19 = (bf16[128,256]{1,0:T(8,128)(2,1)S(1)}, bf16[128,256]{1,0:T(8,128)(2,1)S(1)}, u32[]{:S(2)}, u32[]{:S(2)}) collective-permute-start(bf16[128,256]{1,0:T(8,128)(2,1)S(1)} %shard_map.75.refs_4_), channel_id=1, source_target_pairs={{0,8},{1,9},{2,10},{3,11},{4,12},{5,13},{6,14},{7,15},{8,0},{9,1},... | collective-permute-start | bytes 196616 | tf_op jit(solution)/shard_map/ppermute | solution.py:268
  48.7 4.7 %collective-permute-start.18 = (bf16[128,256]{1,0:T(8,128)(2,1)S(1)}, bf16[128,256]{1,0:T(8,128)(2,1)S(1)}, u32[]{:S(2)}, u32[]{:S(2)}) collective-permute-start(bf16[128,256]{1,0:T(8,128)(2,1)S(1)} %shard_map.75.refs_4_), channel_id=1, source_target_pairs={{0,16},{1,17},{2,18},{3,19},{4,20},{5,21},{6,22},{7,23},{8,24},{9,... | collective-permute-start | bytes 196616 | tf_op jit(solution)/shard_map/ppermute | solution.py:268
  50.8 4.3 %collective-permute-start.22 = (bf16[128,256]{1,0:T(8,128)(2,1)S(1)}, bf16[128,256]{1,0:T(8,128)(2,1)S(1)}, u32[]{:S(2)}, u32[]{:S(2)}) collective-permute-start(bf16[128,256]{1,0:T(8,128)(2,1)S(1)} %shard_map.76.refs_8_), channel_id=1, source_target_pairs={{0,16},{1,17},{2,18},{3,19},{4,20},{5,21},{6,22},{7,23},{8,24},{9,... | collective-permute-start | bytes 196616 | tf_op jit(solution)/shard_map/ppermute | solution.py:268
  52.3 2.9 %collective-permute-start.15 = (bf16[128,256]{1,0:T(8,128)(2,1)S(1)}, bf16[128,256]{1,0:T(8,128)(2,1)S(1)}, u32[]{:S(2)}, u32[]{:S(2)}) collective-permute-start(bf16[128,256]{1,0:T(8,128)(2,1)S(1)} %shard_map.74.refs_0_), channel_id=1, source_target_pairs={{0,8},{1,9},{2,10},{3,11},{4,12},{5,13},{6,14},{7,15},{8,0},{9,1},... | collective-permute-start | bytes 196616 | tf_op jit(solution)/shard_map/ppermute | solution.py:268
  52.3 2.9 %collective-permute-start.23 = (bf16[128,256]{1,0:T(8,128)(2,1)S(1)}, bf16[128,256]{1,0:T(8,128)(2,1)S(1)}, u32[]{:S(2)}, u32[]{:S(2)}) collective-permute-start(bf16[128,256]{1,0:T(8,128)(2,1)S(1)} %shard_map.76.refs_8_), channel_id=1, source_target_pairs={{0,8},{1,9},{2,10},{3,11},{4,12},{5,13},{6,14},{7,15},{8,0},{9,1},... | collective-permute-start | bytes 196616 | tf_op jit(solution)/shard_map/ppermute | solution.py:268
  53.4 1.8 %collective-permute-start.20 = (bf16[128,256]{1,0:T(8,128)(2,1)S(1)}, bf16[128,256]{1,0:T(8,128)(2,1)S(1)}, u32[]{:S(2)}, u32[]{:S(2)}) collective-permute-start(bf16[128,256]{1,0:T(8,128)(2,1)S(1)} %collective-permute-done.18.refs_5_), channel_id=1, source_target_pairs={{0,8},{1,9},{2,10},{3,11},{4,12},{5,13},{6,14},{7,15},{8,0},{9,1},... | collective-permute-start | bytes 196616 | tf_op jit(solution)/shard_map/ppermute | solution.py:268
  53.4 1.8 %collective-permute-start.16 = (bf16[128,256]{1,0:T(8,128)(2,1)S(1)}, bf16[128,256]{1,0:T(8,128)(2,1)S(1)}, u32[]{:S(2)}, u32[]{:S(2)}) collective-permute-start(bf16[128,256]{1,0:T(8,128)(2,1)S(1)} %collective-permute-done.14.refs_1_), channel_id=1, source_target_pairs={{0,8},{1,9},{2,10},{3,11},{4,12},{5,13},{6,14},{7,15},{8,0},{9,1},... | collective-permute-start | bytes 196616 | tf_op jit(solution)/shard_map/ppermute | solution.py:268
  55.2 1.3 %collective-permute-start.24 = (bf16[128,256]{1,0:T(8,128)(2,1)S(1)}, bf16[128,256]{1,0:T(8,128)(2,1)S(1)}, u32[]{:S(2)}, u32[]{:S(2)}) collective-permute-start(bf16[128,256]{1,0:T(8,128)(2,1)S(1)} %collective-permute-done.22.refs_9_), channel_id=1, source_target_pairs={{0,8},{1,9},{2,10},{3,11},{4,12},{5,13},{6,14},{7,15},{8,0},{9,1},... | collective-permute-start | bytes 196616 | tf_op jit(solution)/shard_map/ppermute | solution.py:268

commit v8 on v7

--- a/solution.py
+++ b/solution.py
@@ -365,7 +365,7 @@
         return final, facing, swap(final, sibling, sibling), swap(facing, sibling, sibling)
 
     latest = kept[0]
-    for part, level in ((0, 1), (1, 1), (2, 1), (0, 2), (1, 2), (2, 2), (0, 3), (1, 3), (2, 3)):
+    for part, level in ((0, 1), (1, 1), (2, 1), (0, 2), (1, 2), (2, 2), (0, 3), (2, 3), (1, 3)):
         kept[part], latest, here[part] = step(
             kept[part], after(here[part], latest), orders[part][level]
         )

time: 58.4 us -> 58.2 us (level)
  starting transfers between devices: 30.4 us -> 29.1 us
  waiting for transfers between devices: 14.5 us -> 15.6 us
    ppermute x25, starting transfers between devices: 30.4 us -> 29.1 us  [on_device(): lax.ppermute(value, AXES, partners(core0, core1, seq_count, dp_count))]
    ppermute x25, waiting for transfers between devices: 14.5 us -> 15.6 us  [on_device(): lax.ppermute(value, AXES, partners(core0, core1, seq_count, dp_count))]
  transfers between devices with their start and end apart: 25 -> 25, of which waited for: 11 -> 14; matrix products, arithmetic and copies ran while one was open for 1% -> 1% of each run, Pallas kernels for 15% -> 15%
where the time goes in v8:
time: 58.2 us; the launch traced here: 58 us
  starting transfers between devices  29.1 us (50%)
  waiting for transfers between devices  15.6 us (27%)
  Pallas kernels  11.6 us (20%)
  between operations  0.88 us (2%)
    ppermute x25, starting transfers between devices, on_device(): lax.ppermute(value, AXES, partners(core0, core1, seq_count, dp_count))  29.1 us
    ppermute x25, waiting for transfers between devices, on_device(): lax.ppermute(value, AXES, partners(core0, core1, seq_count, dp_count))  15.6 us
    pallas_call x1, Pallas kernels, on_device(): pl.pallas_call(keep_kernel, in_specs=[smem()] + [vmem()] * 3, out_specs=[...  2.49 us
    pallas_call x2, Pallas kernels, on_device(): pl.pallas_call(functools.partial(other_kernel, part=part), in_specs=[smem...  2.2 us
    pallas_call x1, Pallas kernels, on_device(): pl.pallas_call(state_kernel, in_specs=[smem()] + [hbm()] * 4, out_specs=[...  1.9 us
    pallas_call x1, Pallas kernels, place(): pl.pallas_call(functools.partial(place_kernel, parts=parts, first=first),...  1.78 us
    pallas_call x1, Pallas kernels, on_device(): pl.pallas_call(local_kernel, in_specs=[hbm()] + [vmem()] * 2, out_specs=[...  1.6 us
    pallas_call x1, Pallas kernels, on_device(): pl.pallas_call(functools.partial(first_kernel, scale=scale), in_specs=[sm...  1.34 us
  transfers between devices with their start and end apart: 25, of which 14 were waited for; matrix products, arithmetic and copies ran while one was open for 1% of the time, Pallas kernels for 15%

profile of v8, /device:TPU:0, one launch (start us, length us, event | category | flops | bytes accessed | tf_op | source)
XLA Modules:
  0.0 58.0 jit_solution(18164656060893844706)
XLA Ops:
  0.6 0.5 collective-permute-start.3
  1.2 1.9 %shard_map.68 = (bf16[2,128,128]{2,1,0:T(8,128)(2,1)S(1)}, bf16[4,256,256]{2,1,0:T(8,128)(2,1)S(1)}) custom-call(s32[52]{0:T(128)S(1)} %compare_select_fusion.2.meta, bf16[256,256]{1,0:T(8,128)(2,1)} %bitcast.8, bf16[256,256]{1,0:T(8,128)(2,1)} %bitcast.9, bf16[256,256]{1,0:T(8,128)(2,1)} %bitcast.10, bf16[256,256]{1,0:T(8,128)(2,1)} %bitcast.11), custom_call_target="tpu_custom_call" | custom-call | tf_op jit(solution)/shard_map/pallas_call | solution.py:294
  3.1 0.1 collective-permute-start
  3.2 2.9 %collective-permute-start.1 = (bf16[2,128,128]{2,1,0:T(8,128)(2,1)S(1)}, bf16[2,128,128]{2,1,0:T(8,128)(2,1)S(1)}, u32[]{:S(2)}, u32[]{:S(2)}) collective-permute-start(bf16[2,128,128]{2,1,0:T(8,128)(2,1)S(1)} %get-tuple-element.34), channel_id=1, source_target_pairs={{0,16},{1,17},{2,18},{3,19},{4,20},{5,21},{6,22},{7,23},{8,24},{9,... | collective-permute-start | bytes 196616 | tf_op jit(solution)/shard_map/ppermute | solution.py:268
  6.1 0.0 collective-permute-done.other
  6.1 1.6 %shard_map.69 = (f32[2,3,256,256]{3,2,1,0:T(8,128)S(1)}, bf16[2,3,2,128,256]{4,3,2,1,0:T(8,128)(2,1)S(1)}, bf16[2,2,2,128,128]{4,3,2,1,0:T(8,128)(2,1)S(1)}, bf16[256,4096]{1,0:T(8,128)(2,1)S(1)}) custom-call(bf16[256,4096]{1,0:T(8,128)(2,1)} %bitcast.7, bf16[4,256,256]{2,1,0:T(8,128)(2,1)S(1)} %get-tuple-element.30.mine, ...), custom_call_target="tpu_custom_call" | custom-call | tf_op jit(solution)/shard_map/pallas_call | solution.py:309
  7.8 0.7 %collective-permute-done.1.near = bf16[2,128,128]{2,1,0:T(8,128)(2,1)S(1)} collective-permute-done((bf16[2,128,128]{2,1,0:T(8,128)(2,1)S(1)}, bf16[2,128,128]{2,1,0:T(8,128)(2,1)S(1)}, u32[]{:S(2)}, u32[]{:S(2)}) %collective-permute-start.1) | collective-permute-done | bytes 65568 | tf_op jit(solution)/shard_map/ppermute | solution.py:268
  8.5 0.0 collective-permute-start.2
  8.5 1.3 %collective-permute-done.2.far = bf16[2,128,128]{2,1,0:T(8,128)(2,1)S(1)} collective-permute-done((bf16[2,128,128]{2,1,0:T(8,128)(2,1)S(1)}, bf16[2,128,128]{2,1,0:T(8,128)(2,1)S(1)}, u32[]{:S(2)}, u32[]{:S(2)}) %collective-permute-start.2) | collective-permute-done | bytes 65568 | tf_op jit(solution)/shard_map/ppermute | solution.py:268
  9.7 0.0 collective-permute-done.3.x1
  9.7 1.3 %shard_map.70 = (bf16[768,512]{1,0:T(8,128)(2,1)S(1)}, bf16[8,256,128]{2,1,0:T(8,128)(2,1)S(1)}) custom-call(s32[52]{0:T(128)S(1)} %compare_select_fusion.2.meta, f32[2,3,256,256]{3,2,1,0:T(8,128)S(1)} %get-tuple-element.31.local, bf16[2,3,2,128,256]{4,3,2,1,0:T(8,128)(2,1)S(1)} %get-tuple-element.32.turned, ...), custom_call_target="tpu_custom_call" | custom-call | tf_op jit(solution)/shard_map/pallas_call | solution.py:325
  11.1 2.0 %collective-permute-start.4 = (bf16[8,256,128]{2,1,0:T(8,128)(2,1)S(1)}, bf16[8,256,128]{2,1,0:T(8,128)(2,1)S(1)}, u32[]{:S(2)}, u32[]{:S(2)}) collective-permute-start(bf16[8,256,128]{2,1,0:T(8,128)(2,1)S(1)} %get-tuple-element.42), channel_id=1, source_target_pairs={{0,16},{1,17},{2,18},{3,19},{4,20},{5,21},{6,22},{7,23},{8,9},{9,8... | collective-permute-start | bytes 1572872 | tf_op jit(solution)/shard_map/ppermute | solution.py:268
  13.1 1.1 %shard_map.71 = bf16[8,256,128]{2,1,0:T(8,128)(2,1)S(1)} custom-call(s32[52]{0:T(128)S(1)} %compare_select_fusion.2.meta, bf16[768,512]{1,0:T(8,128)(2,1)S(1)} %get-tuple-element.39.grads, bf16[256,4096]{1,0:T(8,128)(2,1)S(1)} %get-tuple-element.36.x0, bf16[256,4096]{1,0:T(8,128)(2,1)S(1)} %collective-permute-done.3.x1), custom_call_target="tpu_custom_call" | custom-call | tf_op jit(solution)/shard_map/pallas_call | solution.py:334
  14.2 1.1 %shard_map.72 = bf16[8,256,128]{2,1,0:T(8,128)(2,1)S(1)} custom-call(s32[52]{0:T(128)S(1)} %compare_select_fusion.2.meta, bf16[768,512]{1,0:T(8,128)(2,1)S(1)} %get-tuple-element.39.grads, bf16[256,4096]{1,0:T(8,128)(2,1)S(1)} %get-tuple-element.36.x0, bf16[256,4096]{1,0:T(8,128)(2,1)S(1)} %collective-permute-done.3.x1), custom_call_target="tpu_custom_call" | custom-call | tf_op jit(solution)/shard_map/pallas_call | solution.py:334
  15.3 0.2 collective-permute-start.7
  15.5 2.0 %collective-permute-start.6 = (bf16[8,256,128]{2,1,0:T(8,128)(2,1)S(1)}, bf16[8,256,128]{2,1,0:T(8,128)(2,1)S(1)}, u32[]{:S(2)}, u32[]{:S(2)}) collective-permute-start(bf16[8,256,128]{2,1,0:T(8,128)(2,1)S(1)} %shard_map.71), channel_id=1, source_target_pairs={{0,2},{1,3},{2,0},{3,1},{4,6},{5,7},{6,4},{7,5},{8,10},{9,11},{10,... | collective-permute-start | bytes 1572872 | tf_op jit(solution)/shard_map/ppermute | solution.py:268
  17.5 2.5 %shard_map.73 = (bf16[8,256,128]{2,1,0:T(8,128)(2,1)S(1)}, bf16[8,256,128]{2,1,0:T(8,128)(2,1)S(1)}, bf16[8,256,128]{2,1,0:T(8,128)(2,1)S(1)}, bf16[256,768]{1,0:T(8,128)(2,1)}) custom-call(s32[52]{0:T(128)S(1)} %compare_select_fusion.2.meta, bf16[768,512]{1,0:T(8,128)(2,1)S(1)} %get-tuple-element.39.grads, bf16[256,4096]{1,0:T(8,128)(2,1)S(1)} %get-tuple-element.36.x0, ...), custom_call_target="tpu_custom_call" | custom-call | tf_op jit(solution)/shard_map/pallas_call | solution.py:342
  20.0 0.4 collective-permute-done.4
  20.3 0.1 convert_add_fusion.2
  20.5 2.0 %collective-permute-start.5 = (bf16[4,256,128]{2,1,0:T(8,128)(2,1)S(1)}, bf16[4,256,128]{2,1,0:T(8,128)(2,1)S(1)}, u32[]{:S(2)}, u32[]{:S(2)}) collective-permute-start(bf16[4,256,128]{2,1,0:T(8,128)(2,1)S(1)} %slice.116), channel_id=1, source_target_pairs={{0,1},{1,0},{2,3},{3,2},{4,5},{5,4},{6,7},{7,6},{8,10},{9,11},{10,... | collective-permute-start | bytes 786440 | tf_op jit(solution)/shard_map/ppermute | solution.py:268
  22.5 3.4 %collective-permute-done.7 = bf16[8,256,128]{2,1,0:T(8,128)(2,1)S(1)} collective-permute-done((bf16[8,256,128]{2,1,0:T(8,128)(2,1)S(1)}, bf16[8,256,128]{2,1,0:T(8,128)(2,1)S(1)}, u32[]{:S(2)}, u32[]{:S(2)}) %collective-permute-start.7) | collective-permute-done | bytes 524320 | tf_op jit(solution)/shard_map/ppermute | solution.py:268
  26.0 0.1 convert_add_fusion.1
  26.1 2.0 %collective-permute-start.10 = (bf16[4,256,128]{2,1,0:T(8,128)(2,1)S(1)}, bf16[4,256,128]{2,1,0:T(8,128)(2,1)S(1)}, u32[]{:S(2)}, u32[]{:S(2)}) collective-permute-start(bf16[4,256,128]{2,1,0:T(8,128)(2,1)S(1)} %slice.115), channel_id=1, source_target_pairs={{0,1},{1,0},{2,3},{3,2},{4,5},{5,4},{6,7},{7,6},{8,24},{9,25},{10,... | collective-permute-start | bytes 786440 | tf_op jit(solution)/shard_map/ppermute | solution.py:268
  28.1 2.1 %collective-permute-done.6 = bf16[8,256,128]{2,1,0:T(8,128)(2,1)S(1)} collective-permute-done((bf16[8,256,128]{2,1,0:T(8,128)(2,1)S(1)}, bf16[8,256,128]{2,1,0:T(8,128)(2,1)S(1)}, u32[]{:S(2)}, u32[]{:S(2)}) %collective-permute-start.6) | collective-permute-done | bytes 524320 | tf_op jit(solution)/shard_map/ppermute | solution.py:268
  30.3 0.1 convert_add_fusion
  30.4 2.1 %collective-permute-start.9 = (bf16[4,256,128]{2,1,0:T(8,128)(2,1)S(1)}, bf16[4,256,128]{2,1,0:T(8,128)(2,1)S(1)}, u32[]{:S(2)}, u32[]{:S(2)}) collective-permute-start(bf16[4,256,128]{2,1,0:T(8,128)(2,1)S(1)} %slice.114), channel_id=1, source_target_pairs={{0,1},{1,0},{2,3},{3,2},{4,5},{5,4},{6,7},{7,6},{8,24},{9,25},{10,... | collective-permute-start | bytes 786440 | tf_op jit(solution)/shard_map/ppermute | solution.py:268
  32.5 0.0 collective-permute-done.5
  32.6 1.6 %collective-permute-start.8 = (bf16[2,256,128]{2,1,0:T(8,128)(2,1)S(1)}, bf16[2,256,128]{2,1,0:T(8,128)(2,1)S(1)}, u32[]{:S(2)}, u32[]{:S(2)}) collective-permute-start(bf16[2,256,128]{2,1,0:T(8,128)(2,1)S(1)} %slice.119), channel_id=1, source_target_pairs={{0,2},{1,3},{2,0},{3,1},{4,6},{5,7},{6,4},{7,5},{8,24},{9,25},{10,... | collective-permute-start | bytes 393224 | tf_op jit(solution)/shard_map/ppermute | solution.py:268
  34.2 0.0 collective-permute-done.10
  34.2 0.1 slice_add_fusion
  34.3 0.5 collective-permute-start.12
  34.8 2.0 %collective-permute-done.9 = bf16[4,256,128]{2,1,0:T(8,128)(2,1)S(1)} collective-permute-done((bf16[4,256,128]{2,1,0:T(8,128)(2,1)S(1)}, bf16[4,256,128]{2,1,0:T(8,128)(2,1)S(1)}, u32[]{:S(2)}, u32[]{:S(2)}) %collective-permute-start.9) | collective-permute-done | bytes 262176 | tf_op jit(solution)/shard_map/ppermute | solution.py:268
  36.9 0.1 slice_add_fusion.1
  37.0 2.0 %collective-permute-start.13 = (bf16[2,256,128]{2,1,0:T(8,128)(2,1)S(1)}, bf16[2,256,128]{2,1,0:T(8,128)(2,1)S(1)}, u32[]{:S(2)}, u32[]{:S(2)}) collective-permute-start(bf16[2,256,128]{2,1,0:T(8,128)(2,1)S(1)} %slice.117), channel_id=1, source_target_pairs={{0,16},{1,17},{2,18},{3,19},{4,20},{5,21},{6,22},{7,23},{8,9},{9,8... | collective-permute-start | bytes 393224 | tf_op jit(solution)/shard_map/ppermute | solution.py:268
  39.0 0.0 collective-permute-done.8
  39.0 2.7 %collective-permute-start.11 = (bf16[1,256,128]{2,1,0:T(8,128)(2,1)S(1)}, bf16[1,256,128]{2,1,0:T(8,128)(2,1)S(1)}, u32[]{:S(2)}, u32[]{:S(2)}) collective-permute-start(bf16[1,256,128]{2,1,0:T(8,128)(2,1)S(1)} %slice.122), channel_id=1, source_target_pairs={{0,4},{1,5},{2,6},{3,7},{4,0},{5,1},{6,2},{7,3},{8,12},{9,13},{10,... | collective-permute-start | bytes 196616 | tf_op jit(solution)/shard_map/ppermute | solution.py:268
  41.7 0.3 collective-permute-done.13
  42.0 0.0 collective-permute-done.12
  42.1 3.1 %collective-permute-start.17 = (bf16[1,256,128]{2,1,0:T(8,128)(2,1)S(1)}, bf16[1,256,128]{2,1,0:T(8,128)(2,1)S(1)}, u32[]{:S(2)}, u32[]{:S(2)}) collective-permute-start(bf16[1,256,128]{2,1,0:T(8,128)(2,1)S(1)} %slice.120), channel_id=1, source_target_pairs={{0,4},{1,5},{2,6},{3,7},{4,0},{5,1},{6,2},{7,3},{8,12},{9,13},{10,... | collective-permute-start | bytes 196616 | tf_op jit(solution)/shard_map/ppermute | solution.py:268
  45.2 0.1 collective-permute-start.21
  45.3 0.8 %collective-permute-done.11.here = bf16[1,256,128]{2,1,0:T(8,128)(2,1)S(1)} collective-permute-done((bf16[1,256,128]{2,1,0:T(8,128)(2,1)S(1)}, bf16[1,256,128]{2,1,0:T(8,128)(2,1)S(1)}, u32[]{:S(2)}, u32[]{:S(2)}) %collective-permute-start.11) | collective-permute-done | bytes 65568 | tf_op jit(solution)/shard_map/ppermute | solution.py:268
  46.1 0.1 shard_map.74.refs_0_
  46.2 1.1 %collective-permute-start.14 = (bf16[128,256]{1,0:T(8,128)(2,1)S(1)}, bf16[128,256]{1,0:T(8,128)(2,1)S(1)}, u32[]{:S(2)}, u32[]{:S(2)}) collective-permute-start(bf16[128,256]{1,0:T(8,128)(2,1)S(1)} %shard_map.74.refs_0_), channel_id=1, source_target_pairs={{0,16},{1,17},{2,18},{3,19},{4,20},{5,21},{6,22},{7,23},{8,24},{9,... | collective-permute-start | bytes 196616 | tf_op jit(solution)/shard_map/ppermute | solution.py:268
  47.3 0.7 %collective-permute-done.17.here = bf16[1,256,128]{2,1,0:T(8,128)(2,1)S(1)} collective-permute-done((bf16[1,256,128]{2,1,0:T(8,128)(2,1)S(1)}, bf16[1,256,128]{2,1,0:T(8,128)(2,1)S(1)}, u32[]{:S(2)}, u32[]{:S(2)}) %collective-permute-start.17) | collective-permute-done | bytes 65568 | tf_op jit(solution)/shard_map/ppermute | solution.py:268
  48.0 0.1 shard_map.75.refs_4_
  48.1 0.1 collective-permute-start.19
  48.2 1.5 %collective-permute-start.18 = (bf16[128,256]{1,0:T(8,128)(2,1)S(1)}, bf16[128,256]{1,0:T(8,128)(2,1)S(1)}, u32[]{:S(2)}, u32[]{:S(2)}) collective-permute-start(bf16[128,256]{1,0:T(8,128)(2,1)S(1)} %shard_map.75.refs_4_), channel_id=1, source_target_pairs={{0,16},{1,17},{2,18},{3,19},{4,20},{5,21},{6,22},{7,23},{8,24},{9,... | collective-permute-start | bytes 196616 | tf_op jit(solution)/shard_map/ppermute | solution.py:268
  49.7 0.8 %collective-permute-done.21.here = bf16[1,256,128]{2,1,0:T(8,128)(2,1)S(1)} collective-permute-done((bf16[1,256,128]{2,1,0:T(8,128)(2,1)S(1)}, bf16[1,256,128]{2,1,0:T(8,128)(2,1)S(1)}, u32[]{:S(2)}, u32[]{:S(2)}) %collective-permute-start.21) | collective-permute-done | bytes 65568 | tf_op jit(solution)/shard_map/ppermute | solution.py:268
  50.5 0.1 collective-permute-done.14.refs_1_
  50.6 0.1 shard_map.76.refs_8_
  50.7 1.5 %collective-permute-start.22 = (bf16[128,256]{1,0:T(8,128)(2,1)S(1)}, bf16[128,256]{1,0:T(8,128)(2,1)S(1)}, u32[]{:S(2)}, u32[]{:S(2)}) collective-permute-start(bf16[128,256]{1,0:T(8,128)(2,1)S(1)} %shard_map.76.refs_8_), channel_id=1, source_target_pairs={{0,16},{1,17},{2,18},{3,19},{4,20},{5,21},{6,22},{7,23},{8,24},{9,... | collective-permute-start | bytes 196616 | tf_op jit(solution)/shard_map/ppermute | solution.py:268
  52.2 0.0 collective-permute-start.15
  52.2 0.5 collective-permute-start.23
  52.7 0.2 collective-permute-done.18.refs_5_
  52.9 0.0 collective-permute-start.20
  52.9 0.0 collective-permute-done.19.refs_6_
  52.9 0.5 collective-permute-start.16
  53.4 1.6 %collective-permute-done.22.refs_9_ = bf16[128,256]{1,0:T(8,128)(2,1)S(1)} collective-permute-done((bf16[128,256]{1,0:T(8,128)(2,1)S(1)}, bf16[128,256]{1,0:T(8,128)(2,1)S(1)}, u32[]{:S(2)}, u32[]{:S(2)}) %collective-permute-start.22) | collective-permute-done | bytes 65568 | tf_op jit(solution)/shard_map/ppermute | solution.py:268
  55.0 0.0 collective-permute-start.24
  55.0 0.0 collective-permute-done.15.refs_2_
  55.0 0.0 collective-permute-done.20.refs_7_
  55.0 0.0 collective-permute-done.16.refs_3_
  55.0 1.2 %collective-permute-done.24.refs_11_ = bf16[128,256]{1,0:T(8,128)(2,1)S(1)} collective-permute-done((bf16[128,256]{1,0:T(8,128)(2,1)S(1)}, bf16[128,256]{1,0:T(8,128)(2,1)S(1)}, u32[]{:S(2)}, u32[]{:S(2)}) %collective-permute-start.24) | collective-permute-done | bytes 65568 | tf_op jit(solution)/shard_map/ppermute | solution.py:268
  56.3 1.8 %shard_map.77 = f32[512,768]{1,0:T(8,128)} custom-call(s32[52]{0:T(128)S(1)} %compare_select_fusion.2.meta, bf16[128,256]{1,0:T(8,128)(2,1)S(1)} %shard_map.74.refs_0_, bf16[128,256]{1,0:T(8,128)(2,1)S(1)} %collective-permute-done.14.refs_1_, bf16[128,256]{1,0:T(8,128)(2,1)S(1)} %collective-permute-done.15.refs_2_, ...), custom_call_target="tpu_custom_call" | custom-call | tf_op jit(solution)/shard_map/pallas_call | solution.py:224
  (18 shorter events, 0.4 us)
Async XLA Ops:
  0.6 9.1 %collective-permute-start.3 = (bf16[256,4096]{1,0:T(8,128)(2,1)}, bf16[256,4096]{1,0:T(8,128)(2,1)S(1)}, u32[]{:S(2)}, u32[]{:S(2)}) collective-permute-start(bf16[256,4096]{1,0:T(8,128)(2,1)} %bitcast.6), channel_id=1, source_target_pairs={{0,8},{1,9},{2,10},{3,11},{4,12},{5,13},{6,14},{7,15},{8,0},{9,1},... | collective-permute-start | bytes 6291464 | tf_op jit(solution)/shard_map/ppermute | solution.py:268
  3.1 3.1 %collective-permute-start = (bf16[4,256,256]{2,1,0:T(8,128)(2,1)S(1)}, bf16[4,256,256]{2,1,0:T(8,128)(2,1)S(1)}, u32[]{:S(2)}, u32[]{:S(2)}) collective-permute-start(bf16[4,256,256]{2,1,0:T(8,128)(2,1)S(1)} %get-tuple-element.30.mine), channel_id=1, source_target_pairs={{0,8},{1,9},{2,10},{3,11},{4,12},{5,13},{6,14},{7,15},{8,0},{9,1},... | collective-permute-start | bytes 1572872 | tf_op jit(solution)/shard_map/ppermute | solution.py:268
  3.2 5.3 %collective-permute-start.1 = (bf16[2,128,128]{2,1,0:T(8,128)(2,1)S(1)}, bf16[2,128,128]{2,1,0:T(8,128)(2,1)S(1)}, u32[]{:S(2)}, u32[]{:S(2)}) collective-permute-start(bf16[2,128,128]{2,1,0:T(8,128)(2,1)S(1)} %get-tuple-element.34), channel_id=1, source_target_pairs={{0,16},{1,17},{2,18},{3,19},{4,20},{5,21},{6,22},{7,23},{8,24},{9,... | collective-permute-start | bytes 196616 | tf_op jit(solution)/shard_map/ppermute | solution.py:268
  8.5 1.3 %collective-permute-start.2 = (bf16[2,128,128]{2,1,0:T(8,128)(2,1)S(1)}, bf16[2,128,128]{2,1,0:T(8,128)(2,1)S(1)}, u32[]{:S(2)}, u32[]{:S(2)}) collective-permute-start(bf16[2,128,128]{2,1,0:T(8,128)(2,1)S(1)} %collective-permute-done.1.near), channel_id=1, source_target_pairs={{0,8},{1,9},{2,10},{3,11},{4,12},{5,13},{6,14},{7,15},{8,0},{9,1},... | collective-permute-start | bytes 196616 | tf_op jit(solution)/shard_map/ppermute | solution.py:268
  11.1 9.2 %collective-permute-start.4 = (bf16[8,256,128]{2,1,0:T(8,128)(2,1)S(1)}, bf16[8,256,128]{2,1,0:T(8,128)(2,1)S(1)}, u32[]{:S(2)}, u32[]{:S(2)}) collective-permute-start(bf16[8,256,128]{2,1,0:T(8,128)(2,1)S(1)} %get-tuple-element.42), channel_id=1, source_target_pairs={{0,16},{1,17},{2,18},{3,19},{4,20},{5,21},{6,22},{7,23},{8,9},{9,8... | collective-permute-start | bytes 1572872 | tf_op jit(solution)/shard_map/ppermute | solution.py:268
  15.3 10.7 %collective-permute-start.7 = (bf16[8,256,128]{2,1,0:T(8,128)(2,1)S(1)}, bf16[8,256,128]{2,1,0:T(8,128)(2,1)S(1)}, u32[]{:S(2)}, u32[]{:S(2)}) collective-permute-start(bf16[8,256,128]{2,1,0:T(8,128)(2,1)S(1)} %shard_map.72), channel_id=1, source_target_pairs={{0,16},{1,17},{2,18},{3,19},{4,20},{5,21},{6,22},{7,23},{8,9},{9,8... | collective-permute-start | bytes 1572872 | tf_op jit(solution)/shard_map/ppermute | solution.py:268
  15.5 14.8 %collective-permute-start.6 = (bf16[8,256,128]{2,1,0:T(8,128)(2,1)S(1)}, bf16[8,256,128]{2,1,0:T(8,128)(2,1)S(1)}, u32[]{:S(2)}, u32[]{:S(2)}) collective-permute-start(bf16[8,256,128]{2,1,0:T(8,128)(2,1)S(1)} %shard_map.71), channel_id=1, source_target_pairs={{0,2},{1,3},{2,0},{3,1},{4,6},{5,7},{6,4},{7,5},{8,10},{9,11},{10,... | collective-permute-start | bytes 1572872 | tf_op jit(solution)/shard_map/ppermute | solution.py:268
  20.5 12.0 %collective-permute-start.5 = (bf16[4,256,128]{2,1,0:T(8,128)(2,1)S(1)}, bf16[4,256,128]{2,1,0:T(8,128)(2,1)S(1)}, u32[]{:S(2)}, u32[]{:S(2)}) collective-permute-start(bf16[4,256,128]{2,1,0:T(8,128)(2,1)S(1)} %slice.116), channel_id=1, source_target_pairs={{0,1},{1,0},{2,3},{3,2},{4,5},{5,4},{6,7},{7,6},{8,10},{9,11},{10,... | collective-permute-start | bytes 786440 | tf_op jit(solution)/shard_map/ppermute | solution.py:268
  26.1 8.1 %collective-permute-start.10 = (bf16[4,256,128]{2,1,0:T(8,128)(2,1)S(1)}, bf16[4,256,128]{2,1,0:T(8,128)(2,1)S(1)}, u32[]{:S(2)}, u32[]{:S(2)}) collective-permute-start(bf16[4,256,128]{2,1,0:T(8,128)(2,1)S(1)} %slice.115), channel_id=1, source_target_pairs={{0,1},{1,0},{2,3},{3,2},{4,5},{5,4},{6,7},{7,6},{8,24},{9,25},{10,... | collective-permute-start | bytes 786440 | tf_op jit(solution)/shard_map/ppermute | solution.py:268
  30.4 6.4 %collective-permute-start.9 = (bf16[4,256,128]{2,1,0:T(8,128)(2,1)S(1)}, bf16[4,256,128]{2,1,0:T(8,128)(2,1)S(1)}, u32[]{:S(2)}, u32[]{:S(2)}) collective-permute-start(bf16[4,256,128]{2,1,0:T(8,128)(2,1)S(1)} %slice.114), channel_id=1, source_target_pairs={{0,1},{1,0},{2,3},{3,2},{4,5},{5,4},{6,7},{7,6},{8,24},{9,25},{10,... | collective-permute-start | bytes 786440 | tf_op jit(solution)/shard_map/ppermute | solution.py:268
  32.6 6.4 %collective-permute-start.8 = (bf16[2,256,128]{2,1,0:T(8,128)(2,1)S(1)}, bf16[2,256,128]{2,1,0:T(8,128)(2,1)S(1)}, u32[]{:S(2)}, u32[]{:S(2)}) collective-permute-start(bf16[2,256,128]{2,1,0:T(8,128)(2,1)S(1)} %slice.119), channel_id=1, source_target_pairs={{0,2},{1,3},{2,0},{3,1},{4,6},{5,7},{6,4},{7,5},{8,24},{9,25},{10,... | collective-permute-start | bytes 393224 | tf_op jit(solution)/shard_map/ppermute | solution.py:268
  34.3 7.7 %collective-permute-start.12 = (bf16[2,256,128]{2,1,0:T(8,128)(2,1)S(1)}, bf16[2,256,128]{2,1,0:T(8,128)(2,1)S(1)}, u32[]{:S(2)}, u32[]{:S(2)}) collective-permute-start(bf16[2,256,128]{2,1,0:T(8,128)(2,1)S(1)} %slice.118), channel_id=1, source_target_pairs={{0,2},{1,3},{2,0},{3,1},{4,6},{5,7},{6,4},{7,5},{8,10},{9,11},{10,... | collective-permute-start | bytes 393224 | tf_op jit(solution)/shard_map/ppermute | solution.py:268
  37.0 5.0 %collective-permute-start.13 = (bf16[2,256,128]{2,1,0:T(8,128)(2,1)S(1)}, bf16[2,256,128]{2,1,0:T(8,128)(2,1)S(1)}, u32[]{:S(2)}, u32[]{:S(2)}) collective-permute-start(bf16[2,256,128]{2,1,0:T(8,128)(2,1)S(1)} %slice.117), channel_id=1, source_target_pairs={{0,16},{1,17},{2,18},{3,19},{4,20},{5,21},{6,22},{7,23},{8,9},{9,8... | collective-permute-start | bytes 393224 | tf_op jit(solution)/shard_map/ppermute | solution.py:268
  39.0 7.1 %collective-permute-start.11 = (bf16[1,256,128]{2,1,0:T(8,128)(2,1)S(1)}, bf16[1,256,128]{2,1,0:T(8,128)(2,1)S(1)}, u32[]{:S(2)}, u32[]{:S(2)}) collective-permute-start(bf16[1,256,128]{2,1,0:T(8,128)(2,1)S(1)} %slice.122), channel_id=1, source_target_pairs={{0,4},{1,5},{2,6},{3,7},{4,0},{5,1},{6,2},{7,3},{8,12},{9,13},{10,... | collective-permute-start | bytes 196616 | tf_op jit(solution)/shard_map/ppermute | solution.py:268
  42.1 5.9 %collective-permute-start.17 = (bf16[1,256,128]{2,1,0:T(8,128)(2,1)S(1)}, bf16[1,256,128]{2,1,0:T(8,128)(2,1)S(1)}, u32[]{:S(2)}, u32[]{:S(2)}) collective-permute-start(bf16[1,256,128]{2,1,0:T(8,128)(2,1)S(1)} %slice.120), channel_id=1, source_target_pairs={{0,4},{1,5},{2,6},{3,7},{4,0},{5,1},{6,2},{7,3},{8,12},{9,13},{10,... | collective-permute-start | bytes 196616 | tf_op jit(solution)/shard_map/ppermute | solution.py:268
  45.2 5.2 %collective-permute-start.21 = (bf16[1,256,128]{2,1,0:T(8,128)(2,1)S(1)}, bf16[1,256,128]{2,1,0:T(8,128)(2,1)S(1)}, u32[]{:S(2)}, u32[]{:S(2)}) collective-permute-start(bf16[1,256,128]{2,1,0:T(8,128)(2,1)S(1)} %slice.121), channel_id=1, source_target_pairs={{0,4},{1,5},{2,6},{3,7},{4,0},{5,1},{6,2},{7,3},{8,12},{9,13},{10,... | collective-permute-start | bytes 196616 | tf_op jit(solution)/shard_map/ppermute | solution.py:268
  46.2 4.3 %collective-permute-start.14 = (bf16[128,256]{1,0:T(8,128)(2,1)S(1)}, bf16[128,256]{1,0:T(8,128)(2,1)S(1)}, u32[]{:S(2)}, u32[]{:S(2)}) collective-permute-start(bf16[128,256]{1,0:T(8,128)(2,1)S(1)} %shard_map.74.refs_0_), channel_id=1, source_target_pairs={{0,16},{1,17},{2,18},{3,19},{4,20},{5,21},{6,22},{7,23},{8,24},{9,... | collective-permute-start | bytes 196616 | tf_op jit(solution)/shard_map/ppermute | solution.py:268
  48.1 4.7 %collective-permute-start.19 = (bf16[128,256]{1,0:T(8,128)(2,1)S(1)}, bf16[128,256]{1,0:T(8,128)(2,1)S(1)}, u32[]{:S(2)}, u32[]{:S(2)}) collective-permute-start(bf16[128,256]{1,0:T(8,128)(2,1)S(1)} %shard_map.75.refs_4_), channel_id=1, source_target_pairs={{0,8},{1,9},{2,10},{3,11},{4,12},{5,13},{6,14},{7,15},{8,0},{9,1},... | collective-permute-start | bytes 196616 | tf_op jit(solution)/shard_map/ppermute | solution.py:268
  48.2 4.6 %collective-permute-start.18 = (bf16[128,256]{1,0:T(8,128)(2,1)S(1)}, bf16[128,256]{1,0:T(8,128)(2,1)S(1)}, u32[]{:S(2)}, u32[]{:S(2)}) collective-permute-start(bf16[128,256]{1,0:T(8,128)(2,1)S(1)} %shard_map.75.refs_4_), channel_id=1, source_target_pairs={{0,16},{1,17},{2,18},{3,19},{4,20},{5,21},{6,22},{7,23},{8,24},{9,... | collective-permute-start | bytes 196616 | tf_op jit(solution)/shard_map/ppermute | solution.py:268
  50.7 4.3 %collective-permute-start.22 = (bf16[128,256]{1,0:T(8,128)(2,1)S(1)}, bf16[128,256]{1,0:T(8,128)(2,1)S(1)}, u32[]{:S(2)}, u32[]{:S(2)}) collective-permute-start(bf16[128,256]{1,0:T(8,128)(2,1)S(1)} %shard_map.76.refs_8_), channel_id=1, source_target_pairs={{0,16},{1,17},{2,18},{3,19},{4,20},{5,21},{6,22},{7,23},{8,24},{9,... | collective-permute-start | bytes 196616 | tf_op jit(solution)/shard_map/ppermute | solution.py:268
  52.2 2.8 %collective-permute-start.15 = (bf16[128,256]{1,0:T(8,128)(2,1)S(1)}, bf16[128,256]{1,0:T(8,128)(2,1)S(1)}, u32[]{:S(2)}, u32[]{:S(2)}) collective-permute-start(bf16[128,256]{1,0:T(8,128)(2,1)S(1)} %shard_map.74.refs_0_), channel_id=1, source_target_pairs={{0,8},{1,9},{2,10},{3,11},{4,12},{5,13},{6,14},{7,15},{8,0},{9,1},... | collective-permute-start | bytes 196616 | tf_op jit(solution)/shard_map/ppermute | solution.py:268
  52.2 2.9 %collective-permute-start.23 = (bf16[128,256]{1,0:T(8,128)(2,1)S(1)}, bf16[128,256]{1,0:T(8,128)(2,1)S(1)}, u32[]{:S(2)}, u32[]{:S(2)}) collective-permute-start(bf16[128,256]{1,0:T(8,128)(2,1)S(1)} %shard_map.76.refs_8_), channel_id=1, source_target_pairs={{0,8},{1,9},{2,10},{3,11},{4,12},{5,13},{6,14},{7,15},{8,0},{9,1},... | collective-permute-start | bytes 196616 | tf_op jit(solution)/shard_map/ppermute | solution.py:268
  52.9 2.2 %collective-permute-start.20 = (bf16[128,256]{1,0:T(8,128)(2,1)S(1)}, bf16[128,256]{1,0:T(8,128)(2,1)S(1)}, u32[]{:S(2)}, u32[]{:S(2)}) collective-permute-start(bf16[128,256]{1,0:T(8,128)(2,1)S(1)} %collective-permute-done.18.refs_5_), channel_id=1, source_target_pairs={{0,8},{1,9},{2,10},{3,11},{4,12},{5,13},{6,14},{7,15},{8,0},{9,1},... | collective-permute-start | bytes 196616 | tf_op jit(solution)/shard_map/ppermute | solution.py:268
  52.9 2.2 %collective-permute-start.16 = (bf16[128,256]{1,0:T(8,128)(2,1)S(1)}, bf16[128,256]{1,0:T(8,128)(2,1)S(1)}, u32[]{:S(2)}, u32[]{:S(2)}) collective-permute-start(bf16[128,256]{1,0:T(8,128)(2,1)S(1)} %collective-permute-done.14.refs_1_), channel_id=1, source_target_pairs={{0,8},{1,9},{2,10},{3,11},{4,12},{5,13},{6,14},{7,15},{8,0},{9,1},... | collective-permute-start | bytes 196616 | tf_op jit(solution)/shard_map/ppermute | solution.py:268
  55.0 1.3 %collective-permute-start.24 = (bf16[128,256]{1,0:T(8,128)(2,1)S(1)}, bf16[128,256]{1,0:T(8,128)(2,1)S(1)}, u32[]{:S(2)}, u32[]{:S(2)}) collective-permute-start(bf16[128,256]{1,0:T(8,128)(2,1)S(1)} %collective-permute-done.22.refs_9_), channel_id=1, source_target_pairs={{0,8},{1,9},{2,10},{3,11},{4,12},{5,13},{6,14},{7,15},{8,0},{9,1},... | collective-permute-start | bytes 196616 | tf_op jit(solution)/shard_map/ppermute | solution.py:268

commit v9 on v8

--- a/solution.py
+++ b/solution.py
@@ -371,8 +371,8 @@
         )
     parts = {}
     parts[0] = finish(kept[0], after(here[0], latest))
-    parts[1] = finish(kept[1], after(here[1], parts[0][0]))
-    parts[2] = finish(kept[2], after(here[2], parts[1][0], parts[0][1]))
+    parts[2] = finish(kept[2], after(here[2], parts[0][0]))
+    parts[1] = finish(kept[1], after(here[1], parts[2][0], parts[0][1]))
     shape = (seq_count * rows, 3 * width)
     weight_grad = place(meta, parts[0] + parts[1] + parts[2], 0, shape)
     return (own[None], weight_grad)

time: 58.2 us -> 58.1 us (level)
  no operation moved by 1% of the time
where the time goes in v9:
time: 58.1 us; the launch traced here: 58 us
  starting transfers between devices  29.2 us (50%)
  waiting for transfers between devices  15.5 us (27%)
  Pallas kernels  11.6 us (20%)
  between operations  0.87 us (1%)
    ppermute x25, starting transfers between devices, on_device(): lax.ppermute(value, AXES, partners(core0, core1, seq_count, dp_count))  29.2 us
    ppermute x25, waiting for transfers between devices, on_device(): lax.ppermute(value, AXES, partners(core0, core1, seq_count, dp_count))  15.5 us
    pallas_call x1, Pallas kernels, on_device(): pl.pallas_call(keep_kernel, in_specs=[smem()] + [vmem()] * 3, out_specs=[...  2.49 us
    pallas_call x2, Pallas kernels, on_device(): pl.pallas_call(functools.partial(other_kernel, part=part), in_specs=[smem...  2.2 us
    pallas_call x1, Pallas kernels, on_device(): pl.pallas_call(state_kernel, in_specs=[smem()] + [hbm()] * 4, out_specs=[...  1.9 us
    pallas_call x1, Pallas kernels, place(): pl.pallas_call(functools.partial(place_kernel, parts=parts, first=first),...  1.78 us
    pallas_call x1, Pallas kernels, on_device(): pl.pallas_call(local_kernel, in_specs=[hbm()] + [vmem()] * 2, out_specs=[...  1.6 us
    pallas_call x1, Pallas kernels, on_device(): pl.pallas_call(functools.partial(first_kernel, scale=scale), in_specs=[sm...  1.34 us
  transfers between devices with their start and end apart: 25, of which 14 were waited for; matrix products, arithmetic and copies ran while one was open for 1% of the time, Pallas kernels for 15%

profile of v9, /device:TPU:0, one launch (start us, length us, event | category | flops | bytes accessed | tf_op | source)
XLA Modules:
  0.0 58.0 jit_solution(4787323708085689921)
XLA Ops:
  0.6 0.5 collective-permute-start.3
  1.2 1.9 %shard_map.68 = (bf16[2,128,128]{2,1,0:T(8,128)(2,1)S(1)}, bf16[4,256,256]{2,1,0:T(8,128)(2,1)S(1)}) custom-call(s32[52]{0:T(128)S(1)} %compare_select_fusion.2.meta, bf16[256,256]{1,0:T(8,128)(2,1)} %bitcast.8, bf16[256,256]{1,0:T(8,128)(2,1)} %bitcast.9, bf16[256,256]{1,0:T(8,128)(2,1)} %bitcast.10, bf16[256,256]{1,0:T(8,128)(2,1)} %bitcast.11), custom_call_target="tpu_custom_call" | custom-call | tf_op jit(solution)/shard_map/pallas_call | solution.py:294
  3.1 0.1 collective-permute-start
  3.2 2.9 %collective-permute-start.1 = (bf16[2,128,128]{2,1,0:T(8,128)(2,1)S(1)}, bf16[2,128,128]{2,1,0:T(8,128)(2,1)S(1)}, u32[]{:S(2)}, u32[]{:S(2)}) collective-permute-start(bf16[2,128,128]{2,1,0:T(8,128)(2,1)S(1)} %get-tuple-element.34), channel_id=1, source_target_pairs={{0,16},{1,17},{2,18},{3,19},{4,20},{5,21},{6,22},{7,23},{8,24},{9,... | collective-permute-start | bytes 196616 | tf_op jit(solution)/shard_map/ppermute | solution.py:268
  6.1 0.0 collective-permute-done.other
  6.1 1.6 %shard_map.69 = (f32[2,3,256,256]{3,2,1,0:T(8,128)S(1)}, bf16[2,3,2,128,256]{4,3,2,1,0:T(8,128)(2,1)S(1)}, bf16[2,2,2,128,128]{4,3,2,1,0:T(8,128)(2,1)S(1)}, bf16[256,4096]{1,0:T(8,128)(2,1)S(1)}) custom-call(bf16[256,4096]{1,0:T(8,128)(2,1)} %bitcast.7, bf16[4,256,256]{2,1,0:T(8,128)(2,1)S(1)} %get-tuple-element.30.mine, ...), custom_call_target="tpu_custom_call" | custom-call | tf_op jit(solution)/shard_map/pallas_call | solution.py:309
  7.8 0.7 %collective-permute-done.1.near = bf16[2,128,128]{2,1,0:T(8,128)(2,1)S(1)} collective-permute-done((bf16[2,128,128]{2,1,0:T(8,128)(2,1)S(1)}, bf16[2,128,128]{2,1,0:T(8,128)(2,1)S(1)}, u32[]{:S(2)}, u32[]{:S(2)}) %collective-permute-start.1) | collective-permute-done | bytes 65568 | tf_op jit(solution)/shard_map/ppermute | solution.py:268
  8.5 0.0 collective-permute-start.2
  8.5 1.3 %collective-permute-done.2.far = bf16[2,128,128]{2,1,0:T(8,128)(2,1)S(1)} collective-permute-done((bf16[2,128,128]{2,1,0:T(8,128)(2,1)S(1)}, bf16[2,128,128]{2,1,0:T(8,128)(2,1)S(1)}, u32[]{:S(2)}, u32[]{:S(2)}) %collective-permute-start.2) | collective-permute-done | bytes 65568 | tf_op jit(solution)/shard_map/ppermute | solution.py:268
  9.7 0.0 collective-permute-done.3.x1
  9.7 1.3 %shard_map.70 = (bf16[768,512]{1,0:T(8,128)(2,1)S(1)}, bf16[8,256,128]{2,1,0:T(8,128)(2,1)S(1)}) custom-call(s32[52]{0:T(128)S(1)} %compare_select_fusion.2.meta, f32[2,3,256,256]{3,2,1,0:T(8,128)S(1)} %get-tuple-element.31.local, bf16[2,3,2,128,256]{4,3,2,1,0:T(8,128)(2,1)S(1)} %get-tuple-element.32.turned, ...), custom_call_target="tpu_custom_call" | custom-call | tf_op jit(solution)/shard_map/pallas_call | solution.py:325
  11.1 2.0 %collective-permute-start.4 = (bf16[8,256,128]{2,1,0:T(8,128)(2,1)S(1)}, bf16[8,256,128]{2,1,0:T(8,128)(2,1)S(1)}, u32[]{:S(2)}, u32[]{:S(2)}) collective-permute-start(bf16[8,256,128]{2,1,0:T(8,128)(2,1)S(1)} %get-tuple-element.42), channel_id=1, source_target_pairs={{0,16},{1,17},{2,18},{3,19},{4,20},{5,21},{6,22},{7,23},{8,9},{9,8... | collective-permute-start | bytes 1572872 | tf_op jit(solution)/shard_map/ppermute | solution.py:268
  13.1 1.1 %shard_map.71 = bf16[8,256,128]{2,1,0:T(8,128)(2,1)S(1)} custom-call(s32[52]{0:T(128)S(1)} %compare_select_fusion.2.meta, bf16[768,512]{1,0:T(8,128)(2,1)S(1)} %get-tuple-element.39.grads, bf16[256,4096]{1,0:T(8,128)(2,1)S(1)} %get-tuple-element.36.x0, bf16[256,4096]{1,0:T(8,128)(2,1)S(1)} %collective-permute-done.3.x1), custom_call_target="tpu_custom_call" | custom-call | tf_op jit(solution)/shard_map/pallas_call | solution.py:334
  14.2 1.1 %shard_map.72 = bf16[8,256,128]{2,1,0:T(8,128)(2,1)S(1)} custom-call(s32[52]{0:T(128)S(1)} %compare_select_fusion.2.meta, bf16[768,512]{1,0:T(8,128)(2,1)S(1)} %get-tuple-element.39.grads, bf16[256,4096]{1,0:T(8,128)(2,1)S(1)} %get-tuple-element.36.x0, bf16[256,4096]{1,0:T(8,128)(2,1)S(1)} %collective-permute-done.3.x1), custom_call_target="tpu_custom_call" | custom-call | tf_op jit(solution)/shard_map/pallas_call | solution.py:334
  15.3 0.2 collective-permute-start.7
  15.5 2.0 %collective-permute-start.6 = (bf16[8,256,128]{2,1,0:T(8,128)(2,1)S(1)}, bf16[8,256,128]{2,1,0:T(8,128)(2,1)S(1)}, u32[]{:S(2)}, u32[]{:S(2)}) collective-permute-start(bf16[8,256,128]{2,1,0:T(8,128)(2,1)S(1)} %shard_map.71), channel_id=1, source_target_pairs={{0,2},{1,3},{2,0},{3,1},{4,6},{5,7},{6,4},{7,5},{8,10},{9,11},{10,... | collective-permute-start | bytes 1572872 | tf_op jit(solution)/shard_map/ppermute | solution.py:268
  17.5 2.5 %shard_map.73 = (bf16[8,256,128]{2,1,0:T(8,128)(2,1)S(1)}, bf16[8,256,128]{2,1,0:T(8,128)(2,1)S(1)}, bf16[8,256,128]{2,1,0:T(8,128)(2,1)S(1)}, bf16[256,768]{1,0:T(8,128)(2,1)}) custom-call(s32[52]{0:T(128)S(1)} %compare_select_fusion.2.meta, bf16[768,512]{1,0:T(8,128)(2,1)S(1)} %get-tuple-element.39.grads, bf16[256,4096]{1,0:T(8,128)(2,1)S(1)} %get-tuple-element.36.x0, ...), custom_call_target="tpu_custom_call" | custom-call | tf_op jit(solution)/shard_map/pallas_call | solution.py:342
  20.0 0.4 collective-permute-done.4
  20.3 0.1 convert_add_fusion.2
  20.5 2.0 %collective-permute-start.5 = (bf16[4,256,128]{2,1,0:T(8,128)(2,1)S(1)}, bf16[4,256,128]{2,1,0:T(8,128)(2,1)S(1)}, u32[]{:S(2)}, u32[]{:S(2)}) collective-permute-start(bf16[4,256,128]{2,1,0:T(8,128)(2,1)S(1)} %slice.116), channel_id=1, source_target_pairs={{0,1},{1,0},{2,3},{3,2},{4,5},{5,4},{6,7},{7,6},{8,10},{9,11},{10,... | collective-permute-start | bytes 786440 | tf_op jit(solution)/shard_map/ppermute | solution.py:268
  22.5 3.4 %collective-permute-done.7 = bf16[8,256,128]{2,1,0:T(8,128)(2,1)S(1)} collective-permute-done((bf16[8,256,128]{2,1,0:T(8,128)(2,1)S(1)}, bf16[8,256,128]{2,1,0:T(8,128)(2,1)S(1)}, u32[]{:S(2)}, u32[]{:S(2)}) %collective-permute-start.7) | collective-permute-done | bytes 524320 | tf_op jit(solution)/shard_map/ppermute | solution.py:268
  26.0 0.1 convert_add_fusion.1
  26.1 2.0 %collective-permute-start.10 = (bf16[4,256,128]{2,1,0:T(8,128)(2,1)S(1)}, bf16[4,256,128]{2,1,0:T(8,128)(2,1)S(1)}, u32[]{:S(2)}, u32[]{:S(2)}) collective-permute-start(bf16[4,256,128]{2,1,0:T(8,128)(2,1)S(1)} %slice.115), channel_id=1, source_target_pairs={{0,1},{1,0},{2,3},{3,2},{4,5},{5,4},{6,7},{7,6},{8,24},{9,25},{10,... | collective-permute-start | bytes 786440 | tf_op jit(solution)/shard_map/ppermute | solution.py:268
  28.1 2.1 %collective-permute-done.6 = bf16[8,256,128]{2,1,0:T(8,128)(2,1)S(1)} collective-permute-done((bf16[8,256,128]{2,1,0:T(8,128)(2,1)S(1)}, bf16[8,256,128]{2,1,0:T(8,128)(2,1)S(1)}, u32[]{:S(2)}, u32[]{:S(2)}) %collective-permute-start.6) | collective-permute-done | bytes 524320 | tf_op jit(solution)/shard_map/ppermute | solution.py:268
  30.3 0.1 convert_add_fusion
  30.4 2.1 %collective-permute-start.9 = (bf16[4,256,128]{2,1,0:T(8,128)(2,1)S(1)}, bf16[4,256,128]{2,1,0:T(8,128)(2,1)S(1)}, u32[]{:S(2)}, u32[]{:S(2)}) collective-permute-start(bf16[4,256,128]{2,1,0:T(8,128)(2,1)S(1)} %slice.114), channel_id=1, source_target_pairs={{0,1},{1,0},{2,3},{3,2},{4,5},{5,4},{6,7},{7,6},{8,24},{9,25},{10,... | collective-permute-start | bytes 786440 | tf_op jit(solution)/shard_map/ppermute | solution.py:268
  32.5 0.0 collective-permute-done.5
  32.6 1.6 %collective-permute-start.8 = (bf16[2,256,128]{2,1,0:T(8,128)(2,1)S(1)}, bf16[2,256,128]{2,1,0:T(8,128)(2,1)S(1)}, u32[]{:S(2)}, u32[]{:S(2)}) collective-permute-start(bf16[2,256,128]{2,1,0:T(8,128)(2,1)S(1)} %slice.119), channel_id=1, source_target_pairs={{0,2},{1,3},{2,0},{3,1},{4,6},{5,7},{6,4},{7,5},{8,24},{9,25},{10,... | collective-permute-start | bytes 393224 | tf_op jit(solution)/shard_map/ppermute | solution.py:268
  34.2 0.0 collective-permute-done.10
  34.2 0.1 slice_add_fusion
  34.3 0.5 collective-permute-start.12
  34.8 2.0 %collective-permute-done.9 = bf16[4,256,128]{2,1,0:T(8,128)(2,1)S(1)} collective-permute-done((bf16[4,256,128]{2,1,0:T(8,128)(2,1)S(1)}, bf16[4,256,128]{2,1,0:T(8,128)(2,1)S(1)}, u32[]{:S(2)}, u32[]{:S(2)}) %collective-permute-start.9) | collective-permute-done | bytes 262176 | tf_op jit(solution)/shard_map/ppermute | solution.py:268
  36.9 0.1 slice_add_fusion.1
  37.0 2.0 %collective-permute-start.13 = (bf16[2,256,128]{2,1,0:T(8,128)(2,1)S(1)}, bf16[2,256,128]{2,1,0:T(8,128)(2,1)S(1)}, u32[]{:S(2)}, u32[]{:S(2)}) collective-permute-start(bf16[2,256,128]{2,1,0:T(8,128)(2,1)S(1)} %slice.117), channel_id=1, source_target_pairs={{0,16},{1,17},{2,18},{3,19},{4,20},{5,21},{6,22},{7,23},{8,9},{9,8... | collective-permute-start | bytes 393224 | tf_op jit(solution)/shard_map/ppermute | solution.py:268
  39.0 0.0 collective-permute-done.8
  39.0 2.7 %collective-permute-start.11 = (bf16[1,256,128]{2,1,0:T(8,128)(2,1)S(1)}, bf16[1,256,128]{2,1,0:T(8,128)(2,1)S(1)}, u32[]{:S(2)}, u32[]{:S(2)}) collective-permute-start(bf16[1,256,128]{2,1,0:T(8,128)(2,1)S(1)} %slice.122), channel_id=1, source_target_pairs={{0,4},{1,5},{2,6},{3,7},{4,0},{5,1},{6,2},{7,3},{8,12},{9,13},{10,... | collective-permute-start | bytes 196616 | tf_op jit(solution)/shard_map/ppermute | solution.py:268
  41.7 0.2 collective-permute-done.13
  42.0 3.1 %collective-permute-start.18 = (bf16[1,256,128]{2,1,0:T(8,128)(2,1)S(1)}, bf16[1,256,128]{2,1,0:T(8,128)(2,1)S(1)}, u32[]{:S(2)}, u32[]{:S(2)}) collective-permute-start(bf16[1,256,128]{2,1,0:T(8,128)(2,1)S(1)} %slice.121), channel_id=1, source_target_pairs={{0,4},{1,5},{2,6},{3,7},{4,0},{5,1},{6,2},{7,3},{8,12},{9,13},{10,... | collective-permute-start | bytes 196616 | tf_op jit(solution)/shard_map/ppermute | solution.py:268
  45.2 0.0 collective-permute-done.12
  45.2 0.1 collective-permute-start.17
  45.3 0.8 %collective-permute-done.11.here = bf16[1,256,128]{2,1,0:T(8,128)(2,1)S(1)} collective-permute-done((bf16[1,256,128]{2,1,0:T(8,128)(2,1)S(1)}, bf16[1,256,128]{2,1,0:T(8,128)(2,1)S(1)}, u32[]{:S(2)}, u32[]{:S(2)}) %collective-permute-start.11) | collective-permute-done | bytes 65568 | tf_op jit(solution)/shard_map/ppermute | solution.py:268
  46.1 0.1 shard_map.74.refs_0_
  46.2 1.1 %collective-permute-start.14 = (bf16[128,256]{1,0:T(8,128)(2,1)S(1)}, bf16[128,256]{1,0:T(8,128)(2,1)S(1)}, u32[]{:S(2)}, u32[]{:S(2)}) collective-permute-start(bf16[128,256]{1,0:T(8,128)(2,1)S(1)} %shard_map.74.refs_0_), channel_id=1, source_target_pairs={{0,16},{1,17},{2,18},{3,19},{4,20},{5,21},{6,22},{7,23},{8,24},{9,... | collective-permute-start | bytes 196616 | tf_op jit(solution)/shard_map/ppermute | solution.py:268
  47.3 0.7 %collective-permute-done.18.here = bf16[1,256,128]{2,1,0:T(8,128)(2,1)S(1)} collective-permute-done((bf16[1,256,128]{2,1,0:T(8,128)(2,1)S(1)}, bf16[1,256,128]{2,1,0:T(8,128)(2,1)S(1)}, u32[]{:S(2)}, u32[]{:S(2)}) %collective-permute-start.18) | collective-permute-done | bytes 65568 | tf_op jit(solution)/shard_map/ppermute | solution.py:268
  48.0 0.1 shard_map.75.refs_8_
  48.1 0.1 collective-permute-start.23
  48.2 1.5 %collective-permute-start.22 = (bf16[128,256]{1,0:T(8,128)(2,1)S(1)}, bf16[128,256]{1,0:T(8,128)(2,1)S(1)}, u32[]{:S(2)}, u32[]{:S(2)}) collective-permute-start(bf16[128,256]{1,0:T(8,128)(2,1)S(1)} %shard_map.75.refs_8_), channel_id=1, source_target_pairs={{0,16},{1,17},{2,18},{3,19},{4,20},{5,21},{6,22},{7,23},{8,24},{9,... | collective-permute-start | bytes 196616 | tf_op jit(solution)/shard_map/ppermute | solution.py:268
  49.7 0.8 %collective-permute-done.17.here = bf16[1,256,128]{2,1,0:T(8,128)(2,1)S(1)} collective-permute-done((bf16[1,256,128]{2,1,0:T(8,128)(2,1)S(1)}, bf16[1,256,128]{2,1,0:T(8,128)(2,1)S(1)}, u32[]{:S(2)}, u32[]{:S(2)}) %collective-permute-start.17) | collective-permute-done | bytes 65568 | tf_op jit(solution)/shard_map/ppermute | solution.py:268
  50.4 0.1 collective-permute-done.14.refs_1_
  50.5 0.1 shard_map.76.refs_4_
  50.6 1.5 %collective-permute-start.19 = (bf16[128,256]{1,0:T(8,128)(2,1)S(1)}, bf16[128,256]{1,0:T(8,128)(2,1)S(1)}, u32[]{:S(2)}, u32[]{:S(2)}) collective-permute-start(bf16[128,256]{1,0:T(8,128)(2,1)S(1)} %shard_map.76.refs_4_), channel_id=1, source_target_pairs={{0,16},{1,17},{2,18},{3,19},{4,20},{5,21},{6,22},{7,23},{8,24},{9,... | collective-permute-start | bytes 196616 | tf_op jit(solution)/shard_map/ppermute | solution.py:268
  52.1 0.0 collective-permute-start.15
  52.1 0.5 collective-permute-start.20
  52.7 0.1 collective-permute-done.22.refs_9_
  52.8 0.0 collective-permute-start.24
  52.8 0.5 collective-permute-start.16
  53.3 1.7 %collective-permute-done.19.refs_5_ = bf16[128,256]{1,0:T(8,128)(2,1)S(1)} collective-permute-done((bf16[128,256]{1,0:T(8,128)(2,1)S(1)}, bf16[128,256]{1,0:T(8,128)(2,1)S(1)}, u32[]{:S(2)}, u32[]{:S(2)}) %collective-permute-start.19) | collective-permute-done | bytes 65568 | tf_op jit(solution)/shard_map/ppermute | solution.py:268
  54.9 0.0 collective-permute-start.21
  54.9 0.0 collective-permute-done.15.refs_2_
  55.0 0.0 collective-permute-done.24.refs_11_
  55.0 0.0 collective-permute-done.20.refs_6_
  55.0 0.0 collective-permute-done.16.refs_3_
  55.0 1.2 %collective-permute-done.21.refs_7_ = bf16[128,256]{1,0:T(8,128)(2,1)S(1)} collective-permute-done((bf16[128,256]{1,0:T(8,128)(2,1)S(1)}, bf16[128,256]{1,0:T(8,128)(2,1)S(1)}, u32[]{:S(2)}, u32[]{:S(2)}) %collective-permute-start.21) | collective-permute-done | bytes 65568 | tf_op jit(solution)/shard_map/ppermute | solution.py:268
  56.2 1.8 %shard_map.77 = f32[512,768]{1,0:T(8,128)} custom-call(s32[52]{0:T(128)S(1)} %compare_select_fusion.2.meta, bf16[128,256]{1,0:T(8,128)(2,1)S(1)} %shard_map.74.refs_0_, bf16[128,256]{1,0:T(8,128)(2,1)S(1)} %collective-permute-done.14.refs_1_, bf16[128,256]{1,0:T(8,128)(2,1)S(1)} %collective-permute-done.15.refs_2_, ...), custom_call_target="tpu_custom_call" | custom-call | tf_op jit(solution)/shard_map/pallas_call | solution.py:224
  (18 shorter events, 0.4 us)
Async XLA Ops:
  0.6 9.1 %collective-permute-start.3 = (bf16[256,4096]{1,0:T(8,128)(2,1)}, bf16[256,4096]{1,0:T(8,128)(2,1)S(1)}, u32[]{:S(2)}, u32[]{:S(2)}) collective-permute-start(bf16[256,4096]{1,0:T(8,128)(2,1)} %bitcast.6), channel_id=1, source_target_pairs={{0,8},{1,9},{2,10},{3,11},{4,12},{5,13},{6,14},{7,15},{8,0},{9,1},... | collective-permute-start | bytes 6291464 | tf_op jit(solution)/shard_map/ppermute | solution.py:268
  3.1 3.1 %collective-permute-start = (bf16[4,256,256]{2,1,0:T(8,128)(2,1)S(1)}, bf16[4,256,256]{2,1,0:T(8,128)(2,1)S(1)}, u32[]{:S(2)}, u32[]{:S(2)}) collective-permute-start(bf16[4,256,256]{2,1,0:T(8,128)(2,1)S(1)} %get-tuple-element.30.mine), channel_id=1, source_target_pairs={{0,8},{1,9},{2,10},{3,11},{4,12},{5,13},{6,14},{7,15},{8,0},{9,1},... | collective-permute-start | bytes 1572872 | tf_op jit(solution)/shard_map/ppermute | solution.py:268
  3.2 5.3 %collective-permute-start.1 = (bf16[2,128,128]{2,1,0:T(8,128)(2,1)S(1)}, bf16[2,128,128]{2,1,0:T(8,128)(2,1)S(1)}, u32[]{:S(2)}, u32[]{:S(2)}) collective-permute-start(bf16[2,128,128]{2,1,0:T(8,128)(2,1)S(1)} %get-tuple-element.34), channel_id=1, source_target_pairs={{0,16},{1,17},{2,18},{3,19},{4,20},{5,21},{6,22},{7,23},{8,24},{9,... | collective-permute-start | bytes 196616 | tf_op jit(solution)/shard_map/ppermute | solution.py:268
  8.5 1.3 %collective-permute-start.2 = (bf16[2,128,128]{2,1,0:T(8,128)(2,1)S(1)}, bf16[2,128,128]{2,1,0:T(8,128)(2,1)S(1)}, u32[]{:S(2)}, u32[]{:S(2)}) collective-permute-start(bf16[2,128,128]{2,1,0:T(8,128)(2,1)S(1)} %collective-permute-done.1.near), channel_id=1, source_target_pairs={{0,8},{1,9},{2,10},{3,11},{4,12},{5,13},{6,14},{7,15},{8,0},{9,1},... | collective-permute-start | bytes 196616 | tf_op jit(solution)/shard_map/ppermute | solution.py:268
  11.1 9.2 %collective-permute-start.4 = (bf16[8,256,128]{2,1,0:T(8,128)(2,1)S(1)}, bf16[8,256,128]{2,1,0:T(8,128)(2,1)S(1)}, u32[]{:S(2)}, u32[]{:S(2)}) collective-permute-start(bf16[8,256,128]{2,1,0:T(8,128)(2,1)S(1)} %get-tuple-element.42), channel_id=1, source_target_pairs={{0,16},{1,17},{2,18},{3,19},{4,20},{5,21},{6,22},{7,23},{8,9},{9,8... | collective-permute-start | bytes 1572872 | tf_op jit(solution)/shard_map/ppermute | solution.py:268
  15.3 10.7 %collective-permute-start.7 = (bf16[8,256,128]{2,1,0:T(8,128)(2,1)S(1)}, bf16[8,256,128]{2,1,0:T(8,128)(2,1)S(1)}, u32[]{:S(2)}, u32[]{:S(2)}) collective-permute-start(bf16[8,256,128]{2,1,0:T(8,128)(2,1)S(1)} %shard_map.72), channel_id=1, source_target_pairs={{0,16},{1,17},{2,18},{3,19},{4,20},{5,21},{6,22},{7,23},{8,9},{9,8... | collective-permute-start | bytes 1572872 | tf_op jit(solution)/shard_map/ppermute | solution.py:268
  15.5 14.8 %collective-permute-start.6 = (bf16[8,256,128]{2,1,0:T(8,128)(2,1)S(1)}, bf16[8,256,128]{2,1,0:T(8,128)(2,1)S(1)}, u32[]{:S(2)}, u32[]{:S(2)}) collective-permute-start(bf16[8,256,128]{2,1,0:T(8,128)(2,1)S(1)} %shard_map.71), channel_id=1, source_target_pairs={{0,2},{1,3},{2,0},{3,1},{4,6},{5,7},{6,4},{7,5},{8,10},{9,11},{10,... | collective-permute-start | bytes 1572872 | tf_op jit(solution)/shard_map/ppermute | solution.py:268
  20.5 12.0 %collective-permute-start.5 = (bf16[4,256,128]{2,1,0:T(8,128)(2,1)S(1)}, bf16[4,256,128]{2,1,0:T(8,128)(2,1)S(1)}, u32[]{:S(2)}, u32[]{:S(2)}) collective-permute-start(bf16[4,256,128]{2,1,0:T(8,128)(2,1)S(1)} %slice.116), channel_id=1, source_target_pairs={{0,1},{1,0},{2,3},{3,2},{4,5},{5,4},{6,7},{7,6},{8,10},{9,11},{10,... | collective-permute-start | bytes 786440 | tf_op jit(solution)/shard_map/ppermute | solution.py:268
  26.1 8.1 %collective-permute-start.10 = (bf16[4,256,128]{2,1,0:T(8,128)(2,1)S(1)}, bf16[4,256,128]{2,1,0:T(8,128)(2,1)S(1)}, u32[]{:S(2)}, u32[]{:S(2)}) collective-permute-start(bf16[4,256,128]{2,1,0:T(8,128)(2,1)S(1)} %slice.115), channel_id=1, source_target_pairs={{0,1},{1,0},{2,3},{3,2},{4,5},{5,4},{6,7},{7,6},{8,24},{9,25},{10,... | collective-permute-start | bytes 786440 | tf_op jit(solution)/shard_map/ppermute | solution.py:268
  30.4 6.4 %collective-permute-start.9 = (bf16[4,256,128]{2,1,0:T(8,128)(2,1)S(1)}, bf16[4,256,128]{2,1,0:T(8,128)(2,1)S(1)}, u32[]{:S(2)}, u32[]{:S(2)}) collective-permute-start(bf16[4,256,128]{2,1,0:T(8,128)(2,1)S(1)} %slice.114), channel_id=1, source_target_pairs={{0,1},{1,0},{2,3},{3,2},{4,5},{5,4},{6,7},{7,6},{8,24},{9,25},{10,... | collective-permute-start | bytes 786440 | tf_op jit(solution)/shard_map/ppermute | solution.py:268
  32.6 6.4 %collective-permute-start.8 = (bf16[2,256,128]{2,1,0:T(8,128)(2,1)S(1)}, bf16[2,256,128]{2,1,0:T(8,128)(2,1)S(1)}, u32[]{:S(2)}, u32[]{:S(2)}) collective-permute-start(bf16[2,256,128]{2,1,0:T(8,128)(2,1)S(1)} %slice.119), channel_id=1, source_target_pairs={{0,2},{1,3},{2,0},{3,1},{4,6},{5,7},{6,4},{7,5},{8,24},{9,25},{10,... | collective-permute-start | bytes 393224 | tf_op jit(solution)/shard_map/ppermute | solution.py:268
  34.3 10.8 %collective-permute-start.12 = (bf16[2,256,128]{2,1,0:T(8,128)(2,1)S(1)}, bf16[2,256,128]{2,1,0:T(8,128)(2,1)S(1)}, u32[]{:S(2)}, u32[]{:S(2)}) collective-permute-start(bf16[2,256,128]{2,1,0:T(8,128)(2,1)S(1)} %slice.118), channel_id=1, source_target_pairs={{0,2},{1,3},{2,0},{3,1},{4,6},{5,7},{6,4},{7,5},{8,10},{9,11},{10,... | collective-permute-start | bytes 393224 | tf_op jit(solution)/shard_map/ppermute | solution.py:268
  37.0 5.0 %collective-permute-start.13 = (bf16[2,256,128]{2,1,0:T(8,128)(2,1)S(1)}, bf16[2,256,128]{2,1,0:T(8,128)(2,1)S(1)}, u32[]{:S(2)}, u32[]{:S(2)}) collective-permute-start(bf16[2,256,128]{2,1,0:T(8,128)(2,1)S(1)} %slice.117), channel_id=1, source_target_pairs={{0,16},{1,17},{2,18},{3,19},{4,20},{5,21},{6,22},{7,23},{8,9},{9,8... | collective-permute-start | bytes 393224 | tf_op jit(solution)/shard_map/ppermute | solution.py:268
  39.0 7.0 %collective-permute-start.11 = (bf16[1,256,128]{2,1,0:T(8,128)(2,1)S(1)}, bf16[1,256,128]{2,1,0:T(8,128)(2,1)S(1)}, u32[]{:S(2)}, u32[]{:S(2)}) collective-permute-start(bf16[1,256,128]{2,1,0:T(8,128)(2,1)S(1)} %slice.122), channel_id=1, source_target_pairs={{0,4},{1,5},{2,6},{3,7},{4,0},{5,1},{6,2},{7,3},{8,12},{9,13},{10,... | collective-permute-start | bytes 196616 | tf_op jit(solution)/shard_map/ppermute | solution.py:268
  42.0 5.9 %collective-permute-start.18 = (bf16[1,256,128]{2,1,0:T(8,128)(2,1)S(1)}, bf16[1,256,128]{2,1,0:T(8,128)(2,1)S(1)}, u32[]{:S(2)}, u32[]{:S(2)}) collective-permute-start(bf16[1,256,128]{2,1,0:T(8,128)(2,1)S(1)} %slice.121), channel_id=1, source_target_pairs={{0,4},{1,5},{2,6},{3,7},{4,0},{5,1},{6,2},{7,3},{8,12},{9,13},{10,... | collective-permute-start | bytes 196616 | tf_op jit(solution)/shard_map/ppermute | solution.py:268
  45.2 5.2 %collective-permute-start.17 = (bf16[1,256,128]{2,1,0:T(8,128)(2,1)S(1)}, bf16[1,256,128]{2,1,0:T(8,128)(2,1)S(1)}, u32[]{:S(2)}, u32[]{:S(2)}) collective-permute-start(bf16[1,256,128]{2,1,0:T(8,128)(2,1)S(1)} %slice.120), channel_id=1, source_target_pairs={{0,4},{1,5},{2,6},{3,7},{4,0},{5,1},{6,2},{7,3},{8,12},{9,13},{10,... | collective-permute-start | bytes 196616 | tf_op jit(solution)/shard_map/ppermute | solution.py:268
  46.2 4.3 %collective-permute-start.14 = (bf16[128,256]{1,0:T(8,128)(2,1)S(1)}, bf16[128,256]{1,0:T(8,128)(2,1)S(1)}, u32[]{:S(2)}, u32[]{:S(2)}) collective-permute-start(bf16[128,256]{1,0:T(8,128)(2,1)S(1)} %shard_map.74.refs_0_), channel_id=1, source_target_pairs={{0,16},{1,17},{2,18},{3,19},{4,20},{5,21},{6,22},{7,23},{8,24},{9,... | collective-permute-start | bytes 196616 | tf_op jit(solution)/shard_map/ppermute | solution.py:268
  48.1 4.7 %collective-permute-start.23 = (bf16[128,256]{1,0:T(8,128)(2,1)S(1)}, bf16[128,256]{1,0:T(8,128)(2,1)S(1)}, u32[]{:S(2)}, u32[]{:S(2)}) collective-permute-start(bf16[128,256]{1,0:T(8,128)(2,1)S(1)} %shard_map.75.refs_8_), channel_id=1, source_target_pairs={{0,8},{1,9},{2,10},{3,11},{4,12},{5,13},{6,14},{7,15},{8,0},{9,1},... | collective-permute-start | bytes 196616 | tf_op jit(solution)/shard_map/ppermute | solution.py:268
  48.2 4.6 %collective-permute-start.22 = (bf16[128,256]{1,0:T(8,128)(2,1)S(1)}, bf16[128,256]{1,0:T(8,128)(2,1)S(1)}, u32[]{:S(2)}, u32[]{:S(2)}) collective-permute-start(bf16[128,256]{1,0:T(8,128)(2,1)S(1)} %shard_map.75.refs_8_), channel_id=1, source_target_pairs={{0,16},{1,17},{2,18},{3,19},{4,20},{5,21},{6,22},{7,23},{8,24},{9,... | collective-permute-start | bytes 196616 | tf_op jit(solution)/shard_map/ppermute | solution.py:268
  50.6 4.3 %collective-permute-start.19 = (bf16[128,256]{1,0:T(8,128)(2,1)S(1)}, bf16[128,256]{1,0:T(8,128)(2,1)S(1)}, u32[]{:S(2)}, u32[]{:S(2)}) collective-permute-start(bf16[128,256]{1,0:T(8,128)(2,1)S(1)} %shard_map.76.refs_4_), channel_id=1, source_target_pairs={{0,16},{1,17},{2,18},{3,19},{4,20},{5,21},{6,22},{7,23},{8,24},{9,... | collective-permute-start | bytes 196616 | tf_op jit(solution)/shard_map/ppermute | solution.py:268
  52.1 2.8 %collective-permute-start.15 = (bf16[128,256]{1,0:T(8,128)(2,1)S(1)}, bf16[128,256]{1,0:T(8,128)(2,1)S(1)}, u32[]{:S(2)}, u32[]{:S(2)}) collective-permute-start(bf16[128,256]{1,0:T(8,128)(2,1)S(1)} %shard_map.74.refs_0_), channel_id=1, source_target_pairs={{0,8},{1,9},{2,10},{3,11},{4,12},{5,13},{6,14},{7,15},{8,0},{9,1},... | collective-permute-start | bytes 196616 | tf_op jit(solution)/shard_map/ppermute | solution.py:268
  52.1 2.8 %collective-permute-start.20 = (bf16[128,256]{1,0:T(8,128)(2,1)S(1)}, bf16[128,256]{1,0:T(8,128)(2,1)S(1)}, u32[]{:S(2)}, u32[]{:S(2)}) collective-permute-start(bf16[128,256]{1,0:T(8,128)(2,1)S(1)} %shard_map.76.refs_4_), channel_id=1, source_target_pairs={{0,8},{1,9},{2,10},{3,11},{4,12},{5,13},{6,14},{7,15},{8,0},{9,1},... | collective-permute-start | bytes 196616 | tf_op jit(solution)/shard_map/ppermute | solution.py:268
  52.8 2.2 %collective-permute-start.24 = (bf16[128,256]{1,0:T(8,128)(2,1)S(1)}, bf16[128,256]{1,0:T(8,128)(2,1)S(1)}, u32[]{:S(2)}, u32[]{:S(2)}) collective-permute-start(bf16[128,256]{1,0:T(8,128)(2,1)S(1)} %collective-permute-done.22.refs_9_), channel_id=1, source_target_pairs={{0,8},{1,9},{2,10},{3,11},{4,12},{5,13},{6,14},{7,15},{8,0},{9,1},... | collective-permute-start | bytes 196616 | tf_op jit(solution)/shard_map/ppermute | solution.py:268
  52.8 2.2 %collective-permute-start.16 = (bf16[128,256]{1,0:T(8,128)(2,1)S(1)}, bf16[128,256]{1,0:T(8,128)(2,1)S(1)}, u32[]{:S(2)}, u32[]{:S(2)}) collective-permute-start(bf16[128,256]{1,0:T(8,128)(2,1)S(1)} %collective-permute-done.14.refs_1_), channel_id=1, source_target_pairs={{0,8},{1,9},{2,10},{3,11},{4,12},{5,13},{6,14},{7,15},{8,0},{9,1},... | collective-permute-start | bytes 196616 | tf_op jit(solution)/shard_map/ppermute | solution.py:268
  54.9 1.3 %collective-permute-start.21 = (bf16[128,256]{1,0:T(8,128)(2,1)S(1)}, bf16[128,256]{1,0:T(8,128)(2,1)S(1)}, u32[]{:S(2)}, u32[]{:S(2)}) collective-permute-start(bf16[128,256]{1,0:T(8,128)(2,1)S(1)} %collective-permute-done.19.refs_5_), channel_id=1, source_target_pairs={{0,8},{1,9},{2,10},{3,11},{4,12},{5,13},{6,14},{7,15},{8,0},{9,1},... | collective-permute-start | bytes 196616 | tf_op jit(solution)/shard_map/ppermute | solution.py:268
